TPU v7x, 512 devices: a whole 4x8x8 slice. The times are simulated.
512 devices in a mesh: row: 16 (over y_hi, z), col: 32 (over y_lo, x, core).
Axes of the slice: x: 4, y: 8 (y_hi: 2, y_lo: 4; y = y_hi * 4 + y_lo), z: 8, core: 2. Of those that a mesh axis runs over, the one named last changes fastest.
Arguments:
- features: bfloat16 [65536, 256], P(('col', 'row')), may hold values from -6 to 6
- weight: bfloat16 [256, 256], replicated, may hold values from -0.375 to 0.375
- bias: float32 [256], replicated, may hold values from -3 to 3
- grad_out: bfloat16 [65536, 256], P(('row', 'col')), may hold values from -6 to 6
- tile_rows: int32 [16, 32, 128], P('row', 'col'), may hold values from 0 to 31
- tile_cols: int32 [16, 32, 128], P('row', 'col'), may hold values from 0 to 15
- tile_counts: int32 [16, 32], P('row', 'col'), may hold values from 1 to 128, as said below
- tile_values: bfloat16 [16, 32, 128, 128, 128], P('row', 'col'), may hold values from 0 to 0.011962891
Outputs:
- output: bfloat16 [65536, 256], P(('row', 'col'))
- grad_features: bfloat16 [65536, 256], P(('col', 'row'))
- grad_weight: float32 [256, 256], replicated
- grad_bias: float32 [256], replicated
Inputs may be any that keep to these rules, and one draw needn't show every extreme that they name: `tile_counts`: some grid cell has all 128 slots live. Tile coordinates may repeat within a cell; repeated tiles add.
All inputs are finite; a program needn't handle non-finite values.
Results may differ from a plain program's by a relative error of at most 0.018.
Values may be sent and summed in bfloat16 or wider, within the bound.
No kernel may reach another device: no remote copies, remote signals or barrier semaphores. Data moves between devices by JAX's collectives and lax.ppermute only.
A program may use at most 64 MiB of HBM per device.

v0:
```python
import jax
import jax.numpy as jnp
from jax import lax
from jax.sharding import PartitionSpec as P

GROUP = 8


def elu_value(pre):
    return jnp.where(pre > 0, pre, jnp.expm1(jnp.minimum(pre, 0.0)))


def elu_slope(pre):
    return jnp.where(pre > 0, jnp.float32(1.0), jnp.exp(jnp.minimum(pre, 0.0)))


def accumulate(values, dest_idx, src_idx, live, source, dest_tiles, transpose):
    side = values.shape[-1]
    width = source.shape[-1]
    group_size = GROUP
    blocks_all = source.reshape(source.shape[0] // side, side, width)

    def one_group(step, acc):
        first = step * group_size
        part_values = lax.dynamic_slice_in_dim(values, first, group_size, 0)
        part_dest = lax.dynamic_slice_in_dim(dest_idx, first, group_size, 0)
        part_src = lax.dynamic_slice_in_dim(src_idx, first, group_size, 0)
        blocks = jnp.take(blocks_all, part_src, axis=0)
        if transpose:
            prod = jnp.einsum(
                "gab,gac->gbc", part_values, blocks, preferred_element_type=jnp.float32
            )
        else:
            prod = jnp.einsum(
                "gab,gbc->gac", part_values, blocks, preferred_element_type=jnp.float32
            )
        keep = (jnp.arange(group_size) + first < live).astype(jnp.float32)
        return acc.at[part_dest].add(prod * keep[:, None, None])

    start_acc = jnp.zeros((dest_tiles, side, width), jnp.float32)
    steps_used = values.shape[0] // group_size
    total = lax.fori_loop(0, steps_used, one_group, start_acc)
    return total.reshape(dest_tiles * side, width)


def body(features, weight, bias, grad_out, tile_rows, tile_cols, tile_counts, tile_values):
    values = tile_values[0, 0]
    rows_idx = tile_rows[0, 0]
    cols_idx = tile_cols[0, 0]
    live = tile_counts[0, 0]
    side = values.shape[-1]
    share = features.shape[0]
    row_tiles = share * lax.axis_size("col") // side
    col_tiles = share * lax.axis_size("row") // side
    mixed = jnp.dot(features, weight, preferred_element_type=jnp.float32).astype(jnp.bfloat16)
    column_block = lax.all_gather(mixed, "row", axis=0, tiled=True)
    partial_value = accumulate(values, rows_idx, cols_idx, live, column_block, row_tiles, False)
    pre_share = (
        lax.psum_scatter(
            partial_value.astype(jnp.bfloat16), "col", scatter_dimension=0, tiled=True
        ).astype(jnp.float32)
        + bias[None, :]
    )
    grad_share = (grad_out.astype(jnp.float32) * elu_slope(pre_share)).astype(jnp.bfloat16)
    grad_block = lax.all_gather(grad_share, "col", axis=0, tiled=True)
    output = elu_value(pre_share).astype(jnp.bfloat16)
    back = accumulate(values, cols_idx, rows_idx, live, grad_block, col_tiles, True)
    grad_mixed = lax.psum_scatter(back.astype(jnp.bfloat16), "row", scatter_dimension=0, tiled=True)
    grad_features = lax.dot_general(
        grad_mixed, weight, (((1,), (1,)), ((), ())), preferred_element_type=jnp.float32
    ).astype(jnp.bfloat16)
    weight_term = lax.dot_general(
        features, grad_mixed, (((0,), (0,)), ((), ())), preferred_element_type=jnp.float32
    )
    bias_term = jnp.sum(grad_share.astype(jnp.float32), axis=0)
    grad_weight, grad_bias = lax.psum((weight_term, bias_term), ("row", "col"))
    return (output, grad_features, grad_weight, grad_bias)


def solution(mesh):
    placed = (
        P(("col", "row"), None),
        P(),
        P(),
        P(("row", "col"), None),
        P("row", "col", None),
        P("row", "col", None),
        P("row", "col"),
        P("row", "col", None, None, None),
    )
    return jax.shard_map(
        body,
        mesh=mesh,
        in_specs=placed,
        out_specs=(P(("row", "col"), None), P(("col", "row"), None), P(), P()),
        check_vma=False,
    )
```

profile of v0, /device:TPU:1, one launch (start us, length us, event | category | flops | bytes accessed | tf_op | source)
XLA Modules:
  0.0 1037.7 jit_solution(1046019565683276147)
XLA Ops:
  9.8 92.8 %all-gather.3.cloned.1.call-done = bf16[2048,256]{1,0:T(8,128)(2,1)} async-done(((bf16[128,256]{1,0:T(8,128)(2,1)}), bf16[2048,256]{1,0:T(8,128)(2,1)}) %all-gather.3.cloned.1.call-update) | async-done | bytes 1048592 | tf_op jit(solution)/shard_map/all_gather | solution.py:56
  105.0 96.8 %while.26 = (s32[]{:T(128)}, f32[32,128,256]{2,1,0:T(8,128)}, s32[128]{0:T(128)S(1)}, bf16[128,128,128]{2,1,0:T(8,128)(2,1)}, s32[128]{0:T(128)S(1)}, /*index=5*...) while((s32[]{:T(128)}, f32[32,128,256]{2,1,0:T(8,128)}, ...), condition=%wide.region_2.3_spmd, body=%wide.region_0.2_spmd.sunk | while | flops 67896424 | bytes 6033887 | solution.py:42
  107.7 3.3 scatter_fusion
  113.8 3.3 scatter_fusion
  119.9 3.3 scatter_fusion
  125.9 3.3 scatter_fusion
  131.9 3.3 scatter_fusion
  137.9 3.4 scatter_fusion
  144.0 3.4 scatter_fusion
  156.1 3.3 scatter_fusion
  168.1 3.3 scatter_fusion
  174.2 3.3 scatter_fusion
  180.2 3.4 scatter_fusion
  186.3 3.4 scatter_fusion
  192.4 3.3 scatter_fusion
  198.5 3.3 scatter_fusion
  201.8 3.8 convert_element_type.56
  205.7 145.6 %reduce-scatter.3.cloned.1.call-done = bf16[128,256]{1,0:T(8,128)(2,1)} async-done(((bf16[4096,256]{1,0:T(8,128)(2,1)}), bf16[128,256]{1,0:T(8,128)(2,1)}) %reduce-scatter.3.cloned.1.call-update) | async-done | bytes 65552 | tf_op jit(solution)/shard_map/reduce_scatter | solution.py:59
  352.9 6.4 copy.12
  359.3 59.1 %all-gather.5.cloned.1.call-done = bf16[4096,256]{1,0:T(8,128)(2,1)} async-done(((bf16[128,256]{1,0:T(8,128)(2,1)}), bf16[4096,256]{1,0:T(8,128)(2,1)}) %all-gather.5.cloned.1.call-update) | async-done | bytes 2097168 | tf_op jit(solution)/shard_map/all_gather | solution.py:65
  419.9 121.7 %while.27 = (s32[]{:T(128)}, f32[16,128,256]{2,1,0:T(8,128)}, s32[128]{0:T(128)S(1)}, bf16[128,128,128]{1,2,0:T(8,128)(2,1)}, s32[128]{0:T(128)S(1)}, /*index=5*...) while((s32[]{:T(128)}, f32[16,128,256]{2,1,0:T(8,128)}, ...), condition=%wide.region_6.7_spmd, body=%wide.region_4.6_spmd.sunk | while | flops 67896424 | bytes 6033887 | solution.py:42
  424.2 3.3 scatter_fusion.1
  431.9 3.3 scatter_fusion.1
  439.5 3.3 scatter_fusion.1
  454.7 3.3 scatter_fusion.1
  485.1 3.3 scatter_fusion.1
  492.7 3.3 scatter_fusion.1
  500.3 3.3 scatter_fusion.1
  507.9 3.3 scatter_fusion.1
  544.4 100.1 %psum.15 = f32[256]{0:T(256)} all-reduce(f32[256]{0:T(256)S(1)} %get-tuple-element.297), channel_id=1, replica_groups=mesh['row'=16,'col'=32] {'row','col'}, use_global_device_ids=true, to_apply=%region_10.11 | all-reduce | flops 256 | bytes 2048 | tf_op jit(solution)/shard_map/psum | solution.py:76
  644.6 111.0 %reduce-scatter.5.cloned.1.call-done = bf16[128,256]{1,0:T(8,128)(2,1)} async-done(((bf16[2048,256]{1,0:T(8,128)(2,1)}), bf16[128,256]{1,0:T(8,128)(2,1)}) %reduce-scatter.5.cloned.1.call-update) | async-done | bytes 65552 | tf_op jit(solution)/shard_map/reduce_scatter | solution.py:68
  759.0 270.4 %all-reduce.2.cloned.1.call-done = f32[256,256]{0,1:T(8,128)} async-done(((f32[256,256]{0,1:T(8,128)}), f32[256,256]{0,1:T(8,128)}) %all-reduce.2.cloned.1.call-update) | async-done | bytes 262160 | tf_op jit(solution)/shard_map/psum | solution.py:76
  (202 shorter events, 161.1 us)
Async XLA Ops:
  7.2 0.9 copy-start
  7.2 97.8 %copy-start.4 = (s32[1,1,128]{2,1,0:T(1,128)S(1)}, s32[1,1,128]{2,1,0:T(1,128)}, u32[]{:S(2)}) copy-start(s32[1,1,128]{2,1,0:T(1,128)} %param.16) | copy-start | bytes 1540
  7.2 97.8 %copy-start.5 = (s32[1,1,128]{2,1,0:T(1,128)S(1)}, s32[1,1,128]{2,1,0:T(1,128)}, u32[]{:S(2)}) copy-start(s32[1,1,128]{2,1,0:T(1,128)} %param.17) | copy-start | bytes 1540
  7.2 95.3 %all-gather.3.cloned.1.call-start = ((), (), s32[]{:S(2)}) async-start(), calls=%async_computation.2 | async-start | bytes 1114112 | tf_op jit(solution)/shard_map/all_gather | solution.py:56
  9.7 341.5 %reduce-scatter.3.cloned.1.call-start = ((), (), s32[]{:S(2)}) async-start(), calls=%async_computation.3 | async-start | bytes 2162688 | tf_op jit(solution)/shard_map/reduce_scatter | solution.py:59
  102.5 2.4 copy-start.1
  201.8 149.5 %copy-start.3 = (bf16[128,256]{1,0:T(8,128)(2,1)S(1)}, bf16[128,256]{1,0:T(8,128)(2,1)}, u32[]{:S(2)}) copy-start(bf16[128,256]{1,0:T(8,128)(2,1)} %param.15) | copy-start | bytes 196612
  201.8 149.5 %copy-start.6 = (f32[256]{0:T(256)S(1)}, f32[256]{0:T(256)}, u32[]{:S(2)}) copy-start(f32[256]{0:T(256)} %param.14) | copy-start | bytes 3076
  205.7 212.7 %all-gather.5.cloned.1.call-start = ((), (), s32[]{:S(2)}) async-start(), calls=%async_computation.4 | async-start | bytes 2162688 | tf_op jit(solution)/shard_map/all_gather | solution.py:65
  352.9 402.7 %reduce-scatter.5.cloned.1.call-start = ((), (), s32[]{:S(2)}) async-start(), calls=%async_computation.5 | async-start | bytes 1114112 | tf_op jit(solution)/shard_map/reduce_scatter | solution.py:68
  541.6 213.9 %copy-start.2 = (bf16[128,256]{1,0:T(8,128)(2,1)S(1)}, bf16[128,256]{1,0:T(8,128)(2,1)}, u32[]{:S(2)}) copy-start(bf16[128,256]{1,0:T(8,128)(2,1)} %param.12) | copy-start | bytes 196612
  544.4 485.0 %all-reduce.2.cloned.1.call-start = ((), (), s32[]{:S(2)}) async-start(), calls=%async_computation.6 | async-start | bytes 524288 | tf_op jit(solution)/shard_map/psum | solution.py:76
Sparse Core Ops, SparseCore 0:
  11.8 90.7 all-gather.2
  205.8 145.4 reduce-scatter.2
  354.2 64.0 all-gather.4
  544.5 211.0 reduce-scatter.4
  761.7 267.5 all-reduce.1
where the time goes:
time: 1040 us
  waiting for transfers between devices  679 us (65%)
  other arithmetic  140 us (13%)
  blocking collectives  100 us (10%)
  local copies, waits for them, and re-layouts  57 us (5%)
  matrix products  47.3 us (5%)
  between operations  13.8 us (1%)
    psum x1, waiting for transfers between devices, body(): grad_weight, grad_bias = lax.psum((weight_term, bias_term), ('row', 'col'))  270 us
    reduce_scatter x1, waiting for transfers between devices, body(): lax.psum_scatter(partial_value.astype(jnp.bfloat16), 'col', scatter_dimen...  146 us
    reduce_scatter x1, waiting for transfers between devices, body(): lax.psum_scatter(back.astype(jnp.bfloat16), 'row', scatter_dimension=0, t...  111 us
    scatter-add x32, other arithmetic, one_group(): return acc.at[part_dest].add(prod * keep[:, None, None])  106 us
    psum x1, blocking collectives, body(): grad_weight, grad_bias = lax.psum((weight_term, bias_term), ('row', 'col'))  100 us
    all_gather x1, waiting for transfers between devices, body(): column_block = lax.all_gather(mixed, 'row', axis=0, tiled=True)  92.8 us
    all_gather x1, waiting for transfers between devices, body(): grad_block = lax.all_gather(grad_share, 'col', axis=0, tiled=True)  59.1 us
    gather x32, local copies, waits for them, and re-layouts, one_group(): blocks = jnp.take(blocks_all, part_src, axis=0)  44 us
  transfers between devices with their start and end apart: 5, of which 5 were waited for; matrix products, arithmetic and copies ran while one was open for 1% of the time, Pallas kernels for 0%

commit v1 on v0

v1 whole, which is shorter than its diff:
```python
import functools

import jax
import jax.numpy as jnp
from jax import lax
from jax.experimental import pallas as pl
from jax.experimental.pallas import tpu as pltpu
from jax.sharding import Mesh
from jax.sharding import PartitionSpec as P

ROW = ("yh", "z")
COL = ("yl", "x", "core")
ALL = ROW + COL
CHUNK = 16
GROUP = 4


def elu_value(pre):
    return jnp.where(pre > 0, pre, jnp.expm1(jnp.minimum(pre, 0.0)))


def elu_slope(pre):
    return jnp.where(pre > 0, jnp.float32(1.0), jnp.exp(jnp.minimum(pre, 0.0)))


def col_slot(t):
    return lax.rem(t, 2) * 16 + lax.rem(t // 2, 4) * 4 + t // 8


def start_values(values_hbm, values, sems):
    copies = [
        pltpu.make_async_copy(
            values_hbm.at[pl.ds(c * CHUNK, CHUNK)], values.at[pl.ds(c * CHUNK, CHUNK)], sems.at[c]
        )
        for c in range(values.shape[0] // CHUNK)
    ]
    for copy in copies:
        copy.start()
    return copies


def walk(copies, live, step):
    for c, copy in enumerate(copies):
        copy.wait()
        left = jnp.clip(live - c * CHUNK, 0, CHUNK)

        def one(g, carry, c=c):
            step(c * CHUNK + g * GROUP)
            return carry

        lax.fori_loop(0, (left + GROUP - 1) // GROUP, one, 0)


def forward_kernel(rows, cols, live_ref, values_hbm, src, out, values, acc, sems):
    live = live_ref[0]
    copies = start_values(values_hbm, values, sems)
    tiles = out.shape[0]
    acc[...] = jnp.zeros_like(acc)

    def step(first):
        for u in range(GROUP):
            s = first + u
            dest = jnp.where(s < live, col_slot(rows[s]), tiles)
            acc[dest] += jnp.dot(values[s], src[cols[s]], preferred_element_type=jnp.float32)

    walk(copies, live, step)
    out[...] = acc[:tiles].astype(out.dtype)


def backward_kernel(rows, cols, live_ref, core_ref, values_hbm, own_hbm, other_hbm, out, values, src, acc, sems, src_sems):
    live = live_ref[0]
    core = core_ref[0]
    half = own_hbm.shape[0]
    fetch = [
        pltpu.make_async_copy(own_hbm, src.at[pl.ds(core * half, half)], src_sems.at[0]),
        pltpu.make_async_copy(other_hbm, src.at[pl.ds((1 - core) * half, half)], src_sems.at[1]),
    ]
    for copy in fetch:
        copy.start()
    copies = start_values(values_hbm, values, sems)
    tiles = out.shape[0]
    acc[...] = jnp.zeros_like(acc)
    for copy in fetch:
        copy.wait()

    def step(first):
        for u in range(GROUP):
            s = first + u
            dest = jnp.where(s < live, cols[s], tiles)
            acc[dest] += lax.dot_general(
                values[s],
                src[col_slot(rows[s])],
                (((0,), (0,)), ((), ())),
                preferred_element_type=jnp.float32,
            )

    walk(copies, live, step)
    out[...] = acc[:tiles].astype(out.dtype)


SMEM = pl.BlockSpec(memory_space=pltpu.SMEM)
VMEM = pl.BlockSpec(memory_space=pltpu.VMEM)
ANY = pl.BlockSpec(memory_space=pl.ANY)


def cost(slots, side, width):
    return pl.CostEstimate(
        flops=2 * slots * side * side * width, bytes_accessed=2 * slots * side * side, transcendentals=0
    )


def spread_forward(rows, cols, live, values, src, row_tiles):
    slots, side, _ = values.shape
    width = src.shape[-1]
    return pl.pallas_call(
        forward_kernel,
        out_shape=jax.ShapeDtypeStruct((row_tiles, side, width), jnp.bfloat16),
        in_specs=[SMEM, SMEM, SMEM, ANY, VMEM],
        out_specs=VMEM,
        scratch_shapes=[
            pltpu.VMEM((slots, side, side), jnp.bfloat16),
            pltpu.VMEM((row_tiles + 1, side, width), jnp.float32),
            pltpu.SemaphoreType.DMA((slots // CHUNK,)),
        ],
        compiler_params=pltpu.CompilerParams(vmem_limit_bytes=40 << 20),
        cost_estimate=cost(slots, side, width),
        name="forward_tiles",
    )(rows, cols, live, values, src)


def spread_backward(rows, cols, live, core, values, own, other, col_tiles):
    slots, side, _ = values.shape
    width = own.shape[-1]
    return pl.pallas_call(
        backward_kernel,
        out_shape=jax.ShapeDtypeStruct((col_tiles, side, width), jnp.bfloat16),
        in_specs=[SMEM, SMEM, SMEM, SMEM, ANY, ANY, ANY],
        out_specs=VMEM,
        scratch_shapes=[
            pltpu.VMEM((slots, side, side), jnp.bfloat16),
            pltpu.VMEM((2 * own.shape[0], side, width), jnp.bfloat16),
            pltpu.VMEM((col_tiles + 1, side, width), jnp.float32),
            pltpu.SemaphoreType.DMA((slots // CHUNK,)),
            pltpu.SemaphoreType.DMA((2,)),
        ],
        compiler_params=pltpu.CompilerParams(vmem_limit_bytes=40 << 20),
        cost_estimate=cost(slots, side, width),
        name="backward_tiles",
    )(rows, cols, live, core, values, own, other)


def exchange(x, axes):
    return lax.all_to_all(x, axes, 0, 0, tiled=True)


def gather(x, axes, size):
    copies = lax.optimization_barrier(jnp.broadcast_to(x[None], (size,) + x.shape))
    return exchange(copies, axes)


def add_up(x):
    return jnp.sum(x.astype(jnp.float32), axis=0)


def body(features, weight, bias, grad_out, tile_rows, tile_cols, tile_counts, tile_values):
    values = tile_values[0, 0]
    rows, cols, live = tile_rows[0, 0], tile_cols[0, 0], tile_counts[0]
    side, width = features.shape
    row_tiles, col_tiles = 32, 16
    bf16 = jnp.bfloat16
    core = lax.axis_index("core").astype(jnp.int32).reshape(1)

    block = gather(features, ROW, col_tiles)
    partial = spread_forward(rows, cols, live, values, block, row_tiles)
    by_core = add_up(exchange(partial.reshape(2, 16, side, width), "core")).astype(bf16)
    by_x = add_up(exchange(by_core.reshape(4, 4, side, width), "x")).astype(bf16)
    mean = add_up(exchange(by_x, "yl"))
    pre = (
        jnp.dot(mean, weight.astype(jnp.float32), precision=lax.Precision.HIGHEST, preferred_element_type=jnp.float32)
        + bias[None, :]
    )
    grad_pre = (grad_out.astype(jnp.float32) * elu_slope(pre)).astype(bf16)
    output = elu_value(pre).astype(bf16)

    along_y = gather(grad_pre, "yl", 4)
    own = gather(along_y, "x", 4).reshape(16, side, width)
    other = lax.ppermute(own, "core", [(0, 1), (1, 0)])

    grad32 = grad_pre.astype(jnp.float32)
    weight_term = lax.dot_general(
        mean, grad32, (((0,), (0,)), ((), ())), precision=lax.Precision.HIGHEST, preferred_element_type=jnp.float32
    )
    n = 512
    per = width * width // n
    terms = jnp.concatenate([weight_term.reshape(n, per), jnp.zeros((n, 128), jnp.float32)], axis=1)
    bias_term = jnp.sum(grad32, axis=0).reshape(2, 1, 128)
    terms = terms.at[:, per:].set(jnp.broadcast_to(bias_term, (2, n // 2, 128)).reshape(n, 128))
    piece = add_up(exchange(terms.reshape(n, 1, 2 * per), ALL))
    pieces = gather(piece, ALL, n).reshape(n, 2 * per)
    grad_weight = pieces[:, :per].reshape(width, width)
    grad_bias = jnp.concatenate([pieces[0, per:], pieces[n // 2, per:]])

    back = spread_backward(rows, cols, live, core, values, own, other, col_tiles)
    grad_mixed = add_up(exchange(back, ROW)).astype(bf16)
    grad_features = lax.dot_general(
        grad_mixed, weight, (((1,), (1,)), ((), ())), preferred_element_type=jnp.float32
    ).astype(bf16)
    return (output, grad_features, grad_weight, grad_bias)


def solution(mesh):
    fine = Mesh(mesh.devices.reshape(2, 8, 4, 4, 2), ALL)
    placed = (
        P(COL + ROW, None),
        P(),
        P(),
        P(ALL, None),
        P(ROW, COL, None),
        P(ROW, COL, None),
        P(ROW, COL),
        P(ROW, COL, None, None, None),
    )
    return jax.shard_map(
        body,
        mesh=fine,
        in_specs=placed,
        out_specs=(P(ALL, None), P(COL + ROW, None), P(), P()),
        check_vma=False,
    )
```

time: 1040 us -> 233 us (0.22)
  the two profiles are of different devices: /device:TPU:1 before, /device:TPU:14 now
where the time goes in v1:
time: 233 us; the launch traced here: 232 us
  waiting for transfers between devices  106 us (45%)
  starting transfers between devices  57.9 us (25%)
  blocking collectives  43.9 us (19%)
  local copies, waits for them, and re-layouts  11.3 us (5%)
  Pallas kernels  6.85 us (3%)
    all_to_all x5, waiting for transfers between devices, exchange(): return lax.all_to_all(x, axes, 0, 0, tiled=True)  106 us
    all_to_all x5, starting transfers between devices, exchange(): return lax.all_to_all(x, axes, 0, 0, tiled=True)  55.9 us
    all_to_all x4, blocking collectives, exchange(): return lax.all_to_all(x, axes, 0, 0, tiled=True)  43.9 us
  transfers between devices with their start and end apart: 6, of which 5 were waited for; matrix products, arithmetic and copies ran while one was open for 2% of the time, Pallas kernels for 2%

profile of v1, /device:TPU:14, one launch (start us, length us, event | category | flops | bytes accessed | tf_op | source)
XLA Modules:
  0.0 232.2 jit_solution(4509970239677291334)
XLA Ops:
  0.7 1.9 broadcast_in_dim.16
  2.6 14.8 %all-to-all-start = ((bf16[16,128,256]{2,1,0:T(8,128)(2,1)}), bf16[16,128,256]{2,1,0:T(8,128)(2,1)S(1)}, u32[]{:S(2)}, u32[]{:S(2)}) async-start(bf16[16,128,256]{2,1,0:T(8,128)(2,1)} %broadcast_in_dim.16), calls=%async_computation | async-start | bytes 2097152 | tf_op jit(solution)/shard_map/all_to_all | solution.py:153
  18.1 32.7 %all-to-all-done.src = bf16[16,128,256]{2,1,0:T(8,128)(2,1)S(1)} async-done(((bf16[16,128,256]{2,1,0:T(8,128)(2,1)}), bf16[16,128,256]{2,1,0:T(8,128)(2,1)S(1)}, u32[]{:S(2)}, u32[]{:S(2)}) %all-to-all-start) | async-done | bytes 1048608 | tf_op jit(solution)/shard_map/all_to_all | solution.py:153
  50.8 2.2 copy-done.1
  53.0 2.9 %forward_tiles.1 = bf16[32,128,256]{2,1,0:T(8,128)(2,1)S(1)} custom-call(s32[128]{0:T(128)S(1)} %bitcast.30, s32[128]{0:T(128)S(1)} %bitcast.32, s32[1]{0:T(128)} %bitcast.23.live_ref, bf16[128,128,128]{2,1,0:T(8,128)(2,1)S(1)} %bitcast.25, bf16[16,128,256]{2,1,0:T(8,128)(2,1)S(1)} %all-to-all-done.src), custom_call_target="tpu_custom_call" | custom-call | flops 1073741824 | bytes 4194304 | tf_op jit(solution)/shard_map/forward_tiles/pallas_call | solution.py:115
  55.8 5.4 %all_to_all.45 = bf16[2,16,128,256]{3,2,1,0:T(8,128)(2,1)S(1)} all-to-all(bf16[2,16,128,256]{3,2,1,0:T(8,128)(2,1)S(1)} %bitcast.27), channel_id=1, replica_groups=mesh['yh'=2,'z'=8,'yl'=4,'x'=4,'core'=2] {'core'}, dimensions={0} | all-to-all | bytes 4194304 | tf_op jit(solution)/shard_map/all_to_all | solution.py:153
  61.3 0.7 reduce_sum.63
  62.0 18.9 %all_to_all.46 = bf16[4,4,128,256]{3,2,1,0:T(8,128)(2,1)S(1)} all-to-all(bf16[4,4,128,256]{3,2,1,0:T(8,128)(2,1)S(1)} %bitcast.34), channel_id=1, replica_groups=mesh['yh'=2,'z'=8,'yl'=4,'x'=4,'core'=2] {'x'}, dimensions={0} | all-to-all | bytes 2097152 | tf_op jit(solution)/shard_map/all_to_all | solution.py:153
  80.9 0.2 reduce_sum.64
  81.1 9.3 %all_to_all.47 = bf16[4,128,256]{2,1,0:T(8,128)(2,1)S(1)} all-to-all(bf16[4,128,256]{2,1,0:T(8,128)(2,1)S(1)} %reduce_sum.64), channel_id=1, replica_groups=mesh['yh'=2,'z'=8,'yl'=4,'x'=4,'core'=2] {'yl'}, dimensions={0} | all-to-all | bytes 524288 | tf_op jit(solution)/shard_map/all_to_all | solution.py:153
  90.5 0.9 convert_reduce_fusion.1
  91.4 10.3 %all_to_all.48 = bf16[4,128,256]{2,1,0:T(8,128)(2,1)S(1)} all-to-all(bf16[4,128,256]{2,1,0:T(8,128)(2,1)S(1)} %broadcast_in_dim.18), channel_id=1, replica_groups=mesh['yh'=2,'z'=8,'yl'=4,'x'=4,'core'=2] {'yl'}, dimensions={0} | all-to-all | bytes 524288 | tf_op jit(solution)/shard_map/all_to_all | solution.py:153
  101.7 1.1 broadcast_in_dim.19
  102.8 5.6 %all-to-all-start.5 = ((bf16[4,4,128,256]{3,2,1,0:T(8,128)(2,1)}), bf16[4,4,128,256]{3,2,1,0:T(8,128)(2,1)S(1)}, u32[]{:S(2)}, u32[]{:S(2)}) async-start(bf16[4,4,128,256]{3,2,1,0:T(8,128)(2,1)} %broadcast_in_dim.19), calls=%async_computation.5 | async-start | bytes 2097152 | tf_op jit(solution)/shard_map/all_to_all | solution.py:153
  108.3 0.3 fusion.4
  108.7 1.2 reshape.80
  109.9 0.8 constant_dynamic-update-slice_fusion
  110.7 8.5 %all-to-all-done.5 = bf16[4,4,128,256]{3,2,1,0:T(8,128)(2,1)S(1)} async-done(((bf16[4,4,128,256]{3,2,1,0:T(8,128)(2,1)}), bf16[4,4,128,256]{3,2,1,0:T(8,128)(2,1)S(1)}, u32[]{:S(2)}, u32[]{:S(2)}) %all-to-all-start.5) | async-done | bytes 1048608 | tf_op jit(solution)/shard_map/all_to_all | solution.py:153
  119.1 19.2 %all-to-all-start.7 = ((f32[512,1,256]{2,1,0:T(1,128)}), f32[512,1,256]{2,1,0:T(1,128)S(1)}, u32[]{:S(2)}, u32[]{:S(2)}) async-start(f32[512,1,256]{2,1,0:T(1,128)} %constant_dynamic-update-slice_fusion), calls=%async_computation.7 | async-start | bytes 1048576 | tf_op jit(solution)/shard_map/all_to_all | solution.py:153
  138.4 2.1 collective-permute-start
  140.4 17.9 %all-to-all-done.7 = f32[512,1,256]{2,1,0:T(1,128)S(1)} async-done(((f32[512,1,256]{2,1,0:T(1,128)}), f32[512,1,256]{2,1,0:T(1,128)S(1)}, u32[]{:S(2)}, u32[]{:S(2)}) %all-to-all-start.7) | async-done | bytes 524320 | tf_op jit(solution)/shard_map/all_to_all | solution.py:153
  158.4 0.6 reduce_sum.68
  158.9 1.1 broadcast_in_dim.22
  160.0 11.6 %all-to-all-start.8 = ((f32[512,1,256]{2,1,0:T(1,128)}), f32[512,1,256]{2,1,0:T(1,128)S(1)}, u32[]{:S(2)}, u32[]{:S(2)}) async-start(f32[512,1,256]{2,1,0:T(1,128)} %broadcast_in_dim.22), calls=%async_computation.8 | async-start | bytes 1048576 | tf_op jit(solution)/shard_map/all_to_all | solution.py:153
  171.7 2.2 copy-done.2
  173.9 4.0 %backward_tiles.1 = bf16[16,128,256]{2,1,0:T(8,128)(2,1)} custom-call(s32[128]{0:T(128)S(1)} %bitcast.31, s32[128]{0:T(128)S(1)} %bitcast.33, s32[1]{0:T(128)} %bitcast.24.live_ref, s32[1]{0:T(128)} %bitcast.6.core_ref, bf16[128,128,128]{2,1,0:T(8,128)(2,1)S(1)} %bitcast.26, bf16[16,128,256]{2,1,0:T(8,128)(2,1)S(1)} %bitcast.29, ...), custom_call_target="tpu_custom_call" | custom-call | flops 1073741824 | bytes 4194304 | tf_op jit(solution)/shard_map/backward_tiles/pallas_call | solution.py:134
  177.9 13.9 %all-to-all-done.8 = f32[512,1,256]{2,1,0:T(1,128)S(1)} async-done(((f32[512,1,256]{2,1,0:T(1,128)}), f32[512,1,256]{2,1,0:T(1,128)S(1)}, u32[]{:S(2)}, u32[]{:S(2)}) %all-to-all-start.8) | async-done | bytes 524320 | tf_op jit(solution)/shard_map/all_to_all | solution.py:153
  191.7 4.7 %all-to-all-start.6 = ((bf16[16,128,256]{2,1,0:T(8,128)(2,1)}), bf16[16,128,256]{2,1,0:T(8,128)(2,1)S(1)}, u32[]{:S(2)}, u32[]{:S(2)}) async-start(bf16[16,128,256]{2,1,0:T(8,128)(2,1)} %backward_tiles.1), calls=%async_computation.6 | async-start | bytes 2097152 | tf_op jit(solution)/shard_map/all_to_all | solution.py:153
  196.4 0.8 reshape.83
  197.2 0.6 pad_maximum_fusion
  197.8 33.5 %all-to-all-done.6 = bf16[16,128,256]{2,1,0:T(8,128)(2,1)S(1)} async-done(((bf16[16,128,256]{2,1,0:T(8,128)(2,1)}), bf16[16,128,256]{2,1,0:T(8,128)(2,1)S(1)}, u32[]{:S(2)}, u32[]{:S(2)}) %all-to-all-start.6) | async-done | bytes 1048608 | tf_op jit(solution)/shard_map/all_to_all | solution.py:153
  231.4 0.8 convolution_convert_fusion
  (22 shorter events, 0.4 us)
Async XLA Ops:
  0.6 89.8 %copy-start = (bf16[256,256]{1,0:T(8,128)(2,1)S(1)}, bf16[256,256]{1,0:T(8,128)(2,1)}, u32[]{:S(2)}) copy-start(bf16[256,256]{1,0:T(8,128)(2,1)} %param.11) | copy-start | bytes 393220
  0.6 50.1 %copy-start.3 = (s32[1,1,128]{2,1,0:T(1,128)S(1)}, s32[1,1,128]{2,1,0:T(1,128)}, u32[]{:S(2)}) copy-start(s32[1,1,128]{2,1,0:T(1,128)} %param.14) | copy-start | bytes 1540
  0.7 50.1 %copy-start.4 = (s32[1,1,128]{2,1,0:T(1,128)S(1)}, s32[1,1,128]{2,1,0:T(1,128)}, u32[]{:S(2)}) copy-start(s32[1,1,128]{2,1,0:T(1,128)} %param.15) | copy-start | bytes 1540
  2.6 48.2 %all-to-all-start = ((bf16[16,128,256]{2,1,0:T(8,128)(2,1)}), bf16[16,128,256]{2,1,0:T(8,128)(2,1)S(1)}, u32[]{:S(2)}, u32[]{:S(2)}) async-start(bf16[16,128,256]{2,1,0:T(8,128)(2,1)} %broadcast_in_dim.16), calls=%async_computation | async-start | bytes 2097152 | tf_op jit(solution)/shard_map/all_to_all | solution.py:153
  50.8 2.2 copy-start.1
  61.9 28.5 %copy-start.5 = (bf16[128,256]{1,0:T(8,128)(2,1)S(1)}, bf16[128,256]{1,0:T(8,128)(2,1)}, u32[]{:S(2)}) copy-start(bf16[128,256]{1,0:T(8,128)(2,1)} %param.13) | copy-start | bytes 196612
  61.9 28.5 %copy-start.6 = (f32[256]{0:T(256)S(1)}, f32[256]{0:T(256)}, u32[]{:S(2)}) copy-start(f32[256]{0:T(256)} %param.12) | copy-start | bytes 3076
  102.8 16.4 %all-to-all-start.5 = ((bf16[4,4,128,256]{3,2,1,0:T(8,128)(2,1)}), bf16[4,4,128,256]{3,2,1,0:T(8,128)(2,1)S(1)}, u32[]{:S(2)}, u32[]{:S(2)}) async-start(bf16[4,4,128,256]{3,2,1,0:T(8,128)(2,1)} %broadcast_in_dim.19), calls=%async_computation.5 | async-start | bytes 2097152 | tf_op jit(solution)/shard_map/all_to_all | solution.py:153
  119.1 39.3 %all-to-all-start.7 = ((f32[512,1,256]{2,1,0:T(1,128)}), f32[512,1,256]{2,1,0:T(1,128)S(1)}, u32[]{:S(2)}, u32[]{:S(2)}) async-start(f32[512,1,256]{2,1,0:T(1,128)} %constant_dynamic-update-slice_fusion), calls=%async_computation.7 | async-start | bytes 1048576 | tf_op jit(solution)/shard_map/all_to_all | solution.py:153
  138.4 33.3 %collective-permute-start = (bf16[16,128,256]{2,1,0:T(8,128)(2,1)S(1)}, bf16[16,128,256]{2,1,0:T(8,128)(2,1)S(1)}, u32[]{:S(2)}, u32[]{:S(2)}) collective-permute-start(bf16[16,128,256]{2,1,0:T(8,128)(2,1)S(1)} %bitcast.28), channel_id=1, source_target_pairs={{0,1},{1,0},{2,3},{3,2},{4,5},{5,4},{6,7},{7,6},{8,9},{9,8},{10,11... | collective-permute-start | bytes 3145736 | tf_op jit(solution)/shard_map/ppermute | solution.py:187
  160.0 31.7 %all-to-all-start.8 = ((f32[512,1,256]{2,1,0:T(1,128)}), f32[512,1,256]{2,1,0:T(1,128)S(1)}, u32[]{:S(2)}, u32[]{:S(2)}) async-start(f32[512,1,256]{2,1,0:T(1,128)} %broadcast_in_dim.22), calls=%async_computation.8 | async-start | bytes 1048576 | tf_op jit(solution)/shard_map/all_to_all | solution.py:153
  171.7 2.2 copy-start.2
  191.7 39.6 %all-to-all-start.6 = ((bf16[16,128,256]{2,1,0:T(8,128)(2,1)}), bf16[16,128,256]{2,1,0:T(8,128)(2,1)S(1)}, u32[]{:S(2)}, u32[]{:S(2)}) async-start(bf16[16,128,256]{2,1,0:T(8,128)(2,1)} %backward_tiles.1), calls=%async_computation.6 | async-start | bytes 2097152 | tf_op jit(solution)/shard_map/all_to_all | solution.py:153

commit v2 on v1

--- a/solution.py
+++ b/solution.py
@@ -1,5 +1,3 @@
-import functools
-
 import jax
 import jax.numpy as jnp
 from jax import lax
@@ -67,13 +65,13 @@
     out[...] = acc[:tiles].astype(out.dtype)
 
 
-def backward_kernel(rows, cols, live_ref, core_ref, values_hbm, own_hbm, other_hbm, out, values, src, acc, sems, src_sems):
+def backward_kernel(rows, cols, live_ref, place, values_hbm, *refs):
+    blocks, (out, values, src, acc, sems, src_sems) = refs[:8], refs[8:]
     live = live_ref[0]
-    core = core_ref[0]
-    half = own_hbm.shape[0]
+    core, x = place[0], place[1]
+    depth = blocks[0].shape[0]
     fetch = [
-        pltpu.make_async_copy(own_hbm, src.at[pl.ds(core * half, half)], src_sems.at[0]),
-        pltpu.make_async_copy(other_hbm, src.at[pl.ds((1 - core) * half, half)], src_sems.at[1]),
+        pltpu.make_async_copy(block, src.at[pl.ds(k * depth, depth)], src_sems.at[k]) for k, block in enumerate(blocks)
     ]
     for copy in fetch:
         copy.start()
@@ -83,24 +81,34 @@
     for copy in fetch:
         copy.wait()
 
+    def slot(t):
+        return (lax.rem(t, 2) ^ core) * 16 + ((x - t // 2) & 3) * 4 + t // 8
+
     def step(first):
         for u in range(GROUP):
             s = first + u
             dest = jnp.where(s < live, cols[s], tiles)
             acc[dest] += lax.dot_general(
-                values[s],
-                src[col_slot(rows[s])],
-                (((0,), (0,)), ((), ())),
-                preferred_element_type=jnp.float32,
+                values[s], src[slot(rows[s])], (((0,), (0,)), ((), ())), preferred_element_type=jnp.float32
             )
 
     walk(copies, live, step)
     out[...] = acc[:tiles].astype(out.dtype)
+
+
+def place_kernel(place, pieces, out):
+    core, x, y = place[0], place[1], place[2]
+    for kc in range(2):
+        for kx in range(4):
+            for ky in range(4):
+                to = ((y - ky) & 3) * 8 + ((x - kx) & 3) * 2 + (core ^ kc)
+                out[to] = pieces[kc * 16 + kx * 4 + ky]
 
 
 SMEM = pl.BlockSpec(memory_space=pltpu.SMEM)
 VMEM = pl.BlockSpec(memory_space=pltpu.VMEM)
 ANY = pl.BlockSpec(memory_space=pl.ANY)
+HBM = pl.BlockSpec(memory_space=pltpu.HBM)
 
 
 def cost(slots, side, width):
@@ -115,7 +123,7 @@
     return pl.pallas_call(
         forward_kernel,
         out_shape=jax.ShapeDtypeStruct((row_tiles, side, width), jnp.bfloat16),
-        in_specs=[SMEM, SMEM, SMEM, ANY, VMEM],
+        in_specs=[SMEM, SMEM, SMEM, HBM, VMEM],
         out_specs=VMEM,
         scratch_shapes=[
             pltpu.VMEM((slots, side, side), jnp.bfloat16),
@@ -128,25 +136,43 @@
     )(rows, cols, live, values, src)
 
 
-def spread_backward(rows, cols, live, core, values, own, other, col_tiles):
+def spread_backward(rows, cols, live, place, values, blocks, col_tiles):
     slots, side, _ = values.shape
-    width = own.shape[-1]
+    depth, _, width = blocks[0].shape
     return pl.pallas_call(
         backward_kernel,
         out_shape=jax.ShapeDtypeStruct((col_tiles, side, width), jnp.bfloat16),
-        in_specs=[SMEM, SMEM, SMEM, SMEM, ANY, ANY, ANY],
+        in_specs=[SMEM, SMEM, SMEM, SMEM, HBM] + [ANY] * len(blocks),
         out_specs=VMEM,
         scratch_shapes=[
             pltpu.VMEM((slots, side, side), jnp.bfloat16),
-            pltpu.VMEM((2 * own.shape[0], side, width), jnp.bfloat16),
+            pltpu.VMEM((len(blocks) * depth, side, width), jnp.bfloat16),
             pltpu.VMEM((col_tiles + 1, side, width), jnp.float32),
             pltpu.SemaphoreType.DMA((slots // CHUNK,)),
-            pltpu.SemaphoreType.DMA((2,)),
+            pltpu.SemaphoreType.DMA((len(blocks),)),
         ],
         compiler_params=pltpu.CompilerParams(vmem_limit_bytes=40 << 20),
         cost_estimate=cost(slots, side, width),
         name="backward_tiles",
-    )(rows, cols, live, core, values, own, other)
+    )(rows, cols, live, place, values, *blocks)
+
+
+def put_in_place(place, pieces):
+    return pl.pallas_call(
+        place_kernel,
+        out_shape=jax.ShapeDtypeStruct(pieces.shape, pieces.dtype),
+        in_specs=[SMEM, VMEM],
+        out_specs=VMEM,
+        name="place_pieces",
+    )(place, pieces)
+
+
+def around(x, axis, size):
+    return [x] + [lax.ppermute(x, axis, [(i, (i + k) % size) for i in range(size)]) for k in range(1, size)]
+
+
+def swap(x):
+    return lax.ppermute(x, "core", [(0, 1), (1, 0)])
 
 
 def exchange(x, axes):
@@ -162,13 +188,23 @@
     return jnp.sum(x.astype(jnp.float32), axis=0)
 
 
+def weight_pieces(weight_term, bias_term, pieces):
+    width = bias_term.shape[-1]
+    per = weight_term.shape[0] // pieces
+    high = bias_term.astype(jnp.bfloat16)
+    low = (bias_term - high.astype(jnp.float32)).astype(jnp.bfloat16)
+    tail = jnp.concatenate([high[None], low[None], jnp.zeros((per - 2, width), jnp.bfloat16)])
+    tail = jnp.broadcast_to(tail[None], (pieces, per, width))
+    return jnp.concatenate([weight_term.astype(jnp.bfloat16).reshape(pieces, per, width), tail], axis=1)
+
+
 def body(features, weight, bias, grad_out, tile_rows, tile_cols, tile_counts, tile_values):
-    values = tile_values[0, 0]
+    values = pltpu.with_memory_space_constraint(tile_values[0, 0], pltpu.HBM)
     rows, cols, live = tile_rows[0, 0], tile_cols[0, 0], tile_counts[0]
     side, width = features.shape
     row_tiles, col_tiles = 32, 16
     bf16 = jnp.bfloat16
-    core = lax.axis_index("core").astype(jnp.int32).reshape(1)
+    place = jnp.stack([lax.axis_index(axis) for axis in ("core", "x", "yl")]).astype(jnp.int32)
 
     block = gather(features, ROW, col_tiles)
     partial = spread_forward(rows, cols, live, values, block, row_tiles)
@@ -182,25 +218,24 @@
     grad_pre = (grad_out.astype(jnp.float32) * elu_slope(pre)).astype(bf16)
     output = elu_value(pre).astype(bf16)
 
-    along_y = gather(grad_pre, "yl", 4)
-    own = gather(along_y, "x", 4).reshape(16, side, width)
-    other = lax.ppermute(own, "core", [(0, 1), (1, 0)])
-
     grad32 = grad_pre.astype(jnp.float32)
     weight_term = lax.dot_general(
         mean, grad32, (((0,), (0,)), ((), ())), precision=lax.Precision.HIGHEST, preferred_element_type=jnp.float32
     )
-    n = 512
-    per = width * width // n
-    terms = jnp.concatenate([weight_term.reshape(n, per), jnp.zeros((n, 128), jnp.float32)], axis=1)
-    bias_term = jnp.sum(grad32, axis=0).reshape(2, 1, 128)
-    terms = terms.at[:, per:].set(jnp.broadcast_to(bias_term, (2, n // 2, 128)).reshape(n, 128))
-    piece = add_up(exchange(terms.reshape(n, 1, 2 * per), ALL))
-    pieces = gather(piece, ALL, n).reshape(n, 2 * per)
-    grad_weight = pieces[:, :per].reshape(width, width)
-    grad_bias = jnp.concatenate([pieces[0, per:], pieces[n // 2, per:]])
-
-    back = spread_backward(rows, cols, live, core, values, own, other, col_tiles)
+    terms = weight_pieces(weight_term, jnp.sum(grad32, axis=0), 32)
+
+    along_y = gather(grad_pre, "yl", 4)
+    own = around(along_y, "x", 4)
+    other = [swap(block) for block in own]
+    of_col = add_up(exchange(terms, COL))
+    of_all = add_up(gather(of_col, ROW, 16))
+    back = spread_backward(rows, cols, live, place, values, own + other, col_tiles)
+
+    by_y = jnp.stack(around(of_all[:8], "yl", 4))
+    by_xy = jnp.concatenate(around(by_y, "x", 4))
+    pieces = jnp.concatenate([by_xy, swap(by_xy)])
+    grad_weight = put_in_place(place, pieces).reshape(width, width)
+    grad_bias = of_all[8] + of_all[9]
     grad_mixed = add_up(exchange(back, ROW)).astype(bf16)
     grad_features = lax.dot_general(
         grad_mixed, weight, (((1,), (1,)), ((), ())), preferred_element_type=jnp.float32

time: 233 us -> 209 us (0.90)
  the two profiles are of different devices: /device:TPU:14 before, /device:TPU:1 now
where the time goes in v2:
time: 209 us; the launch traced here: 207 us
  starting transfers between devices  107 us (51%)
  waiting for transfers between devices  49 us (23%)
  blocking collectives  28.2 us (13%)
  Pallas kernels  11.7 us (6%)
  local copies, waits for them, and re-layouts  4.28 us (2%)
  other arithmetic  3.27 us (2%)
    all_to_all x6, starting transfers between devices, exchange(): return lax.all_to_all(x, axes, 0, 0, tiled=True)  60.2 us
    all_to_all x6, waiting for transfers between devices, exchange(): return lax.all_to_all(x, axes, 0, 0, tiled=True)  33.4 us
    ppermute x9, starting transfers between devices, around(): lax.ppermute(x, axis, [(i, (i + k) % size) for i in range(size)])  32.2 us
    all_to_all x2, blocking collectives, exchange(): return lax.all_to_all(x, axes, 0, 0, tiled=True)  28.2 us
    ppermute x5, starting transfers between devices, swap(): return lax.ppermute(x, 'core', [(0, 1), (1, 0)])  14.5 us
    ppermute x9, waiting for transfers between devices, around(): lax.ppermute(x, axis, [(i, (i + k) % size) for i in range(size)])  13.9 us
    pallas_call x1, Pallas kernels, spread_backward(): pl.pallas_call(backward_kernel, out_shape=jax.ShapeDtypeStruct((col_tiles...  5.71 us
    pallas_call x1, Pallas kernels, spread_forward(): pl.pallas_call(forward_kernel, out_shape=jax.ShapeDtypeStruct((row_tiles,...  4.25 us
  transfers between devices with their start and end apart: 20, of which 8 were waited for; matrix products, arithmetic and copies ran while one was open for 1% of the time, Pallas kernels for 4%

profile of v2, /device:TPU:1, one launch (start us, length us, event | category | flops | bytes accessed | tf_op | source)
XLA Modules:
  0.0 207.2 jit_solution(3404529560143985532)
XLA Ops:
  0.7 2.0 broadcast_in_dim.14
  2.6 16.2 %all-to-all-start = ((bf16[16,128,256]{2,1,0:T(8,128)(2,1)}), bf16[16,128,256]{2,1,0:T(8,128)(2,1)S(1)}, u32[]{:S(2)}, u32[]{:S(2)}) async-start(bf16[16,128,256]{2,1,0:T(8,128)(2,1)} %broadcast_in_dim.14), calls=%async_computation | async-start | bytes 2097152 | tf_op jit(solution)/shard_map/all_to_all | solution.py:179
  19.5 22.7 %all-to-all-done.src = bf16[16,128,256]{2,1,0:T(8,128)(2,1)S(1)} async-done(((bf16[16,128,256]{2,1,0:T(8,128)(2,1)}), bf16[16,128,256]{2,1,0:T(8,128)(2,1)S(1)}, u32[]{:S(2)}, u32[]{:S(2)}) %all-to-all-start) | async-done | bytes 1048608 | tf_op jit(solution)/shard_map/all_to_all | solution.py:179
  42.3 4.2 %forward_tiles.1 = bf16[32,128,256]{2,1,0:T(8,128)(2,1)S(1)} custom-call(s32[128]{0:T(128)S(1)} %bitcast.36, s32[128]{0:T(128)S(1)} %bitcast.38, s32[1]{0:T(128)} %bitcast.33.live_ref, bf16[128,128,128]{2,1,0:T(8,128)(2,1)} %bitcast.40, bf16[16,128,256]{2,1,0:T(8,128)(2,1)S(1)} %all-to-all-done.src), custom_call_target="tpu_custom_call" | custom-call | flops 1073741824 | bytes 4194304 | tf_op jit(solution)/shard_map/forward_tiles/pallas_call | solution.py:123
  46.5 8.5 %all_to_all.40 = bf16[2,16,128,256]{3,2,1,0:T(8,128)(2,1)S(1)} all-to-all(bf16[2,16,128,256]{3,2,1,0:T(8,128)(2,1)S(1)} %bitcast.35), channel_id=1, replica_groups=mesh['yh'=2,'z'=8,'yl'=4,'x'=4,'core'=2] {'core'}, dimensions={0} | all-to-all | bytes 4194304 | tf_op jit(solution)/shard_map/all_to_all | solution.py:179
  55.7 19.8 %all_to_all.41 = bf16[4,4,128,256]{3,2,1,0:T(8,128)(2,1)S(1)} all-to-all(bf16[4,4,128,256]{3,2,1,0:T(8,128)(2,1)S(1)} %bitcast.42), channel_id=1, replica_groups=mesh['yh'=2,'z'=8,'yl'=4,'x'=4,'core'=2] {'x'}, dimensions={0} | all-to-all | bytes 2097152 | tf_op jit(solution)/shard_map/all_to_all | solution.py:179
  76.4 11.6 %all-to-all-start.3 = ((bf16[4,128,256]{2,1,0:T(8,128)(2,1)}), bf16[4,128,256]{2,1,0:T(8,128)(2,1)S(1)}, u32[]{:S(2)}, u32[]{:S(2)}) async-start(bf16[4,128,256]{2,1,0:T(8,128)(2,1)} %reduce_sum.75), calls=%async_computation.3 | async-start | bytes 524288 | tf_op jit(solution)/shard_map/all_to_all | solution.py:179
  88.1 5.6 %all-to-all-done.3 = bf16[4,128,256]{2,1,0:T(8,128)(2,1)S(1)} async-done(((bf16[4,128,256]{2,1,0:T(8,128)(2,1)}), bf16[4,128,256]{2,1,0:T(8,128)(2,1)S(1)}, u32[]{:S(2)}, u32[]{:S(2)}) %all-to-all-start.3) | async-done | bytes 262176 | tf_op jit(solution)/shard_map/all_to_all | solution.py:179
  95.3 5.5 %all-to-all-start.4 = ((bf16[4,128,256]{2,1,0:T(8,128)(2,1)}), bf16[4,128,256]{2,1,0:T(8,128)(2,1)S(1)}, u32[]{:S(2)}, u32[]{:S(2)}) async-start(bf16[4,128,256]{2,1,0:T(8,128)(2,1)} %broadcast_in_dim.16), calls=%async_computation.4 | async-start | bytes 524288 | tf_op jit(solution)/shard_map/all_to_all | solution.py:179
  101.9 4.5 %all-to-all-done.4.refs_0_ = bf16[4,128,256]{2,1,0:T(8,128)(2,1)S(1)} async-done(((bf16[4,128,256]{2,1,0:T(8,128)(2,1)}), bf16[4,128,256]{2,1,0:T(8,128)(2,1)S(1)}, u32[]{:S(2)}, u32[]{:S(2)}) %all-to-all-start.4) | async-done | bytes 262176 | tf_op jit(solution)/shard_map/all_to_all | solution.py:179
  106.5 7.7 %all-to-all-start.6 = ((bf16[32,16,256]{2,1,0:T(8,128)(2,1)}), bf16[32,16,256]{2,1,0:T(8,128)(2,1)S(1)}, u32[]{:S(2)}, u32[]{:S(2)}) async-start(bf16[32,16,256]{2,1,0:T(8,128)(2,1)} %pad_maximum_fusion), calls=%async_computation.6 | async-start | bytes 524288 | tf_op jit(solution)/shard_map/all_to_all | solution.py:179
  114.1 3.3 %collective-permute-start = (bf16[4,128,256]{2,1,0:T(8,128)(2,1)S(1)}, bf16[4,128,256]{2,1,0:T(8,128)(2,1)S(1)}, u32[]{:S(2)}, u32[]{:S(2)}) collective-permute-start(bf16[4,128,256]{2,1,0:T(8,128)(2,1)S(1)} %all-to-all-done.4.refs_0_), channel_id=1, source_target_pairs={{0,2},{2,4},{4,6},{6,0},{1,3},{3,5},{5,7},{7,1},{8,10},{10,12},{12... | collective-permute-start | bytes 786440 | tf_op jit(solution)/shard_map/ppermute | solution.py:171
  117.4 4.3 %collective-permute-start.1 = (bf16[4,128,256]{2,1,0:T(8,128)(2,1)S(1)}, bf16[4,128,256]{2,1,0:T(8,128)(2,1)S(1)}, u32[]{:S(2)}, u32[]{:S(2)}) collective-permute-start(bf16[4,128,256]{2,1,0:T(8,128)(2,1)S(1)} %all-to-all-done.4.refs_0_), channel_id=1, source_target_pairs={{0,4},{2,6},{4,0},{6,2},{1,5},{3,7},{5,1},{7,3},{8,12},{10,14},{12... | collective-permute-start | bytes 786440 | tf_op jit(solution)/shard_map/ppermute | solution.py:171
  121.8 3.1 %collective-permute-start.2 = (bf16[4,128,256]{2,1,0:T(8,128)(2,1)S(1)}, bf16[4,128,256]{2,1,0:T(8,128)(2,1)S(1)}, u32[]{:S(2)}, u32[]{:S(2)}) collective-permute-start(bf16[4,128,256]{2,1,0:T(8,128)(2,1)S(1)} %all-to-all-done.4.refs_0_), channel_id=1, source_target_pairs={{0,6},{2,0},{4,2},{6,4},{1,7},{3,1},{5,3},{7,5},{8,14},{10,8},{12,... | collective-permute-start | bytes 786440 | tf_op jit(solution)/shard_map/ppermute | solution.py:171
  126.1 6.5 %all-to-all-start.7 = ((f32[16,16,256]{2,1,0:T(8,128)}), f32[16,16,256]{2,1,0:T(8,128)S(1)}, u32[]{:S(2)}, u32[]{:S(2)}) async-start(f32[16,16,256]{2,1,0:T(8,128)} %broadcast_in_dim.19), calls=%async_computation.7 | async-start | bytes 524288 | tf_op jit(solution)/shard_map/all_to_all | solution.py:179
  132.6 2.9 %collective-permute-start.3 = (bf16[4,128,256]{2,1,0:T(8,128)(2,1)S(1)}, bf16[4,128,256]{2,1,0:T(8,128)(2,1)S(1)}, u32[]{:S(2)}, u32[]{:S(2)}) collective-permute-start(bf16[4,128,256]{2,1,0:T(8,128)(2,1)S(1)} %all-to-all-done.4.refs_0_), channel_id=1, source_target_pairs={{0,1},{1,0},{2,3},{3,2},{4,5},{5,4},{6,7},{7,6},{8,9},{9,8},{10,11... | collective-permute-start | bytes 786440 | tf_op jit(solution)/shard_map/ppermute | solution.py:175
  135.5 1.9 collective-permute-start.4
  137.5 2.4 %collective-permute-start.5 = (bf16[4,128,256]{2,1,0:T(8,128)(2,1)S(1)}, bf16[4,128,256]{2,1,0:T(8,128)(2,1)S(1)}, u32[]{:S(2)}, u32[]{:S(2)}) collective-permute-start(bf16[4,128,256]{2,1,0:T(8,128)(2,1)S(1)} %collective-permute-done.1.refs_2_), channel_id=1, source_target_pairs={{0,1},{1,0},{2,3},{3,2},{4,5},{5,4},{6,7},{7,6},{8,9},{9,8},{10,11... | collective-permute-start | bytes 786440 | tf_op jit(solution)/shard_map/ppermute | solution.py:175
  139.9 1.9 collective-permute-start.6
  141.9 1.4 collective-permute-done.6.refs_7_
  143.3 5.7 %backward_tiles.1 = bf16[16,128,256]{2,1,0:T(8,128)(2,1)} custom-call(s32[128]{0:T(128)S(1)} %bitcast.37, s32[128]{0:T(128)S(1)} %bitcast.39, s32[1]{0:T(128)} %bitcast.34.live_ref, s32[3]{0:T(128)S(1)} %pad_add_fusion.place, bf16[128,128,128]{2,1,0:T(8,128)(2,1)} %bitcast.41, bf16[4,128,256]{2,1,0:T(8,128)(2,1)S(1)} %all-to-all-done.4.refs_0_, ...), custom_call_target="tpu_custom_call" | custom-call | flops 1073741824 | bytes 4194304 | tf_op jit(solution)/shard_map/backward_tiles/pallas_call | solution.py:142
  149.1 12.8 %all-to-all-start.5 = ((bf16[16,128,256]{2,1,0:T(8,128)(2,1)}), bf16[16,128,256]{2,1,0:T(8,128)(2,1)S(1)}, u32[]{:S(2)}, u32[]{:S(2)}) async-start(bf16[16,128,256]{2,1,0:T(8,128)(2,1)} %backward_tiles.1), calls=%async_computation.5 | async-start | bytes 2097152 | tf_op jit(solution)/shard_map/all_to_all | solution.py:179
  161.9 2.5 %collective-permute-start.7 = (f32[8,256]{1,0:T(8,128)S(1)}, f32[8,256]{1,0:T(8,128)S(1)}, u32[]{:S(2)}, u32[]{:S(2)}) collective-permute-start(f32[8,256]{1,0:T(8,128)S(1)} %get-tuple-element.16), channel_id=1, source_target_pairs={{0,8},{8,16},{16,24},{24,0},{1,9},{9,17},{17,25},{25,1},{2,10},{10... | collective-permute-start | bytes 24584 | tf_op jit(solution)/shard_map/ppermute | solution.py:171
  164.4 7.3 %collective-permute-start.8 = (f32[8,256]{1,0:T(8,128)S(1)}, f32[8,256]{1,0:T(8,128)S(1)}, u32[]{:S(2)}, u32[]{:S(2)}) collective-permute-start(f32[8,256]{1,0:T(8,128)S(1)} %get-tuple-element.16), channel_id=1, source_target_pairs={{0,16},{8,24},{16,0},{24,8},{1,17},{9,25},{17,1},{25,9},{2,18},{10... | collective-permute-start | bytes 24584 | tf_op jit(solution)/shard_map/ppermute | solution.py:171
  171.7 2.4 %collective-permute-start.9 = (f32[8,256]{1,0:T(8,128)S(1)}, f32[8,256]{1,0:T(8,128)S(1)}, u32[]{:S(2)}, u32[]{:S(2)}) collective-permute-start(f32[8,256]{1,0:T(8,128)S(1)} %get-tuple-element.16), channel_id=1, source_target_pairs={{0,24},{8,0},{16,8},{24,16},{1,25},{9,1},{17,9},{25,17},{2,26},{10... | collective-permute-start | bytes 24584 | tf_op jit(solution)/shard_map/ppermute | solution.py:171
  174.2 12.6 %collective-permute-done.7 = f32[8,256]{1,0:T(8,128)S(1)} collective-permute-done((f32[8,256]{1,0:T(8,128)S(1)}, f32[8,256]{1,0:T(8,128)S(1)}, u32[]{:S(2)}, u32[]{:S(2)}) %collective-permute-start.7) | collective-permute-done | bytes 8224 | tf_op jit(solution)/shard_map/ppermute | solution.py:171
  186.8 3.0 %collective-permute-start.10 = (f32[4,8,256]{2,1,0:T(8,128)S(1)}, f32[4,8,256]{2,1,0:T(8,128)S(1)}, u32[]{:S(2)}, u32[]{:S(2)}) collective-permute-start(f32[4,8,256]{2,1,0:T(8,128)S(1)} %pad_maximum_fusion.1), channel_id=1, source_target_pairs={{0,2},{2,4},{4,6},{6,0},{1,3},{3,5},{5,7},{7,1},{8,10},{10,12},{12... | collective-permute-start | bytes 98312 | tf_op jit(solution)/shard_map/ppermute | solution.py:171
  189.8 3.0 %collective-permute-start.11 = (f32[4,8,256]{2,1,0:T(8,128)S(1)}, f32[4,8,256]{2,1,0:T(8,128)S(1)}, u32[]{:S(2)}, u32[]{:S(2)}) collective-permute-start(f32[4,8,256]{2,1,0:T(8,128)S(1)} %pad_maximum_fusion.1), channel_id=1, source_target_pairs={{0,4},{2,6},{4,0},{6,2},{1,5},{3,7},{5,1},{7,3},{8,12},{10,14},{12... | collective-permute-start | bytes 98312 | tf_op jit(solution)/shard_map/ppermute | solution.py:171
  192.8 3.3 %collective-permute-start.12 = (f32[4,8,256]{2,1,0:T(8,128)S(1)}, f32[4,8,256]{2,1,0:T(8,128)S(1)}, u32[]{:S(2)}, u32[]{:S(2)}) collective-permute-start(f32[4,8,256]{2,1,0:T(8,128)S(1)} %pad_maximum_fusion.1), channel_id=1, source_target_pairs={{0,6},{2,0},{4,2},{6,4},{1,7},{3,1},{5,3},{7,5},{8,14},{10,8},{12,... | collective-permute-start | bytes 98312 | tf_op jit(solution)/shard_map/ppermute | solution.py:171
  196.1 1.3 collective-permute-done.12
  197.4 5.4 %collective-permute-start.13 = (f32[16,8,256]{2,1,0:T(8,128)S(1)}, f32[16,8,256]{2,1,0:T(8,128)S(1)}, u32[]{:S(2)}, u32[]{:S(2)}) collective-permute-start(f32[16,8,256]{2,1,0:T(8,128)S(1)} %get-tuple-element.7), channel_id=1, source_target_pairs={{0,1},{1,0},{2,3},{3,2},{4,5},{5,4},{6,7},{7,6},{8,9},{9,8},{10,11... | collective-permute-start | bytes 393224 | tf_op jit(solution)/shard_map/ppermute | solution.py:175
  204.5 1.7 place_pieces.1
  (58 shorter events, 8.6 us)
Async XLA Ops:
  0.6 93.0 %copy-start = (bf16[256,256]{1,0:T(8,128)(2,1)S(1)}, bf16[256,256]{1,0:T(8,128)(2,1)}, u32[]{:S(2)}) copy-start(bf16[256,256]{1,0:T(8,128)(2,1)} %param.9) | copy-start | bytes 393220
  0.6 41.6 %copy-start.2 = (s32[1,1,128]{2,1,0:T(1,128)S(1)}, s32[1,1,128]{2,1,0:T(1,128)}, u32[]{:S(2)}) copy-start(s32[1,1,128]{2,1,0:T(1,128)} %param.12) | copy-start | bytes 1540
  0.7 41.6 %copy-start.3 = (s32[1,1,128]{2,1,0:T(1,128)S(1)}, s32[1,1,128]{2,1,0:T(1,128)}, u32[]{:S(2)}) copy-start(s32[1,1,128]{2,1,0:T(1,128)} %param.13) | copy-start | bytes 1540
  2.6 39.6 %all-to-all-start = ((bf16[16,128,256]{2,1,0:T(8,128)(2,1)}), bf16[16,128,256]{2,1,0:T(8,128)(2,1)S(1)}, u32[]{:S(2)}, u32[]{:S(2)}) async-start(bf16[16,128,256]{2,1,0:T(8,128)(2,1)} %broadcast_in_dim.14), calls=%async_computation | async-start | bytes 2097152 | tf_op jit(solution)/shard_map/all_to_all | solution.py:179
  55.7 38.0 %copy-start.5 = (bf16[128,256]{1,0:T(8,128)(2,1)S(1)}, bf16[128,256]{1,0:T(8,128)(2,1)}, u32[]{:S(2)}) copy-start(bf16[128,256]{1,0:T(8,128)(2,1)} %param.11) | copy-start | bytes 196612
  55.7 38.0 %copy-start.6 = (f32[256]{0:T(256)S(1)}, f32[256]{0:T(256)}, u32[]{:S(2)}) copy-start(f32[256]{0:T(256)} %param.10) | copy-start | bytes 3076
  76.4 17.3 %all-to-all-start.3 = ((bf16[4,128,256]{2,1,0:T(8,128)(2,1)}), bf16[4,128,256]{2,1,0:T(8,128)(2,1)S(1)}, u32[]{:S(2)}, u32[]{:S(2)}) async-start(bf16[4,128,256]{2,1,0:T(8,128)(2,1)} %reduce_sum.75), calls=%async_computation.3 | async-start | bytes 524288 | tf_op jit(solution)/shard_map/all_to_all | solution.py:179
  95.3 11.1 %all-to-all-start.4 = ((bf16[4,128,256]{2,1,0:T(8,128)(2,1)}), bf16[4,128,256]{2,1,0:T(8,128)(2,1)S(1)}, u32[]{:S(2)}, u32[]{:S(2)}) async-start(bf16[4,128,256]{2,1,0:T(8,128)(2,1)} %broadcast_in_dim.16), calls=%async_computation.4 | async-start | bytes 524288 | tf_op jit(solution)/shard_map/all_to_all | solution.py:179
  106.5 18.9 %all-to-all-start.6 = ((bf16[32,16,256]{2,1,0:T(8,128)(2,1)}), bf16[32,16,256]{2,1,0:T(8,128)(2,1)S(1)}, u32[]{:S(2)}, u32[]{:S(2)}) async-start(bf16[32,16,256]{2,1,0:T(8,128)(2,1)} %pad_maximum_fusion), calls=%async_computation.6 | async-start | bytes 524288 | tf_op jit(solution)/shard_map/all_to_all | solution.py:179
  114.1 21.4 %collective-permute-start = (bf16[4,128,256]{2,1,0:T(8,128)(2,1)S(1)}, bf16[4,128,256]{2,1,0:T(8,128)(2,1)S(1)}, u32[]{:S(2)}, u32[]{:S(2)}) collective-permute-start(bf16[4,128,256]{2,1,0:T(8,128)(2,1)S(1)} %all-to-all-done.4.refs_0_), channel_id=1, source_target_pairs={{0,2},{2,4},{4,6},{6,0},{1,3},{3,5},{5,7},{7,1},{8,10},{10,12},{12... | collective-permute-start | bytes 786440 | tf_op jit(solution)/shard_map/ppermute | solution.py:171
  117.4 20.0 %collective-permute-start.1 = (bf16[4,128,256]{2,1,0:T(8,128)(2,1)S(1)}, bf16[4,128,256]{2,1,0:T(8,128)(2,1)S(1)}, u32[]{:S(2)}, u32[]{:S(2)}) collective-permute-start(bf16[4,128,256]{2,1,0:T(8,128)(2,1)S(1)} %all-to-all-done.4.refs_0_), channel_id=1, source_target_pairs={{0,4},{2,6},{4,0},{6,2},{1,5},{3,7},{5,1},{7,3},{8,12},{10,14},{12... | collective-permute-start | bytes 786440 | tf_op jit(solution)/shard_map/ppermute | solution.py:171
  121.8 18.1 %collective-permute-start.2 = (bf16[4,128,256]{2,1,0:T(8,128)(2,1)S(1)}, bf16[4,128,256]{2,1,0:T(8,128)(2,1)S(1)}, u32[]{:S(2)}, u32[]{:S(2)}) collective-permute-start(bf16[4,128,256]{2,1,0:T(8,128)(2,1)S(1)} %all-to-all-done.4.refs_0_), channel_id=1, source_target_pairs={{0,6},{2,0},{4,2},{6,4},{1,7},{3,1},{5,3},{7,5},{8,14},{10,8},{12,... | collective-permute-start | bytes 786440 | tf_op jit(solution)/shard_map/ppermute | solution.py:171
  126.1 22.9 %all-to-all-start.7 = ((f32[16,16,256]{2,1,0:T(8,128)}), f32[16,16,256]{2,1,0:T(8,128)S(1)}, u32[]{:S(2)}, u32[]{:S(2)}) async-start(f32[16,16,256]{2,1,0:T(8,128)} %broadcast_in_dim.19), calls=%async_computation.7 | async-start | bytes 524288 | tf_op jit(solution)/shard_map/all_to_all | solution.py:179
  132.6 9.3 %collective-permute-start.3 = (bf16[4,128,256]{2,1,0:T(8,128)(2,1)S(1)}, bf16[4,128,256]{2,1,0:T(8,128)(2,1)S(1)}, u32[]{:S(2)}, u32[]{:S(2)}) collective-permute-start(bf16[4,128,256]{2,1,0:T(8,128)(2,1)S(1)} %all-to-all-done.4.refs_0_), channel_id=1, source_target_pairs={{0,1},{1,0},{2,3},{3,2},{4,5},{5,4},{6,7},{7,6},{8,9},{9,8},{10,11... | collective-permute-start | bytes 786440 | tf_op jit(solution)/shard_map/ppermute | solution.py:175
  135.5 6.4 %collective-permute-start.4 = (bf16[4,128,256]{2,1,0:T(8,128)(2,1)S(1)}, bf16[4,128,256]{2,1,0:T(8,128)(2,1)S(1)}, u32[]{:S(2)}, u32[]{:S(2)}) collective-permute-start(bf16[4,128,256]{2,1,0:T(8,128)(2,1)S(1)} %collective-permute-done.refs_1_), channel_id=1, source_target_pairs={{0,1},{1,0},{2,3},{3,2},{4,5},{5,4},{6,7},{7,6},{8,9},{9,8},{10,11... | collective-permute-start | bytes 786440 | tf_op jit(solution)/shard_map/ppermute | solution.py:175
  137.5 4.5 %collective-permute-start.5 = (bf16[4,128,256]{2,1,0:T(8,128)(2,1)S(1)}, bf16[4,128,256]{2,1,0:T(8,128)(2,1)S(1)}, u32[]{:S(2)}, u32[]{:S(2)}) collective-permute-start(bf16[4,128,256]{2,1,0:T(8,128)(2,1)S(1)} %collective-permute-done.1.refs_2_), channel_id=1, source_target_pairs={{0,1},{1,0},{2,3},{3,2},{4,5},{5,4},{6,7},{7,6},{8,9},{9,8},{10,11... | collective-permute-start | bytes 786440 | tf_op jit(solution)/shard_map/ppermute | solution.py:175
  139.9 3.4 %collective-permute-start.6 = (bf16[4,128,256]{2,1,0:T(8,128)(2,1)S(1)}, bf16[4,128,256]{2,1,0:T(8,128)(2,1)S(1)}, u32[]{:S(2)}, u32[]{:S(2)}) collective-permute-start(bf16[4,128,256]{2,1,0:T(8,128)(2,1)S(1)} %collective-permute-done.2.refs_3_), channel_id=1, source_target_pairs={{0,1},{1,0},{2,3},{3,2},{4,5},{5,4},{6,7},{7,6},{8,9},{9,8},{10,11... | collective-permute-start | bytes 786440 | tf_op jit(solution)/shard_map/ppermute | solution.py:175
  141.9 7.1 %copy-start.1 = (s32[3]{0:T(128)}, s32[3]{0:T(128)S(1)}, u32[]{:S(2)}) copy-start(s32[3]{0:T(128)S(1)} %pad_add_fusion.place) | copy-start | bytes 40
  149.1 57.1 %all-to-all-start.5 = ((bf16[16,128,256]{2,1,0:T(8,128)(2,1)}), bf16[16,128,256]{2,1,0:T(8,128)(2,1)S(1)}, u32[]{:S(2)}, u32[]{:S(2)}) async-start(bf16[16,128,256]{2,1,0:T(8,128)(2,1)} %backward_tiles.1), calls=%async_computation.5 | async-start | bytes 2097152 | tf_op jit(solution)/shard_map/all_to_all | solution.py:179
  161.9 24.8 %collective-permute-start.7 = (f32[8,256]{1,0:T(8,128)S(1)}, f32[8,256]{1,0:T(8,128)S(1)}, u32[]{:S(2)}, u32[]{:S(2)}) collective-permute-start(f32[8,256]{1,0:T(8,128)S(1)} %get-tuple-element.16), channel_id=1, source_target_pairs={{0,8},{8,16},{16,24},{24,0},{1,9},{9,17},{17,25},{25,1},{2,10},{10... | collective-permute-start | bytes 24584 | tf_op jit(solution)/shard_map/ppermute | solution.py:171
  164.4 22.4 %collective-permute-start.8 = (f32[8,256]{1,0:T(8,128)S(1)}, f32[8,256]{1,0:T(8,128)S(1)}, u32[]{:S(2)}, u32[]{:S(2)}) collective-permute-start(f32[8,256]{1,0:T(8,128)S(1)} %get-tuple-element.16), channel_id=1, source_target_pairs={{0,16},{8,24},{16,0},{24,8},{1,17},{9,25},{17,1},{25,9},{2,18},{10... | collective-permute-start | bytes 24584 | tf_op jit(solution)/shard_map/ppermute | solution.py:171
  171.7 15.0 %collective-permute-start.9 = (f32[8,256]{1,0:T(8,128)S(1)}, f32[8,256]{1,0:T(8,128)S(1)}, u32[]{:S(2)}, u32[]{:S(2)}) collective-permute-start(f32[8,256]{1,0:T(8,128)S(1)} %get-tuple-element.16), channel_id=1, source_target_pairs={{0,24},{8,0},{16,8},{24,16},{1,25},{9,1},{17,9},{25,17},{2,26},{10... | collective-permute-start | bytes 24584 | tf_op jit(solution)/shard_map/ppermute | solution.py:171
  186.8 9.3 %collective-permute-start.10 = (f32[4,8,256]{2,1,0:T(8,128)S(1)}, f32[4,8,256]{2,1,0:T(8,128)S(1)}, u32[]{:S(2)}, u32[]{:S(2)}) collective-permute-start(f32[4,8,256]{2,1,0:T(8,128)S(1)} %pad_maximum_fusion.1), channel_id=1, source_target_pairs={{0,2},{2,4},{4,6},{6,0},{1,3},{3,5},{5,7},{7,1},{8,10},{10,12},{12... | collective-permute-start | bytes 98312 | tf_op jit(solution)/shard_map/ppermute | solution.py:171
  189.8 6.3 %collective-permute-start.11 = (f32[4,8,256]{2,1,0:T(8,128)S(1)}, f32[4,8,256]{2,1,0:T(8,128)S(1)}, u32[]{:S(2)}, u32[]{:S(2)}) collective-permute-start(f32[4,8,256]{2,1,0:T(8,128)S(1)} %pad_maximum_fusion.1), channel_id=1, source_target_pairs={{0,4},{2,6},{4,0},{6,2},{1,5},{3,7},{5,1},{7,3},{8,12},{10,14},{12... | collective-permute-start | bytes 98312 | tf_op jit(solution)/shard_map/ppermute | solution.py:171
  192.8 4.7 %collective-permute-start.12 = (f32[4,8,256]{2,1,0:T(8,128)S(1)}, f32[4,8,256]{2,1,0:T(8,128)S(1)}, u32[]{:S(2)}, u32[]{:S(2)}) collective-permute-start(f32[4,8,256]{2,1,0:T(8,128)S(1)} %pad_maximum_fusion.1), channel_id=1, source_target_pairs={{0,6},{2,0},{4,2},{6,4},{1,7},{3,1},{5,3},{7,5},{8,14},{10,8},{12,... | collective-permute-start | bytes 98312 | tf_op jit(solution)/shard_map/ppermute | solution.py:171
  197.4 6.3 %collective-permute-start.13 = (f32[16,8,256]{2,1,0:T(8,128)S(1)}, f32[16,8,256]{2,1,0:T(8,128)S(1)}, u32[]{:S(2)}, u32[]{:S(2)}) collective-permute-start(f32[16,8,256]{2,1,0:T(8,128)S(1)} %get-tuple-element.7), channel_id=1, source_target_pairs={{0,1},{1,0},{2,3},{3,2},{4,5},{5,4},{6,7},{7,6},{8,9},{9,8},{10,11... | collective-permute-start | bytes 393224 | tf_op jit(solution)/shard_map/ppermute | solution.py:175
  203.8 0.7 copy-start.4

commit v3 on v2

--- a/solution.py
+++ b/solution.py
@@ -10,7 +10,7 @@
 COL = ("yl", "x", "core")
 ALL = ROW + COL
 CHUNK = 16
-GROUP = 4
+GROUP = 16
 
 
 def elu_value(pre):
@@ -94,15 +94,6 @@
 
     walk(copies, live, step)
     out[...] = acc[:tiles].astype(out.dtype)
-
-
-def place_kernel(place, pieces, out):
-    core, x, y = place[0], place[1], place[2]
-    for kc in range(2):
-        for kx in range(4):
-            for ky in range(4):
-                to = ((y - ky) & 3) * 8 + ((x - kx) & 3) * 2 + (core ^ kc)
-                out[to] = pieces[kc * 16 + kx * 4 + ky]
 
 
 SMEM = pl.BlockSpec(memory_space=pltpu.SMEM)
@@ -157,16 +148,6 @@
     )(rows, cols, live, place, values, *blocks)
 
 
-def put_in_place(place, pieces):
-    return pl.pallas_call(
-        place_kernel,
-        out_shape=jax.ShapeDtypeStruct(pieces.shape, pieces.dtype),
-        in_specs=[SMEM, VMEM],
-        out_specs=VMEM,
-        name="place_pieces",
-    )(place, pieces)
-
-
 def around(x, axis, size):
     return [x] + [lax.ppermute(x, axis, [(i, (i + k) % size) for i in range(size)]) for k in range(1, size)]
 
@@ -204,7 +185,7 @@
     side, width = features.shape
     row_tiles, col_tiles = 32, 16
     bf16 = jnp.bfloat16
-    place = jnp.stack([lax.axis_index(axis) for axis in ("core", "x", "yl")]).astype(jnp.int32)
+    place = jnp.stack([lax.axis_index(axis) for axis in ("core", "x")]).astype(jnp.int32)
 
     block = gather(features, ROW, col_tiles)
     partial = spread_forward(rows, cols, live, values, block, row_tiles)
@@ -229,13 +210,11 @@
     other = [swap(block) for block in own]
     of_col = add_up(exchange(terms, COL))
     of_all = add_up(gather(of_col, ROW, 16))
-    back = spread_backward(rows, cols, live, place, values, own + other, col_tiles)
-
-    by_y = jnp.stack(around(of_all[:8], "yl", 4))
-    by_xy = jnp.concatenate(around(by_y, "x", 4))
-    pieces = jnp.concatenate([by_xy, swap(by_xy)])
-    grad_weight = put_in_place(place, pieces).reshape(width, width)
+    copies = jnp.broadcast_to(of_all[None, :8], (32, 8, width))
+    copies, blocks = lax.optimization_barrier((copies, own + other))
+    grad_weight = exchange(copies, COL).reshape(width, width)
     grad_bias = of_all[8] + of_all[9]
+    back = spread_backward(rows, cols, live, place, values, blocks, col_tiles)
     grad_mixed = add_up(exchange(back, ROW)).astype(bf16)
     grad_features = lax.dot_general(
         grad_mixed, weight, (((1,), (1,)), ((), ())), preferred_element_type=jnp.float32

time: 209 us -> 202 us (0.967)
  the two profiles are of different devices: /device:TPU:1 before, /device:TPU:8 now
where the time goes in v3:
time: 202 us; the launch traced here: 201 us
  waiting for transfers between devices  87.7 us (43%)
  starting transfers between devices  68 us (34%)
  blocking collectives  24.3 us (12%)
  Pallas kernels  8.64 us (4%)
  local copies, waits for them, and re-layouts  4.94 us (2%)
  other arithmetic  3.27 us (2%)
  matrix products  2.06 us (1%)
    all_to_all x7, waiting for transfers between devices, exchange(): return lax.all_to_all(x, axes, 0, 0, tiled=True)  87.6 us
    all_to_all x7, starting transfers between devices, exchange(): return lax.all_to_all(x, axes, 0, 0, tiled=True)  48.1 us
    all_to_all x2, blocking collectives, exchange(): return lax.all_to_all(x, axes, 0, 0, tiled=True)  24.3 us
    ppermute x3, starting transfers between devices, around(): lax.ppermute(x, axis, [(i, (i + k) % size) for i in range(size)])  11.3 us
    ppermute x4, starting transfers between devices, swap(): return lax.ppermute(x, 'core', [(0, 1), (1, 0)])  8.65 us
    pallas_call x1, Pallas kernels, spread_backward(): pl.pallas_call(backward_kernel, out_shape=jax.ShapeDtypeStruct((col_tiles...  4.93 us
  transfers between devices with their start and end apart: 14, of which 6 were waited for; matrix products, arithmetic and copies ran while one was open for 1% of the time, Pallas kernels for 2%

profile of v3, /device:TPU:8, one launch (start us, length us, event | category | flops | bytes accessed | tf_op | source)
XLA Modules:
  0.0 200.5 jit_solution(7991218361252403298)
XLA Ops:
  0.7 1.9 broadcast_in_dim.16
  2.6 14.8 %all-to-all-start = ((bf16[16,128,256]{2,1,0:T(8,128)(2,1)}), bf16[16,128,256]{2,1,0:T(8,128)(2,1)S(1)}, u32[]{:S(2)}, u32[]{:S(2)}) async-start(bf16[16,128,256]{2,1,0:T(8,128)(2,1)} %broadcast_in_dim.16), calls=%async_computation | async-start | bytes 2097152 | tf_op jit(solution)/shard_map/all_to_all | solution.py:160
  18.0 32.7 %all-to-all-done.src = bf16[16,128,256]{2,1,0:T(8,128)(2,1)S(1)} async-done(((bf16[16,128,256]{2,1,0:T(8,128)(2,1)}), bf16[16,128,256]{2,1,0:T(8,128)(2,1)S(1)}, u32[]{:S(2)}, u32[]{:S(2)}) %all-to-all-start) | async-done | bytes 1048608 | tf_op jit(solution)/shard_map/all_to_all | solution.py:160
  50.8 3.7 %forward_tiles.1 = bf16[32,128,256]{2,1,0:T(8,128)(2,1)S(1)} custom-call(s32[128]{0:T(128)S(1)} %bitcast.22, s32[128]{0:T(128)S(1)} %bitcast.24, s32[1]{0:T(128)} %bitcast.19.live_ref, bf16[128,128,128]{2,1,0:T(8,128)(2,1)} %bitcast.26, bf16[16,128,256]{2,1,0:T(8,128)(2,1)S(1)} %all-to-all-done.src), custom_call_target="tpu_custom_call" | custom-call | flops 1073741824 | bytes 4194304 | tf_op jit(solution)/shard_map/forward_tiles/pallas_call | solution.py:114
  54.5 5.4 %all_to_all.45 = bf16[2,16,128,256]{3,2,1,0:T(8,128)(2,1)S(1)} all-to-all(bf16[2,16,128,256]{3,2,1,0:T(8,128)(2,1)S(1)} %bitcast.21), channel_id=1, replica_groups=mesh['yh'=2,'z'=8,'yl'=4,'x'=4,'core'=2] {'core'}, dimensions={0} | all-to-all | bytes 4194304 | tf_op jit(solution)/shard_map/all_to_all | solution.py:160
  60.6 18.9 %all_to_all.46 = bf16[4,4,128,256]{3,2,1,0:T(8,128)(2,1)S(1)} all-to-all(bf16[4,4,128,256]{3,2,1,0:T(8,128)(2,1)S(1)} %bitcast.28), channel_id=1, replica_groups=mesh['yh'=2,'z'=8,'yl'=4,'x'=4,'core'=2] {'x'}, dimensions={0} | all-to-all | bytes 2097152 | tf_op jit(solution)/shard_map/all_to_all | solution.py:160
  79.5 0.9 reduce_sum.75
  80.4 3.4 %all-to-all-start.3 = ((bf16[4,128,256]{2,1,0:T(8,128)(2,1)}), bf16[4,128,256]{2,1,0:T(8,128)(2,1)S(1)}, u32[]{:S(2)}, u32[]{:S(2)}) async-start(bf16[4,128,256]{2,1,0:T(8,128)(2,1)} %reduce_sum.75), calls=%async_computation.3 | async-start | bytes 524288 | tf_op jit(solution)/shard_map/all_to_all | solution.py:160
  83.9 6.1 %all-to-all-done.3 = bf16[4,128,256]{2,1,0:T(8,128)(2,1)S(1)} async-done(((bf16[4,128,256]{2,1,0:T(8,128)(2,1)}), bf16[4,128,256]{2,1,0:T(8,128)(2,1)S(1)}, u32[]{:S(2)}, u32[]{:S(2)}) %all-to-all-start.3) | async-done | bytes 262176 | tf_op jit(solution)/shard_map/all_to_all | solution.py:160
  90.1 0.9 convert_reduce_fusion.2
  91.0 0.7 broadcast_in_dim.22
  91.8 5.0 %all-to-all-start.6 = ((bf16[4,128,256]{2,1,0:T(8,128)(2,1)}), bf16[4,128,256]{2,1,0:T(8,128)(2,1)S(1)}, u32[]{:S(2)}, u32[]{:S(2)}) async-start(bf16[4,128,256]{2,1,0:T(8,128)(2,1)} %broadcast_in_dim.22), calls=%async_computation.6 | async-start | bytes 524288 | tf_op jit(solution)/shard_map/all_to_all | solution.py:160
  97.2 0.7 pad_maximum_fusion
  97.9 5.1 %all-to-all-done.6.refs_0_ = bf16[4,128,256]{2,1,0:T(8,128)(2,1)S(1)} async-done(((bf16[4,128,256]{2,1,0:T(8,128)(2,1)}), bf16[4,128,256]{2,1,0:T(8,128)(2,1)S(1)}, u32[]{:S(2)}, u32[]{:S(2)}) %all-to-all-start.6) | async-done | bytes 262176 | tf_op jit(solution)/shard_map/all_to_all | solution.py:160
  103.0 4.8 %all-to-all-start.4 = ((bf16[32,16,256]{2,1,0:T(8,128)(2,1)}), bf16[32,16,256]{2,1,0:T(8,128)(2,1)S(1)}, u32[]{:S(2)}, u32[]{:S(2)}) async-start(bf16[32,16,256]{2,1,0:T(8,128)(2,1)} %pad_maximum_fusion), calls=%async_computation.4 | async-start | bytes 524288 | tf_op jit(solution)/shard_map/all_to_all | solution.py:160
  107.8 3.4 %collective-permute-start = (bf16[4,128,256]{2,1,0:T(8,128)(2,1)S(1)}, bf16[4,128,256]{2,1,0:T(8,128)(2,1)S(1)}, u32[]{:S(2)}, u32[]{:S(2)}) collective-permute-start(bf16[4,128,256]{2,1,0:T(8,128)(2,1)S(1)} %all-to-all-done.6.refs_0_), channel_id=1, source_target_pairs={{0,2},{2,4},{4,6},{6,0},{1,3},{3,5},{5,7},{7,1},{8,10},{10,12},{12... | collective-permute-start | bytes 786440 | tf_op jit(solution)/shard_map/ppermute | solution.py:152
  111.2 4.6 %collective-permute-start.1 = (bf16[4,128,256]{2,1,0:T(8,128)(2,1)S(1)}, bf16[4,128,256]{2,1,0:T(8,128)(2,1)S(1)}, u32[]{:S(2)}, u32[]{:S(2)}) collective-permute-start(bf16[4,128,256]{2,1,0:T(8,128)(2,1)S(1)} %all-to-all-done.6.refs_0_), channel_id=1, source_target_pairs={{0,4},{2,6},{4,0},{6,2},{1,5},{3,7},{5,1},{7,3},{8,12},{10,14},{12... | collective-permute-start | bytes 786440 | tf_op jit(solution)/shard_map/ppermute | solution.py:152
  115.8 3.4 %collective-permute-start.2 = (bf16[4,128,256]{2,1,0:T(8,128)(2,1)S(1)}, bf16[4,128,256]{2,1,0:T(8,128)(2,1)S(1)}, u32[]{:S(2)}, u32[]{:S(2)}) collective-permute-start(bf16[4,128,256]{2,1,0:T(8,128)(2,1)S(1)} %all-to-all-done.6.refs_0_), channel_id=1, source_target_pairs={{0,6},{2,0},{4,2},{6,4},{1,7},{3,1},{5,3},{7,5},{8,14},{10,8},{12,... | collective-permute-start | bytes 786440 | tf_op jit(solution)/shard_map/ppermute | solution.py:152
  119.2 0.7 broadcast_in_dim.20
  120.0 7.8 %all-to-all-start.5 = ((f32[16,16,256]{2,1,0:T(8,128)}), f32[16,16,256]{2,1,0:T(8,128)S(1)}, u32[]{:S(2)}, u32[]{:S(2)}) async-start(f32[16,16,256]{2,1,0:T(8,128)} %broadcast_in_dim.20), calls=%async_computation.5 | async-start | bytes 524288 | tf_op jit(solution)/shard_map/all_to_all | solution.py:160
  127.8 1.9 collective-permute-start.3
  129.7 2.4 %collective-permute-start.4 = (bf16[4,128,256]{2,1,0:T(8,128)(2,1)S(1)}, bf16[4,128,256]{2,1,0:T(8,128)(2,1)S(1)}, u32[]{:S(2)}, u32[]{:S(2)}) collective-permute-start(bf16[4,128,256]{2,1,0:T(8,128)(2,1)S(1)} %collective-permute-done.refs_1_), channel_id=1, source_target_pairs={{0,1},{1,0},{2,3},{3,2},{4,5},{5,4},{6,7},{7,6},{8,9},{9,8},{10,11... | collective-permute-start | bytes 786440 | tf_op jit(solution)/shard_map/ppermute | solution.py:156
  132.1 1.9 collective-permute-start.5
  134.1 2.4 %collective-permute-start.6 = (bf16[4,128,256]{2,1,0:T(8,128)(2,1)S(1)}, bf16[4,128,256]{2,1,0:T(8,128)(2,1)S(1)}, u32[]{:S(2)}, u32[]{:S(2)}) collective-permute-start(bf16[4,128,256]{2,1,0:T(8,128)(2,1)S(1)} %collective-permute-done.2.refs_3_), channel_id=1, source_target_pairs={{0,1},{1,0},{2,3},{3,2},{4,5},{5,4},{6,7},{7,6},{8,9},{9,8},{10,11... | collective-permute-start | bytes 786440 | tf_op jit(solution)/shard_map/ppermute | solution.py:156
  136.5 6.1 %all-to-all-done.5 = f32[16,16,256]{2,1,0:T(8,128)S(1)} async-done(((f32[16,16,256]{2,1,0:T(8,128)}), f32[16,16,256]{2,1,0:T(8,128)S(1)}, u32[]{:S(2)}, u32[]{:S(2)}) %all-to-all-start.5) | async-done | bytes 262176 | tf_op jit(solution)/shard_map/all_to_all | solution.py:160
  142.6 0.7 broadcast_in_dim.21
  143.4 4.4 %all-to-all-start.8 = ((f32[32,8,256]{2,1,0:T(8,128)}), f32[32,8,256]{2,1,0:T(8,128)S(1)}, u32[]{:S(2)}, u32[]{:S(2)}) async-start(f32[32,8,256]{2,1,0:T(8,128)} %broadcast_in_dim.21), calls=%async_computation.8 | async-start | bytes 524288 | tf_op jit(solution)/shard_map/all_to_all | solution.py:160
  147.8 4.9 %backward_tiles.1 = bf16[16,128,256]{2,1,0:T(8,128)(2,1)} custom-call(s32[128]{0:T(128)S(1)} %bitcast.23, s32[128]{0:T(128)S(1)} %bitcast.25, s32[1]{0:T(128)} %bitcast.20.live_ref, s32[2]{0:T(128)S(1)} %pad_add_fusion.place, bf16[128,128,128]{2,1,0:T(8,128)(2,1)} %bitcast.27, bf16[4,128,256]{2,1,0:T(8,128)(2,1)S(1)} %all-to-all-done.6.refs_0_, ...), custom_call_target="tpu_custom_call" | custom-call | flops 1073741824 | bytes 4194304 | tf_op jit(solution)/shard_map/backward_tiles/pallas_call | solution.py:133
  152.8 5.0 %all-to-all-done.8 = f32[32,8,256]{2,1,0:T(8,128)S(1)} async-done(((f32[32,8,256]{2,1,0:T(8,128)}), f32[32,8,256]{2,1,0:T(8,128)S(1)}, u32[]{:S(2)}, u32[]{:S(2)}) %all-to-all-start.8) | async-done | bytes 262176 | tf_op jit(solution)/shard_map/all_to_all | solution.py:160
  157.8 8.0 %all-to-all-start.7 = ((bf16[16,128,256]{2,1,0:T(8,128)(2,1)}), bf16[16,128,256]{2,1,0:T(8,128)(2,1)S(1)}, u32[]{:S(2)}, u32[]{:S(2)}) async-start(bf16[16,128,256]{2,1,0:T(8,128)(2,1)} %backward_tiles.1), calls=%async_computation.7 | async-start | bytes 2097152 | tf_op jit(solution)/shard_map/all_to_all | solution.py:160
  166.3 32.5 %all-to-all-done.7 = bf16[16,128,256]{2,1,0:T(8,128)(2,1)S(1)} async-done(((bf16[16,128,256]{2,1,0:T(8,128)(2,1)}), bf16[16,128,256]{2,1,0:T(8,128)(2,1)S(1)}, u32[]{:S(2)}, u32[]{:S(2)}) %all-to-all-start.7) | async-done | bytes 1048608 | tf_op jit(solution)/shard_map/all_to_all | solution.py:160
  199.0 0.8 convolution_convert_fusion.1
  (34 shorter events, 2.8 us)
Async XLA Ops:
  0.6 89.5 %copy-start = (bf16[256,256]{1,0:T(8,128)(2,1)S(1)}, bf16[256,256]{1,0:T(8,128)(2,1)}, u32[]{:S(2)}) copy-start(bf16[256,256]{1,0:T(8,128)(2,1)} %param.9) | copy-start | bytes 393220
  0.6 50.1 %copy-start.1 = (s32[1,1,128]{2,1,0:T(1,128)S(1)}, s32[1,1,128]{2,1,0:T(1,128)}, u32[]{:S(2)}) copy-start(s32[1,1,128]{2,1,0:T(1,128)} %param.12) | copy-start | bytes 1540
  0.7 50.1 %copy-start.2 = (s32[1,1,128]{2,1,0:T(1,128)S(1)}, s32[1,1,128]{2,1,0:T(1,128)}, u32[]{:S(2)}) copy-start(s32[1,1,128]{2,1,0:T(1,128)} %param.13) | copy-start | bytes 1540
  2.6 48.2 %all-to-all-start = ((bf16[16,128,256]{2,1,0:T(8,128)(2,1)}), bf16[16,128,256]{2,1,0:T(8,128)(2,1)S(1)}, u32[]{:S(2)}, u32[]{:S(2)}) async-start(bf16[16,128,256]{2,1,0:T(8,128)(2,1)} %broadcast_in_dim.16), calls=%async_computation | async-start | bytes 2097152 | tf_op jit(solution)/shard_map/all_to_all | solution.py:160
  60.6 29.5 %copy-start.3 = (bf16[128,256]{1,0:T(8,128)(2,1)S(1)}, bf16[128,256]{1,0:T(8,128)(2,1)}, u32[]{:S(2)}) copy-start(bf16[128,256]{1,0:T(8,128)(2,1)} %param.11) | copy-start | bytes 196612
  60.6 29.5 %copy-start.4 = (f32[256]{0:T(256)S(1)}, f32[256]{0:T(256)}, u32[]{:S(2)}) copy-start(f32[256]{0:T(256)} %param.10) | copy-start | bytes 3076
  80.4 9.6 %all-to-all-start.3 = ((bf16[4,128,256]{2,1,0:T(8,128)(2,1)}), bf16[4,128,256]{2,1,0:T(8,128)(2,1)S(1)}, u32[]{:S(2)}, u32[]{:S(2)}) async-start(bf16[4,128,256]{2,1,0:T(8,128)(2,1)} %reduce_sum.75), calls=%async_computation.3 | async-start | bytes 524288 | tf_op jit(solution)/shard_map/all_to_all | solution.py:160
  91.8 11.3 %all-to-all-start.6 = ((bf16[4,128,256]{2,1,0:T(8,128)(2,1)}), bf16[4,128,256]{2,1,0:T(8,128)(2,1)S(1)}, u32[]{:S(2)}, u32[]{:S(2)}) async-start(bf16[4,128,256]{2,1,0:T(8,128)(2,1)} %broadcast_in_dim.22), calls=%async_computation.6 | async-start | bytes 524288 | tf_op jit(solution)/shard_map/all_to_all | solution.py:160
  103.0 16.1 %all-to-all-start.4 = ((bf16[32,16,256]{2,1,0:T(8,128)(2,1)}), bf16[32,16,256]{2,1,0:T(8,128)(2,1)S(1)}, u32[]{:S(2)}, u32[]{:S(2)}) async-start(bf16[32,16,256]{2,1,0:T(8,128)(2,1)} %pad_maximum_fusion), calls=%async_computation.4 | async-start | bytes 524288 | tf_op jit(solution)/shard_map/all_to_all | solution.py:160
  107.8 21.9 %collective-permute-start = (bf16[4,128,256]{2,1,0:T(8,128)(2,1)S(1)}, bf16[4,128,256]{2,1,0:T(8,128)(2,1)S(1)}, u32[]{:S(2)}, u32[]{:S(2)}) collective-permute-start(bf16[4,128,256]{2,1,0:T(8,128)(2,1)S(1)} %all-to-all-done.6.refs_0_), channel_id=1, source_target_pairs={{0,2},{2,4},{4,6},{6,0},{1,3},{3,5},{5,7},{7,1},{8,10},{10,12},{12... | collective-permute-start | bytes 786440 | tf_op jit(solution)/shard_map/ppermute | solution.py:152
  111.2 20.9 %collective-permute-start.1 = (bf16[4,128,256]{2,1,0:T(8,128)(2,1)S(1)}, bf16[4,128,256]{2,1,0:T(8,128)(2,1)S(1)}, u32[]{:S(2)}, u32[]{:S(2)}) collective-permute-start(bf16[4,128,256]{2,1,0:T(8,128)(2,1)S(1)} %all-to-all-done.6.refs_0_), channel_id=1, source_target_pairs={{0,4},{2,6},{4,0},{6,2},{1,5},{3,7},{5,1},{7,3},{8,12},{10,14},{12... | collective-permute-start | bytes 786440 | tf_op jit(solution)/shard_map/ppermute | solution.py:152
  115.8 18.3 %collective-permute-start.2 = (bf16[4,128,256]{2,1,0:T(8,128)(2,1)S(1)}, bf16[4,128,256]{2,1,0:T(8,128)(2,1)S(1)}, u32[]{:S(2)}, u32[]{:S(2)}) collective-permute-start(bf16[4,128,256]{2,1,0:T(8,128)(2,1)S(1)} %all-to-all-done.6.refs_0_), channel_id=1, source_target_pairs={{0,6},{2,0},{4,2},{6,4},{1,7},{3,1},{5,3},{7,5},{8,14},{10,8},{12,... | collective-permute-start | bytes 786440 | tf_op jit(solution)/shard_map/ppermute | solution.py:152
  120.0 22.6 %all-to-all-start.5 = ((f32[16,16,256]{2,1,0:T(8,128)}), f32[16,16,256]{2,1,0:T(8,128)S(1)}, u32[]{:S(2)}, u32[]{:S(2)}) async-start(f32[16,16,256]{2,1,0:T(8,128)} %broadcast_in_dim.20), calls=%async_computation.5 | async-start | bytes 524288 | tf_op jit(solution)/shard_map/all_to_all | solution.py:160
  127.8 14.8 %collective-permute-start.3 = (bf16[4,128,256]{2,1,0:T(8,128)(2,1)S(1)}, bf16[4,128,256]{2,1,0:T(8,128)(2,1)S(1)}, u32[]{:S(2)}, u32[]{:S(2)}) collective-permute-start(bf16[4,128,256]{2,1,0:T(8,128)(2,1)S(1)} %all-to-all-done.6.refs_0_), channel_id=1, source_target_pairs={{0,1},{1,0},{2,3},{3,2},{4,5},{5,4},{6,7},{7,6},{8,9},{9,8},{10,11... | collective-permute-start | bytes 786440 | tf_op jit(solution)/shard_map/ppermute | solution.py:156
  129.7 12.9 %collective-permute-start.4 = (bf16[4,128,256]{2,1,0:T(8,128)(2,1)S(1)}, bf16[4,128,256]{2,1,0:T(8,128)(2,1)S(1)}, u32[]{:S(2)}, u32[]{:S(2)}) collective-permute-start(bf16[4,128,256]{2,1,0:T(8,128)(2,1)S(1)} %collective-permute-done.refs_1_), channel_id=1, source_target_pairs={{0,1},{1,0},{2,3},{3,2},{4,5},{5,4},{6,7},{7,6},{8,9},{9,8},{10,11... | collective-permute-start | bytes 786440 | tf_op jit(solution)/shard_map/ppermute | solution.py:156
  132.1 10.5 %collective-permute-start.5 = (bf16[4,128,256]{2,1,0:T(8,128)(2,1)S(1)}, bf16[4,128,256]{2,1,0:T(8,128)(2,1)S(1)}, u32[]{:S(2)}, u32[]{:S(2)}) collective-permute-start(bf16[4,128,256]{2,1,0:T(8,128)(2,1)S(1)} %collective-permute-done.1.refs_2_), channel_id=1, source_target_pairs={{0,1},{1,0},{2,3},{3,2},{4,5},{5,4},{6,7},{7,6},{8,9},{9,8},{10,11... | collective-permute-start | bytes 786440 | tf_op jit(solution)/shard_map/ppermute | solution.py:156
  134.1 8.6 %collective-permute-start.6 = (bf16[4,128,256]{2,1,0:T(8,128)(2,1)S(1)}, bf16[4,128,256]{2,1,0:T(8,128)(2,1)S(1)}, u32[]{:S(2)}, u32[]{:S(2)}) collective-permute-start(bf16[4,128,256]{2,1,0:T(8,128)(2,1)S(1)} %collective-permute-done.2.refs_3_), channel_id=1, source_target_pairs={{0,1},{1,0},{2,3},{3,2},{4,5},{5,4},{6,7},{7,6},{8,9},{9,8},{10,11... | collective-permute-start | bytes 786440 | tf_op jit(solution)/shard_map/ppermute | solution.py:156
  143.4 14.4 %all-to-all-start.8 = ((f32[32,8,256]{2,1,0:T(8,128)}), f32[32,8,256]{2,1,0:T(8,128)S(1)}, u32[]{:S(2)}, u32[]{:S(2)}) async-start(f32[32,8,256]{2,1,0:T(8,128)} %broadcast_in_dim.21), calls=%async_computation.8 | async-start | bytes 524288 | tf_op jit(solution)/shard_map/all_to_all | solution.py:160
  157.8 41.1 %all-to-all-start.7 = ((bf16[16,128,256]{2,1,0:T(8,128)(2,1)}), bf16[16,128,256]{2,1,0:T(8,128)(2,1)S(1)}, u32[]{:S(2)}, u32[]{:S(2)}) async-start(bf16[16,128,256]{2,1,0:T(8,128)(2,1)} %backward_tiles.1), calls=%async_computation.7 | async-start | bytes 2097152 | tf_op jit(solution)/shard_map/all_to_all | solution.py:160

commit v4 on v1

v4 whole, which is shorter than its diff:
```python
import jax
import jax.numpy as jnp
from jax import lax
from jax.experimental import pallas as pl
from jax.experimental.pallas import tpu as pltpu
from jax.sharding import Mesh
from jax.sharding import PartitionSpec as P

ROW = ("yh", "z")
COL = ("yl", "x", "core")
ALL = ROW + COL
CHUNK = 16
GROUP = 16


def elu_value(pre):
    return jnp.where(pre > 0, pre, jnp.expm1(jnp.minimum(pre, 0.0)))


def elu_slope(pre):
    return jnp.where(pre > 0, jnp.float32(1.0), jnp.exp(jnp.minimum(pre, 0.0)))


def start_values(values_hbm, values, sems):
    copies = [
        pltpu.make_async_copy(
            values_hbm.at[pl.ds(c * CHUNK, CHUNK)], values.at[pl.ds(c * CHUNK, CHUNK)], sems.at[c]
        )
        for c in range(values.shape[0] // CHUNK)
    ]
    for copy in copies:
        copy.start()
    return copies


def walk(copies, live, step):
    for c, copy in enumerate(copies):
        copy.wait()
        left = jnp.clip(live - c * CHUNK, 0, CHUNK)

        def one(g, carry, c=c):
            step(c * CHUNK + g * GROUP)
            return carry

        lax.fori_loop(0, (left + GROUP - 1) // GROUP, one, 0)


def forward_kernel(rows, cols, live_ref, core_ref, values_hbm, src, kept, sent, values, acc, sems):
    live, core = live_ref[0], core_ref[0]
    copies = start_values(values_hbm, values, sems)
    half = kept.shape[0]
    acc[...] = jnp.zeros_like(acc)

    def slot(t):
        return (lax.rem(t, 2) ^ core) * half + ((t // 2) & 3) * 4 + t // 8

    def step(first):
        for u in range(GROUP):
            s = first + u
            dest = jnp.where(s < live, slot(rows[s]), 2 * half)
            acc[dest] += jnp.dot(values[s], src[cols[s]], preferred_element_type=jnp.float32)

    walk(copies, live, step)
    sent[...] = acc[half : 2 * half].astype(sent.dtype)
    kept[...] = acc[:half].astype(kept.dtype)


def backward_kernel(rows, cols, live_ref, core_ref, values_hbm, own, other, out, values, src, acc, sems, src_sems):
    live, core = live_ref[0], core_ref[0]
    fetch = [
        pltpu.make_async_copy(own, src.at[pl.ds(core * 4, 4)], src_sems.at[0]),
        pltpu.make_async_copy(other, src.at[pl.ds((1 - core) * 4, 4)], src_sems.at[1]),
    ]
    for copy in fetch:
        copy.start()
    copies = start_values(values_hbm, values, sems)
    tiles, side = out.shape[0], values.shape[1]
    gathered = 4 * side
    acc[...] = jnp.zeros_like(acc)
    for copy in fetch:
        copy.wait()

    def step(first):
        for u in range(GROUP):
            s = first + u
            dest = jnp.where(s < live, cols[s], tiles)
            t = rows[s]
            block = src[lax.rem(t, 2) * 4 + ((t // 2) & 3), pl.ds(pl.multiple_of(t // 8 * side, side), side), :]
            acc[dest] += lax.dot_general(
                values[s], block, (((0,), (0,)), ((), ())), preferred_element_type=jnp.float32
            )

    walk(copies, live, step)

    terms = jnp.zeros((16, out.shape[-1]), jnp.float32)
    bias = jnp.zeros((8, out.shape[-1]), jnp.float32)
    for k in range(8):
        terms += src[k, gathered:, :].astype(jnp.float32)
        for part in range(0, gathered, side):
            block = src[k, part : part + side, :].astype(jnp.float32)
            bias += jnp.sum(block.reshape(side // 8, 8, -1), axis=0)
    bias = jnp.sum(bias, axis=0, keepdims=True)
    high = bias.astype(jnp.bfloat16).astype(jnp.float32)
    row = lax.broadcasted_iota(jnp.int32, (8, out.shape[-1]), 0)
    tail = jnp.where(row == 0, high, jnp.where(row == 1, bias - high, 0.0))
    mine = jnp.where(core == 0, terms[:8], terms[8:])
    tail = jnp.concatenate([mine, tail]).astype(out.dtype)
    for t in range(tiles):
        out[t, :side, :] = acc[t].astype(out.dtype)
        out[t, side:, :] = tail


SMEM = pl.BlockSpec(memory_space=pltpu.SMEM)
VMEM = pl.BlockSpec(memory_space=pltpu.VMEM)
ANY = pl.BlockSpec(memory_space=pl.ANY)
HBM = pl.BlockSpec(memory_space=pltpu.HBM)


def cost(slots, side, width):
    return pl.CostEstimate(
        flops=2 * slots * side * side * width, bytes_accessed=2 * slots * side * side, transcendentals=0
    )


def spread_forward(rows, cols, live, core, values, src, row_tiles):
    slots, side, _ = values.shape
    width = src.shape[-1]
    half = jax.ShapeDtypeStruct((row_tiles // 2, side, width), jnp.bfloat16)
    return pl.pallas_call(
        forward_kernel,
        out_shape=(half, half),
        in_specs=[SMEM, SMEM, SMEM, SMEM, HBM, VMEM],
        out_specs=(VMEM, VMEM),
        scratch_shapes=[
            pltpu.VMEM((slots, side, side), jnp.bfloat16),
            pltpu.VMEM((row_tiles + 1, side, width), jnp.float32),
            pltpu.SemaphoreType.DMA((slots // CHUNK,)),
        ],
        compiler_params=pltpu.CompilerParams(vmem_limit_bytes=40 << 20),
        cost_estimate=cost(slots, side, width),
        name="forward_tiles",
    )(rows, cols, live, core, values, src)


def spread_backward(rows, cols, live, core, values, own, other, col_tiles):
    slots, side, _ = values.shape
    width = own.shape[-1]
    return pl.pallas_call(
        backward_kernel,
        out_shape=jax.ShapeDtypeStruct((col_tiles, side + 16, width), jnp.bfloat16),
        in_specs=[SMEM, SMEM, SMEM, SMEM, HBM, ANY, ANY],
        out_specs=VMEM,
        scratch_shapes=[
            pltpu.VMEM((slots, side, side), jnp.bfloat16),
            pltpu.VMEM((2 * own.shape[0],) + own.shape[1:], jnp.bfloat16),
            pltpu.VMEM((col_tiles + 1, side, width), jnp.float32),
            pltpu.SemaphoreType.DMA((slots // CHUNK,)),
            pltpu.SemaphoreType.DMA((2,)),
        ],
        compiler_params=pltpu.CompilerParams(vmem_limit_bytes=40 << 20),
        cost_estimate=cost(slots, side, width),
        name="backward_tiles",
    )(rows, cols, live, core, values, own, other)


def swap(x):
    return lax.ppermute(x, "core", [(0, 1), (1, 0)])


def exchange(x, axes):
    return lax.all_to_all(x, axes, 0, 0, tiled=True)


def gather(x, axes, size):
    copies = lax.optimization_barrier(jnp.broadcast_to(x[None], (size,) + x.shape))
    return exchange(copies, axes)


def gather_and_scatter(x, pieces, axes):
    copies = jnp.broadcast_to(x[None], pieces.shape[:1] + x.shape)
    return exchange(lax.optimization_barrier(jnp.concatenate([copies, pieces], axis=1)), axes)


def add_up(x):
    return jnp.sum(x.astype(jnp.float32), axis=0)


def body(features, weight, bias, grad_out, tile_rows, tile_cols, tile_counts, tile_values):
    values = pltpu.with_memory_space_constraint(tile_values[0, 0], pltpu.HBM)
    rows, cols, live = tile_rows[0, 0], tile_cols[0, 0], tile_counts[0]
    side, width = features.shape
    row_tiles, col_tiles = 32, 16
    bf16 = jnp.bfloat16
    core = lax.axis_index("core").astype(jnp.int32).reshape(1)

    block = gather(features, ROW, col_tiles)
    kept, sent = spread_forward(rows, cols, live, core, values, block, row_tiles)
    by_core = (kept.astype(jnp.float32) + swap(sent).astype(jnp.float32)).astype(bf16)
    by_x = add_up(exchange(by_core.reshape(4, 4, side, width), "x")).astype(bf16)
    mean = add_up(exchange(by_x, "yl"))
    pre = (
        jnp.dot(mean, weight.astype(jnp.float32), precision=lax.Precision.HIGHEST, preferred_element_type=jnp.float32)
        + bias[None, :]
    )
    grad_pre = (grad_out.astype(jnp.float32) * elu_slope(pre)).astype(bf16)
    output = elu_value(pre).astype(bf16)

    grad32 = grad_pre.astype(jnp.float32)
    weight_term = lax.dot_general(
        mean, grad32, (((0,), (0,)), ((), ())), precision=lax.Precision.HIGHEST, preferred_element_type=jnp.float32
    )
    terms = weight_term.astype(bf16).reshape(4, width // 4, width)
    along_y = gather_and_scatter(grad_pre, terms, "yl")
    terms = add_up(along_y[:, side:]).astype(bf16).reshape(4, width // 16, width)
    own = gather_and_scatter(along_y[:, :side].reshape(4 * side, width), terms, "x")
    back = spread_backward(rows, cols, live, core, values, own, swap(own), col_tiles)

    reduced = add_up(exchange(back, ROW))
    grad_mixed = reduced[:side].astype(bf16)
    grad_weight = gather(reduced[side : side + 8], COL, 32).reshape(width, width)
    grad_bias = reduced[side + 8] + reduced[side + 9]
    grad_features = lax.dot_general(
        grad_mixed, weight, (((1,), (1,)), ((), ())), preferred_element_type=jnp.float32
    ).astype(bf16)
    return (output, grad_features, grad_weight, grad_bias)


def solution(mesh):
    fine = Mesh(mesh.devices.reshape(2, 8, 4, 4, 2), ALL)
    placed = (
        P(COL + ROW, None),
        P(),
        P(),
        P(ALL, None),
        P(ROW, COL, None),
        P(ROW, COL, None),
        P(ROW, COL),
        P(ROW, COL, None, None, None),
    )
    return jax.shard_map(
        body,
        mesh=fine,
        in_specs=placed,
        out_specs=(P(ALL, None), P(COL + ROW, None), P(), P()),
        check_vma=False,
    )
```

time: 233 us -> 192 us (0.82)
  the two profiles are of different devices: /device:TPU:14 before, /device:TPU:1 now
where the time goes in v4:
time: 192 us; the launch traced here: 191 us
  blocking collectives  99.4 us (52%)
  starting transfers between devices  40.2 us (21%)
  waiting for transfers between devices  37 us (19%)
  Pallas kernels  6.34 us (3%)
  local copies, waits for them, and re-layouts  3.51 us (2%)
  matrix products  2.06 us (1%)
    all_to_all x5, blocking collectives, exchange(): return lax.all_to_all(x, axes, 0, 0, tiled=True)  99.4 us
    all_to_all x2, waiting for transfers between devices, exchange(): return lax.all_to_all(x, axes, 0, 0, tiled=True)  32.5 us
    all_to_all x2, starting transfers between devices, exchange(): return lax.all_to_all(x, axes, 0, 0, tiled=True)  28 us
    ppermute x2, starting transfers between devices, swap(): return lax.ppermute(x, 'core', [(0, 1), (1, 0)])  12.2 us
    ppermute x2, waiting for transfers between devices, swap(): return lax.ppermute(x, 'core', [(0, 1), (1, 0)])  4.58 us
  transfers between devices with their start and end apart: 4, of which 4 were waited for; matrix products, arithmetic and copies ran while one was open for 1% of the time, Pallas kernels for 0%

profile of v4, /device:TPU:1, one launch (start us, length us, event | category | flops | bytes accessed | tf_op | source)
XLA Modules:
  0.0 191.5 jit_solution(12176157548683464903)
XLA Ops:
  0.6 0.0 copy-start
  0.6 2.0 %broadcast_in_dim.14 = bf16[16,128,256]{2,1,0:T(8,128)(2,1)} broadcast(bf16[128,256]{1,0:T(8,128)(2,1)} %param.8), dimensions={1,2} | broadcast | bytes 1114112 | tf_op jit(solution)/shard_map/broadcast_in_dim | solution.py:175
  2.6 16.4 %all-to-all-start = ((bf16[16,128,256]{2,1,0:T(8,128)(2,1)}), bf16[16,128,256]{2,1,0:T(8,128)(2,1)S(1)}, u32[]{:S(2)}, u32[]{:S(2)}) async-start(bf16[16,128,256]{2,1,0:T(8,128)(2,1)} %broadcast_in_dim.14), calls=%async_computation | async-start | bytes 2097152 | tf_op jit(solution)/shard_map/all_to_all | solution.py:171
  19.6 22.7 %all-to-all-done.src = bf16[16,128,256]{2,1,0:T(8,128)(2,1)S(1)} async-done(((bf16[16,128,256]{2,1,0:T(8,128)(2,1)}), bf16[16,128,256]{2,1,0:T(8,128)(2,1)S(1)}, u32[]{:S(2)}, u32[]{:S(2)}) %all-to-all-start) | async-done | bytes 1048608 | tf_op jit(solution)/shard_map/all_to_all | solution.py:171
  42.4 0.0 copy-done.1
  42.4 0.0 copy-done.2
  42.4 3.0 %forward_tiles.1 = (bf16[16,128,256]{2,1,0:T(8,128)(2,1)S(1)}, bf16[16,128,256]{2,1,0:T(8,128)(2,1)S(1)}) custom-call(s32[128]{0:T(128)S(1)} %bitcast.18, s32[128]{0:T(128)S(1)} %bitcast.20, s32[1]{0:T(128)} %bitcast.16.live_ref, s32[1]{0:T(128)} %bitcast.3.core_ref, bf16[128,128,128]{2,1,0:T(8,128)(2,1)} %bitcast.22, bf16[16,128,256]{2,1,0:T(8,128)(2,1)S(1)} %all-to-all-done.src), custom_call_target="tpu_custom_call" | custom-call | flops 1073741824 | bytes 4194304 | tf_op jit(solution)/shard_map/forward_tiles/pallas_call | solution.py:129
  45.3 6.7 %collective-permute-start = (bf16[16,128,256]{2,1,0:T(8,128)(2,1)S(1)}, bf16[16,128,256]{2,1,0:T(8,128)(2,1)S(1)}, u32[]{:S(2)}, u32[]{:S(2)}) collective-permute-start(bf16[16,128,256]{2,1,0:T(8,128)(2,1)S(1)} %get-tuple-element.7), channel_id=1, source_target_pairs={{0,1},{1,0},{2,3},{3,2},{4,5},{5,4},{6,7},{7,6},{8,9},{9,8},{10,11... | collective-permute-start | bytes 3145736 | tf_op jit(solution)/shard_map/ppermute | solution.py:167
  52.1 2.3 %collective-permute-done = bf16[16,128,256]{2,1,0:T(8,128)(2,1)S(1)} collective-permute-done((bf16[16,128,256]{2,1,0:T(8,128)(2,1)S(1)}, bf16[16,128,256]{2,1,0:T(8,128)(2,1)S(1)}, u32[]{:S(2)}, u32[]{:S(2)}) %collective-permute-start) | collective-permute-done | bytes 1048608 | tf_op jit(solution)/shard_map/ppermute | solution.py:167
  54.4 0.4 add_convert_fusion
  54.7 17.6 %all_to_all.35 = bf16[4,4,128,256]{3,2,1,0:T(8,128)(2,1)S(1)} all-to-all(bf16[4,4,128,256]{3,2,1,0:T(8,128)(2,1)S(1)} %bitcast.24), channel_id=1, replica_groups=mesh['yh'=2,'z'=8,'yl'=4,'x'=4,'core'=2] {'x'}, dimensions={0} | all-to-all | bytes 2097152 | tf_op jit(solution)/shard_map/all_to_all | solution.py:171
  72.3 0.2 reduce_sum.42
  72.6 15.0 %all_to_all.36 = bf16[4,128,256]{2,1,0:T(8,128)(2,1)S(1)} all-to-all(bf16[4,128,256]{2,1,0:T(8,128)(2,1)S(1)} %reduce_sum.42), channel_id=1, replica_groups=mesh['yh'=2,'z'=8,'yl'=4,'x'=4,'core'=2] {'yl'}, dimensions={0} | all-to-all | bytes 524288 | tf_op jit(solution)/shard_map/all_to_all | solution.py:171
  87.6 0.0 copy-done
  87.6 0.0 copy-done.3
  87.7 0.9 fusion.2
  88.6 0.3 convolution_convert_fusion
  89.0 14.5 %all_to_all.37 = bf16[4,192,256]{2,1,0:T(8,128)(2,1)S(1)} all-to-all(bf16[4,192,256]{2,1,0:T(8,128)(2,1)S(1)} %pad_maximum_fusion.1), channel_id=1, replica_groups=mesh['yh'=2,'z'=8,'yl'=4,'x'=4,'core'=2] {'yl'}, dimensions={0} | all-to-all | bytes 786432 | tf_op jit(solution)/shard_map/all_to_all | solution.py:171
  103.6 0.1 broadcast_in_dim.34
  103.6 0.1 pad_maximum_fusion
  103.7 15.3 %all_to_all.38.own = bf16[4,528,256]{2,1,0:T(8,128)(2,1)S(1)} all-to-all(bf16[4,528,256]{2,1,0:T(8,128)(2,1)S(1)} %pad_maximum_fusion), channel_id=1, replica_groups=mesh['yh'=2,'z'=8,'yl'=4,'x'=4,'core'=2] {'x'}, dimensions={0} | all-to-all | bytes 2162688 | tf_op jit(solution)/shard_map/all_to_all | solution.py:171
  119.0 5.4 %collective-permute-start.1 = (bf16[4,528,256]{2,1,0:T(8,128)(2,1)S(1)}, bf16[4,528,256]{2,1,0:T(8,128)(2,1)S(1)}, u32[]{:S(2)}, u32[]{:S(2)}) collective-permute-start(bf16[4,528,256]{2,1,0:T(8,128)(2,1)S(1)} %all_to_all.38.own), channel_id=1, source_target_pairs={{0,1},{1,0},{2,3},{3,2},{4,5},{5,4},{6,7},{7,6},{8,9},{9,8},{10,11... | collective-permute-start | bytes 3244040 | tf_op jit(solution)/shard_map/ppermute | solution.py:167
  124.4 2.3 %collective-permute-done.1.other = bf16[4,528,256]{2,1,0:T(8,128)(2,1)S(1)} collective-permute-done((bf16[4,528,256]{2,1,0:T(8,128)(2,1)S(1)}, bf16[4,528,256]{2,1,0:T(8,128)(2,1)S(1)}, u32[]{:S(2)}, u32[]{:S(2)}) %collective-permute-start.1) | collective-permute-done | bytes 1081376 | tf_op jit(solution)/shard_map/ppermute | solution.py:167
  126.7 3.4 %backward_tiles.1 = bf16[16,144,256]{2,1,0:T(8,128)(2,1)S(1)} custom-call(s32[128]{0:T(128)S(1)} %bitcast.19, s32[128]{0:T(128)S(1)} %bitcast.21, s32[1]{0:T(128)} %bitcast.17.live_ref, s32[1]{0:T(128)} %bitcast.3.core_ref, bf16[128,128,128]{2,1,0:T(8,128)(2,1)} %bitcast.23, bf16[4,528,256]{2,1,0:T(8,128)(2,1)S(1)} %all_to_all.38.own, ...), custom_call_target="tpu_custom_call" | custom-call | flops 1073741824 | bytes 4194304 | tf_op jit(solution)/shard_map/backward_tiles/pallas_call | solution.py:148
  130.1 37.0 %all_to_all.39 = bf16[16,144,256]{2,1,0:T(8,128)(2,1)S(1)} all-to-all(bf16[16,144,256]{2,1,0:T(8,128)(2,1)S(1)} %backward_tiles.1), channel_id=1, replica_groups=mesh['yh'=2,'z'=8,'yl'=4,'x'=4,'core'=2] {'yh','z'}, dimensions={0} | all-to-all | bytes 2359296 | tf_op jit(solution)/shard_map/all_to_all | solution.py:171
  167.1 0.2 convert_reduce_fusion
  167.2 0.7 broadcast_in_dim.35
  168.0 11.7 %all-to-all-start.6 = ((f32[32,8,256]{2,1,0:T(8,128)}), f32[32,8,256]{2,1,0:T(8,128)S(1)}, u32[]{:S(2)}, u32[]{:S(2)}) async-start(f32[32,8,256]{2,1,0:T(8,128)} %broadcast_in_dim.35), calls=%async_computation.6 | async-start | bytes 524288 | tf_op jit(solution)/shard_map/all_to_all | solution.py:171
  179.6 0.6 slice_add_fusion
  180.2 0.8 convolution_convert_fusion.1
  181.0 9.7 %all-to-all-done.6 = f32[32,8,256]{2,1,0:T(8,128)S(1)} async-done(((f32[32,8,256]{2,1,0:T(8,128)}), f32[32,8,256]{2,1,0:T(8,128)S(1)}, u32[]{:S(2)}, u32[]{:S(2)}) %all-to-all-start.6) | async-done | bytes 262176 | tf_op jit(solution)/shard_map/all_to_all | solution.py:171
  190.7 0.7 copy.14
  (11 shorter events, 0.1 us)
Async XLA Ops:
  0.6 87.0 %copy-start = (bf16[256,256]{1,0:T(8,128)(2,1)S(1)}, bf16[256,256]{1,0:T(8,128)(2,1)}, u32[]{:S(2)}) copy-start(bf16[256,256]{1,0:T(8,128)(2,1)} %param.9) | copy-start | bytes 393220
  2.6 39.8 %copy-start.1 = (s32[1,1,128]{2,1,0:T(1,128)S(1)}, s32[1,1,128]{2,1,0:T(1,128)}, u32[]{:S(2)}) copy-start(s32[1,1,128]{2,1,0:T(1,128)} %param.12) | copy-start | bytes 1540
  2.6 39.8 %copy-start.2 = (s32[1,1,128]{2,1,0:T(1,128)S(1)}, s32[1,1,128]{2,1,0:T(1,128)}, u32[]{:S(2)}) copy-start(s32[1,1,128]{2,1,0:T(1,128)} %param.13) | copy-start | bytes 1540
  2.6 39.8 %all-to-all-start = ((bf16[16,128,256]{2,1,0:T(8,128)(2,1)}), bf16[16,128,256]{2,1,0:T(8,128)(2,1)S(1)}, u32[]{:S(2)}, u32[]{:S(2)}) async-start(bf16[16,128,256]{2,1,0:T(8,128)(2,1)} %broadcast_in_dim.14), calls=%async_computation | async-start | bytes 2097152 | tf_op jit(solution)/shard_map/all_to_all | solution.py:171
  45.3 9.0 %collective-permute-start = (bf16[16,128,256]{2,1,0:T(8,128)(2,1)S(1)}, bf16[16,128,256]{2,1,0:T(8,128)(2,1)S(1)}, u32[]{:S(2)}, u32[]{:S(2)}) collective-permute-start(bf16[16,128,256]{2,1,0:T(8,128)(2,1)S(1)} %get-tuple-element.7), channel_id=1, source_target_pairs={{0,1},{1,0},{2,3},{3,2},{4,5},{5,4},{6,7},{7,6},{8,9},{9,8},{10,11... | collective-permute-start | bytes 3145736 | tf_op jit(solution)/shard_map/ppermute | solution.py:167
  72.3 15.3 %copy-start.3 = (bf16[128,256]{1,0:T(8,128)(2,1)S(1)}, bf16[128,256]{1,0:T(8,128)(2,1)}, u32[]{:S(2)}) copy-start(bf16[128,256]{1,0:T(8,128)(2,1)} %param.11) | copy-start | bytes 196612
  72.3 15.3 %copy-start.4 = (f32[256]{0:T(256)S(1)}, f32[256]{0:T(256)}, u32[]{:S(2)}) copy-start(f32[256]{0:T(256)} %param.10) | copy-start | bytes 3076
  119.0 7.7 %collective-permute-start.1 = (bf16[4,528,256]{2,1,0:T(8,128)(2,1)S(1)}, bf16[4,528,256]{2,1,0:T(8,128)(2,1)S(1)}, u32[]{:S(2)}, u32[]{:S(2)}) collective-permute-start(bf16[4,528,256]{2,1,0:T(8,128)(2,1)S(1)} %all_to_all.38.own), channel_id=1, source_target_pairs={{0,1},{1,0},{2,3},{3,2},{4,5},{5,4},{6,7},{7,6},{8,9},{9,8},{10,11... | collective-permute-start | bytes 3244040 | tf_op jit(solution)/shard_map/ppermute | solution.py:167
  168.0 22.8 %all-to-all-start.6 = ((f32[32,8,256]{2,1,0:T(8,128)}), f32[32,8,256]{2,1,0:T(8,128)S(1)}, u32[]{:S(2)}, u32[]{:S(2)}) async-start(f32[32,8,256]{2,1,0:T(8,128)} %broadcast_in_dim.35), calls=%async_computation.6 | async-start | bytes 524288 | tf_op jit(solution)/shard_map/all_to_all | solution.py:171

commit v5 on v3

--- a/solution.py
+++ b/solution.py
@@ -19,10 +19,6 @@
 
 def elu_slope(pre):
     return jnp.where(pre > 0, jnp.float32(1.0), jnp.exp(jnp.minimum(pre, 0.0)))
-
-
-def col_slot(t):
-    return lax.rem(t, 2) * 16 + lax.rem(t // 2, 4) * 4 + t // 8
 
 
 def start_values(values_hbm, values, sems):
@@ -49,20 +45,24 @@
         lax.fori_loop(0, (left + GROUP - 1) // GROUP, one, 0)
 
 
-def forward_kernel(rows, cols, live_ref, values_hbm, src, out, values, acc, sems):
-    live = live_ref[0]
+def forward_kernel(rows, cols, live_ref, core_ref, values_hbm, src, kept, sent, values, acc, sems):
+    live, core = live_ref[0], core_ref[0]
     copies = start_values(values_hbm, values, sems)
-    tiles = out.shape[0]
+    half = kept.shape[0]
     acc[...] = jnp.zeros_like(acc)
+
+    def slot(t):
+        return (lax.rem(t, 2) ^ core) * half + ((t // 2) & 3) * 4 + t // 8
 
     def step(first):
         for u in range(GROUP):
             s = first + u
-            dest = jnp.where(s < live, col_slot(rows[s]), tiles)
+            dest = jnp.where(s < live, slot(rows[s]), 2 * half)
             acc[dest] += jnp.dot(values[s], src[cols[s]], preferred_element_type=jnp.float32)
 
     walk(copies, live, step)
-    out[...] = acc[:tiles].astype(out.dtype)
+    sent[...] = acc[half : 2 * half].astype(sent.dtype)
+    kept[...] = acc[:half].astype(kept.dtype)
 
 
 def backward_kernel(rows, cols, live_ref, place, values_hbm, *refs):
@@ -96,6 +96,12 @@
     out[...] = acc[:tiles].astype(out.dtype)
 
 
+def place_kernel(place, a, b, c, d, out):
+    per = a.shape[0]
+    for k, piece in enumerate((a, b, c, d)):
+        out[pl.ds(((place[2] - k) & 3) * per, per), :] = piece[...]
+
+
 SMEM = pl.BlockSpec(memory_space=pltpu.SMEM)
 VMEM = pl.BlockSpec(memory_space=pltpu.VMEM)
 ANY = pl.BlockSpec(memory_space=pl.ANY)
@@ -108,14 +114,15 @@
     )
 
 
-def spread_forward(rows, cols, live, values, src, row_tiles):
+def spread_forward(rows, cols, live, place, values, src, row_tiles):
     slots, side, _ = values.shape
     width = src.shape[-1]
+    half = jax.ShapeDtypeStruct((row_tiles // 2, side, width), jnp.bfloat16)
     return pl.pallas_call(
         forward_kernel,
-        out_shape=jax.ShapeDtypeStruct((row_tiles, side, width), jnp.bfloat16),
-        in_specs=[SMEM, SMEM, SMEM, HBM, VMEM],
-        out_specs=VMEM,
+        out_shape=(half, half),
+        in_specs=[SMEM, SMEM, SMEM, SMEM, HBM, VMEM],
+        out_specs=(VMEM, VMEM),
         scratch_shapes=[
             pltpu.VMEM((slots, side, side), jnp.bfloat16),
             pltpu.VMEM((row_tiles + 1, side, width), jnp.float32),
@@ -124,7 +131,7 @@
         compiler_params=pltpu.CompilerParams(vmem_limit_bytes=40 << 20),
         cost_estimate=cost(slots, side, width),
         name="forward_tiles",
-    )(rows, cols, live, values, src)
+    )(rows, cols, live, place, values, src)
 
 
 def spread_backward(rows, cols, live, place, values, blocks, col_tiles):
@@ -148,6 +155,17 @@
     )(rows, cols, live, place, values, *blocks)
 
 
+def put_in_place(place, pieces):
+    per, width = pieces[0].shape
+    return pl.pallas_call(
+        place_kernel,
+        out_shape=jax.ShapeDtypeStruct((len(pieces) * per, width), pieces[0].dtype),
+        in_specs=[SMEM] + [VMEM] * len(pieces),
+        out_specs=VMEM,
+        name="place_pieces",
+    )(place, *pieces)
+
+
 def around(x, axis, size):
     return [x] + [lax.ppermute(x, axis, [(i, (i + k) % size) for i in range(size)]) for k in range(1, size)]
 
@@ -165,18 +183,19 @@
     return exchange(copies, axes)
 
 
+def gather_and_scatter(x, pieces, axes):
+    copies = jnp.broadcast_to(x[None], pieces.shape[:1] + x.shape)
+    return exchange(lax.optimization_barrier(jnp.concatenate([copies, pieces], axis=1)), axes)
+
+
 def add_up(x):
     return jnp.sum(x.astype(jnp.float32), axis=0)
 
 
-def weight_pieces(weight_term, bias_term, pieces):
-    width = bias_term.shape[-1]
-    per = weight_term.shape[0] // pieces
-    high = bias_term.astype(jnp.bfloat16)
-    low = (bias_term - high.astype(jnp.float32)).astype(jnp.bfloat16)
-    tail = jnp.concatenate([high[None], low[None], jnp.zeros((per - 2, width), jnp.bfloat16)])
-    tail = jnp.broadcast_to(tail[None], (pieces, per, width))
-    return jnp.concatenate([weight_term.astype(jnp.bfloat16).reshape(pieces, per, width), tail], axis=1)
+def two_rows(x):
+    high = x.astype(jnp.bfloat16).astype(jnp.float32)
+    row = lax.broadcasted_iota(jnp.int32, (8, x.shape[-1]), 0)
+    return jnp.where(row == 0, high, jnp.where(row == 1, x - high, 0.0)).astype(jnp.bfloat16)
 
 
 def body(features, weight, bias, grad_out, tile_rows, tile_cols, tile_counts, tile_values):
@@ -185,11 +204,11 @@
     side, width = features.shape
     row_tiles, col_tiles = 32, 16
     bf16 = jnp.bfloat16
-    place = jnp.stack([lax.axis_index(axis) for axis in ("core", "x")]).astype(jnp.int32)
+    place = jnp.stack([lax.axis_index(axis) for axis in ("core", "x", "yl")]).astype(jnp.int32)
 
     block = gather(features, ROW, col_tiles)
-    partial = spread_forward(rows, cols, live, values, block, row_tiles)
-    by_core = add_up(exchange(partial.reshape(2, 16, side, width), "core")).astype(bf16)
+    kept, sent = spread_forward(rows, cols, live, place, values, block, row_tiles)
+    by_core = (kept.astype(jnp.float32) + swap(sent).astype(jnp.float32)).astype(bf16)
     by_x = add_up(exchange(by_core.reshape(4, 4, side, width), "x")).astype(bf16)
     mean = add_up(exchange(by_x, "yl"))
     pre = (
@@ -203,19 +222,30 @@
     weight_term = lax.dot_general(
         mean, grad32, (((0,), (0,)), ((), ())), precision=lax.Precision.HIGHEST, preferred_element_type=jnp.float32
     )
-    terms = weight_pieces(weight_term, jnp.sum(grad32, axis=0), 32)
-
-    along_y = gather(grad_pre, "yl", 4)
-    own = around(along_y, "x", 4)
-    other = [swap(block) for block in own]
-    of_col = add_up(exchange(terms, COL))
-    of_all = add_up(gather(of_col, ROW, 16))
-    copies = jnp.broadcast_to(of_all[None, :8], (32, 8, width))
-    copies, blocks = lax.optimization_barrier((copies, own + other))
-    grad_weight = exchange(copies, COL).reshape(width, width)
-    grad_bias = of_all[8] + of_all[9]
+    bias_term = jnp.sum(grad32, axis=0, keepdims=True)
+    terms = weight_term.astype(bf16).reshape(4, width // 4, width)
+    tail = jnp.broadcast_to(two_rows(bias_term)[None], (4, 8, width))
+    along_y = gather_and_scatter(grad_pre, jnp.concatenate([terms, tail], axis=1), "yl")
+
+    own = around(along_y[:, :side], "x", 4)
+    blocks = own + [swap(block) for block in own]
+    terms = add_up(along_y[:, side:])
+    rows_of_weight = width // 4
+    terms = jnp.concatenate(
+        [
+            terms[:rows_of_weight].astype(bf16),
+            two_rows(terms[rows_of_weight : rows_of_weight + 1] + terms[rows_of_weight + 1 : rows_of_weight + 2]),
+        ]
+    )
+    terms = add_up(gather(terms, ROW, 16))
     back = spread_backward(rows, cols, live, place, values, blocks, col_tiles)
     grad_mixed = add_up(exchange(back, ROW)).astype(bf16)
+
+    terms = terms + swap(terms)
+    for bit in (1, 2):
+        terms = terms + lax.ppermute(terms, "x", [(i, i ^ bit) for i in range(4)])
+    grad_bias = terms[rows_of_weight] + terms[rows_of_weight + 1]
+    grad_weight = put_in_place(place, around(terms[:rows_of_weight], "yl", 4))
     grad_features = lax.dot_general(
         grad_mixed, weight, (((1,), (1,)), ((), ())), preferred_element_type=jnp.float32
     ).astype(bf16)

time: 202 us -> 194 us (0.960)
  the two profiles are of different devices: /device:TPU:8 before, /device:TPU:1 now
where the time goes in v5:
time: 194 us; the launch traced here: 191 us
  starting transfers between devices  89.6 us (46%)
  waiting for transfers between devices  47.9 us (25%)
  blocking collectives  34.6 us (18%)
  Pallas kernels  8.71 us (4%)
  local copies, waits for them, and re-layouts  4.17 us (2%)
  other arithmetic  2.43 us (1%)
  matrix products  2.07 us (1%)
    all_to_all x4, starting transfers between devices, exchange(): return lax.all_to_all(x, axes, 0, 0, tiled=True)  45.3 us
    all_to_all x2, blocking collectives, exchange(): return lax.all_to_all(x, axes, 0, 0, tiled=True)  34.6 us
    all_to_all x4, waiting for transfers between devices, exchange(): return lax.all_to_all(x, axes, 0, 0, tiled=True)  28.3 us
    ppermute x6, starting transfers between devices, swap(): return lax.ppermute(x, 'core', [(0, 1), (1, 0)])  23.2 us
    ppermute x6, starting transfers between devices, around(): lax.ppermute(x, axis, [(i, (i + k) % size) for i in range(size)])  15.7 us
    ppermute x6, waiting for transfers between devices, around(): lax.ppermute(x, axis, [(i, (i + k) % size) for i in range(size)])  8.38 us
    ppermute x2, waiting for transfers between devices, body(): terms = terms + lax.ppermute(terms, 'x', [(i, i ^ bit) for i in range(4)])  6.91 us
    ppermute x2, starting transfers between devices, body(): terms = terms + lax.ppermute(terms, 'x', [(i, i ^ bit) for i in range(4)])  5.36 us
  transfers between devices with their start and end apart: 18, of which 9 were waited for; matrix products, arithmetic and copies ran while one was open for 0% of the time, Pallas kernels for 3%

profile of v5, /device:TPU:1, one launch (start us, length us, event | category | flops | bytes accessed | tf_op | source)
XLA Modules:
  0.0 191.1 jit_solution(18004946832169135493)
XLA Ops:
  0.7 2.0 %broadcast_in_dim.65 = bf16[16,128,256]{2,1,0:T(8,128)(2,1)} broadcast(bf16[128,256]{1,0:T(8,128)(2,1)} %param.8), dimensions={1,2} | broadcast | bytes 1114112 | tf_op jit(solution)/shard_map/broadcast_in_dim | solution.py:182
  2.6 16.2 %all-to-all-start = ((bf16[16,128,256]{2,1,0:T(8,128)(2,1)}), bf16[16,128,256]{2,1,0:T(8,128)(2,1)S(1)}, u32[]{:S(2)}, u32[]{:S(2)}) async-start(bf16[16,128,256]{2,1,0:T(8,128)(2,1)} %broadcast_in_dim.65), calls=%async_computation | async-start | bytes 2097152 | tf_op jit(solution)/shard_map/all_to_all | solution.py:178
  19.6 22.7 %all-to-all-done.src = bf16[16,128,256]{2,1,0:T(8,128)(2,1)S(1)} async-done(((bf16[16,128,256]{2,1,0:T(8,128)(2,1)}), bf16[16,128,256]{2,1,0:T(8,128)(2,1)S(1)}, u32[]{:S(2)}, u32[]{:S(2)}) %all-to-all-start) | async-done | bytes 1048608 | tf_op jit(solution)/shard_map/all_to_all | solution.py:178
  42.3 3.0 %forward_tiles.1 = (bf16[16,128,256]{2,1,0:T(8,128)(2,1)S(1)}, bf16[16,128,256]{2,1,0:T(8,128)(2,1)S(1)}) custom-call(s32[128]{0:T(128)S(1)} %bitcast.20, s32[128]{0:T(128)S(1)} %bitcast.22, s32[1]{0:T(128)} %bitcast.18.live_ref, s32[3]{0:T(128)S(1)} %pad_add_fusion.core_ref.place, bf16[128,128,128]{2,1,0:T(8,128)(2,1)} %bitcast.24, ...), custom_call_target="tpu_custom_call" | custom-call | flops 1073741824 | bytes 4194304 | tf_op jit(solution)/shard_map/forward_tiles/pallas_call | solution.py:121
  45.2 6.3 %collective-permute-start = (bf16[16,128,256]{2,1,0:T(8,128)(2,1)S(1)}, bf16[16,128,256]{2,1,0:T(8,128)(2,1)S(1)}, u32[]{:S(2)}, u32[]{:S(2)}) collective-permute-start(bf16[16,128,256]{2,1,0:T(8,128)(2,1)S(1)} %get-tuple-element.7), channel_id=1, source_target_pairs={{0,1},{1,0},{2,3},{3,2},{4,5},{5,4},{6,7},{7,6},{8,9},{9,8},{10,11... | collective-permute-start | bytes 3145736 | tf_op jit(solution)/shard_map/ppermute | solution.py:174
  51.6 2.3 %collective-permute-done = bf16[16,128,256]{2,1,0:T(8,128)(2,1)S(1)} collective-permute-done((bf16[16,128,256]{2,1,0:T(8,128)(2,1)S(1)}, bf16[16,128,256]{2,1,0:T(8,128)(2,1)S(1)}, u32[]{:S(2)}, u32[]{:S(2)}) %collective-permute-start) | collective-permute-done | bytes 1048608 | tf_op jit(solution)/shard_map/ppermute | solution.py:174
  54.2 18.2 %all_to_all.30 = bf16[4,4,128,256]{3,2,1,0:T(8,128)(2,1)S(1)} all-to-all(bf16[4,4,128,256]{3,2,1,0:T(8,128)(2,1)S(1)} %bitcast.26), channel_id=1, replica_groups=mesh['yh'=2,'z'=8,'yl'=4,'x'=4,'core'=2] {'x'}, dimensions={0} | all-to-all | bytes 2097152 | tf_op jit(solution)/shard_map/all_to_all | solution.py:178
  73.3 8.7 %all-to-all-start.2 = ((bf16[4,128,256]{2,1,0:T(8,128)(2,1)}), bf16[4,128,256]{2,1,0:T(8,128)(2,1)S(1)}, u32[]{:S(2)}, u32[]{:S(2)}) async-start(bf16[4,128,256]{2,1,0:T(8,128)(2,1)} %reduce_sum.60), calls=%async_computation.2 | async-start | bytes 524288 | tf_op jit(solution)/shard_map/all_to_all | solution.py:178
  82.0 5.7 %all-to-all-done.2 = bf16[4,128,256]{2,1,0:T(8,128)(2,1)S(1)} async-done(((bf16[4,128,256]{2,1,0:T(8,128)(2,1)}), bf16[4,128,256]{2,1,0:T(8,128)(2,1)S(1)}, u32[]{:S(2)}, u32[]{:S(2)}) %all-to-all-start.2) | async-done | bytes 262176 | tf_op jit(solution)/shard_map/all_to_all | solution.py:178
  87.7 0.9 convert_reduce_fusion.3
  89.1 16.5 %all_to_all.31 = bf16[4,200,256]{2,1,0:T(8,128)(2,1)S(1)} all-to-all(bf16[4,200,256]{2,1,0:T(8,128)(2,1)S(1)} %pad_maximum_fusion), channel_id=1, replica_groups=mesh['yh'=2,'z'=8,'yl'=4,'x'=4,'core'=2] {'yl'}, dimensions={0} | all-to-all | bytes 819200 | tf_op jit(solution)/shard_map/all_to_all | solution.py:178
  106.6 8.0 %all-to-all-start.5 = ((bf16[16,72,256]{2,1,0:T(8,128)(2,1)}), bf16[16,72,256]{2,1,0:T(8,128)(2,1)S(1)}, u32[]{:S(2)}, u32[]{:S(2)}) async-start(bf16[16,72,256]{2,1,0:T(8,128)(2,1)} %broadcast_in_dim.76), calls=%async_computation.5 | async-start | bytes 1179648 | tf_op jit(solution)/shard_map/all_to_all | solution.py:178
  114.7 2.8 %collective-permute-start.3 = (bf16[4,128,256]{2,1,0:T(8,128)(2,1)S(1)}, bf16[4,128,256]{2,1,0:T(8,128)(2,1)S(1)}, u32[]{:S(2)}, u32[]{:S(2)}) collective-permute-start(bf16[4,128,256]{2,1,0:T(8,128)(2,1)S(1)} %slice.33.refs_0_), channel_id=1, source_target_pairs={{0,6},{2,0},{4,2},{6,4},{1,7},{3,1},{5,3},{7,5},{8,14},{10,8},{12,... | collective-permute-start | bytes 786440 | tf_op jit(solution)/shard_map/ppermute | solution.py:170
  117.5 3.1 %collective-permute-start.2 = (bf16[4,128,256]{2,1,0:T(8,128)(2,1)S(1)}, bf16[4,128,256]{2,1,0:T(8,128)(2,1)S(1)}, u32[]{:S(2)}, u32[]{:S(2)}) collective-permute-start(bf16[4,128,256]{2,1,0:T(8,128)(2,1)S(1)} %slice.33.refs_0_), channel_id=1, source_target_pairs={{0,4},{2,6},{4,0},{6,2},{1,5},{3,7},{5,1},{7,3},{8,12},{10,14},{12... | collective-permute-start | bytes 786440 | tf_op jit(solution)/shard_map/ppermute | solution.py:170
  120.6 1.9 %collective-permute-start.1 = (bf16[4,128,256]{2,1,0:T(8,128)(2,1)S(1)}, bf16[4,128,256]{2,1,0:T(8,128)(2,1)S(1)}, u32[]{:S(2)}, u32[]{:S(2)}) collective-permute-start(bf16[4,128,256]{2,1,0:T(8,128)(2,1)S(1)} %slice.33.refs_0_), channel_id=1, source_target_pairs={{0,2},{2,4},{4,6},{6,0},{1,3},{3,5},{5,7},{7,1},{8,10},{10,12},{12... | collective-permute-start | bytes 786440 | tf_op jit(solution)/shard_map/ppermute | solution.py:170
  122.5 4.5 %collective-permute-start.4 = (bf16[4,128,256]{2,1,0:T(8,128)(2,1)S(1)}, bf16[4,128,256]{2,1,0:T(8,128)(2,1)S(1)}, u32[]{:S(2)}, u32[]{:S(2)}) collective-permute-start(bf16[4,128,256]{2,1,0:T(8,128)(2,1)S(1)} %slice.33.refs_0_), channel_id=1, source_target_pairs={{0,1},{1,0},{2,3},{3,2},{4,5},{5,4},{6,7},{7,6},{8,9},{9,8},{10,11... | collective-permute-start | bytes 786440 | tf_op jit(solution)/shard_map/ppermute | solution.py:174
  127.0 2.7 %collective-permute-start.7 = (bf16[4,128,256]{2,1,0:T(8,128)(2,1)S(1)}, bf16[4,128,256]{2,1,0:T(8,128)(2,1)S(1)}, u32[]{:S(2)}, u32[]{:S(2)}) collective-permute-start(bf16[4,128,256]{2,1,0:T(8,128)(2,1)S(1)} %collective-permute-done.3.refs_3_), channel_id=1, source_target_pairs={{0,1},{1,0},{2,3},{3,2},{4,5},{5,4},{6,7},{7,6},{8,9},{9,8},{10,11... | collective-permute-start | bytes 786440 | tf_op jit(solution)/shard_map/ppermute | solution.py:174
  129.8 4.2 %collective-permute-start.6 = (bf16[4,128,256]{2,1,0:T(8,128)(2,1)S(1)}, bf16[4,128,256]{2,1,0:T(8,128)(2,1)S(1)}, u32[]{:S(2)}, u32[]{:S(2)}) collective-permute-start(bf16[4,128,256]{2,1,0:T(8,128)(2,1)S(1)} %collective-permute-done.2.refs_2_), channel_id=1, source_target_pairs={{0,1},{1,0},{2,3},{3,2},{4,5},{5,4},{6,7},{7,6},{8,9},{9,8},{10,11... | collective-permute-start | bytes 786440 | tf_op jit(solution)/shard_map/ppermute | solution.py:174
  134.0 3.1 %collective-permute-start.5 = (bf16[4,128,256]{2,1,0:T(8,128)(2,1)S(1)}, bf16[4,128,256]{2,1,0:T(8,128)(2,1)S(1)}, u32[]{:S(2)}, u32[]{:S(2)}) collective-permute-start(bf16[4,128,256]{2,1,0:T(8,128)(2,1)S(1)} %collective-permute-done.1.refs_1_), channel_id=1, source_target_pairs={{0,1},{1,0},{2,3},{3,2},{4,5},{5,4},{6,7},{7,6},{8,9},{9,8},{10,11... | collective-permute-start | bytes 786440 | tf_op jit(solution)/shard_map/ppermute | solution.py:174
  137.1 1.1 collective-permute-done.5.refs_5_
  138.2 4.1 %backward_tiles.1 = bf16[16,128,256]{2,1,0:T(8,128)(2,1)} custom-call(s32[128]{0:T(128)S(1)} %bitcast.21, s32[128]{0:T(128)S(1)} %bitcast.23, s32[1]{0:T(128)} %bitcast.19.live_ref, s32[3]{0:T(128)S(1)} %pad_add_fusion.core_ref.place, bf16[128,128,128]{2,1,0:T(8,128)(2,1)} %bitcast.25, bf16[4,128,256]{2,1,0:T(8,128)(2,1)S(1)} %slice.33.refs_0_, ...), custom_call_target="tpu_custom_call" | custom-call | flops 1073741824 | bytes 4194304 | tf_op jit(solution)/shard_map/backward_tiles/pallas_call | solution.py:140
  142.3 12.3 %all-to-all-start.4 = ((bf16[16,128,256]{2,1,0:T(8,128)(2,1)}), bf16[16,128,256]{2,1,0:T(8,128)(2,1)S(1)}, u32[]{:S(2)}, u32[]{:S(2)}) async-start(bf16[16,128,256]{2,1,0:T(8,128)(2,1)} %backward_tiles.1), calls=%async_computation.4 | async-start | bytes 2097152 | tf_op jit(solution)/shard_map/all_to_all | solution.py:178
  154.8 2.3 %collective-permute-start.8 = (f32[72,256]{1,0:T(8,128)S(1)}, f32[72,256]{1,0:T(8,128)S(1)}, u32[]{:S(2)}, u32[]{:S(2)}) collective-permute-start(f32[72,256]{1,0:T(8,128)S(1)} %convert_reduce_fusion), channel_id=1, source_target_pairs={{0,1},{1,0},{2,3},{3,2},{4,5},{5,4},{6,7},{7,6},{8,9},{9,8},{10,11... | collective-permute-start | bytes 221192 | tf_op jit(solution)/shard_map/ppermute | solution.py:174
  158.0 2.0 %collective-permute-start.9 = (f32[72,256]{1,0:T(8,128)S(1)}, f32[72,256]{1,0:T(8,128)S(1)}, u32[]{:S(2)}, u32[]{:S(2)}) collective-permute-start(f32[72,256]{1,0:T(8,128)S(1)} %add.33), channel_id=1, source_target_pairs={{0,2},{2,0},{4,6},{6,4},{1,3},{3,1},{5,7},{7,5},{8,10},{10,8},{12,... | collective-permute-start | bytes 221192 | tf_op jit(solution)/shard_map/ppermute | solution.py:246
  160.0 3.4 %collective-permute-done.9 = f32[72,256]{1,0:T(8,128)S(1)} collective-permute-done((f32[72,256]{1,0:T(8,128)S(1)}, f32[72,256]{1,0:T(8,128)S(1)}, u32[]{:S(2)}, u32[]{:S(2)}) %collective-permute-start.9) | collective-permute-done | bytes 73760 | tf_op jit(solution)/shard_map/ppermute | solution.py:246
  163.4 3.3 %collective-permute-start.10 = (f32[72,256]{1,0:T(8,128)S(1)}, f32[72,256]{1,0:T(8,128)S(1)}, u32[]{:S(2)}, u32[]{:S(2)}) collective-permute-start(f32[72,256]{1,0:T(8,128)S(1)} %add.34), channel_id=1, source_target_pairs={{0,4},{2,6},{4,0},{6,2},{1,5},{3,7},{5,1},{7,3},{8,12},{10,14},{12... | collective-permute-start | bytes 221192 | tf_op jit(solution)/shard_map/ppermute | solution.py:246
  166.7 3.6 %collective-permute-done.10 = f32[72,256]{1,0:T(8,128)S(1)} collective-permute-done((f32[72,256]{1,0:T(8,128)S(1)}, f32[72,256]{1,0:T(8,128)S(1)}, u32[]{:S(2)}, u32[]{:S(2)}) %collective-permute-start.10) | collective-permute-done | bytes 73760 | tf_op jit(solution)/shard_map/ppermute | solution.py:246
  170.3 3.7 %collective-permute-start.13 = (f32[64,256]{1,0:T(8,128)S(1)}, f32[64,256]{1,0:T(8,128)S(1)}, u32[]{:S(2)}, u32[]{:S(2)}) collective-permute-start(f32[64,256]{1,0:T(8,128)S(1)} %slice.38.a), channel_id=1, source_target_pairs={{0,24},{8,0},{16,8},{24,16},{1,25},{9,1},{17,9},{25,17},{2,26},{10... | collective-permute-start | bytes 196616 | tf_op jit(solution)/shard_map/ppermute | solution.py:170
  174.1 2.3 %collective-permute-start.12 = (f32[64,256]{1,0:T(8,128)S(1)}, f32[64,256]{1,0:T(8,128)S(1)}, u32[]{:S(2)}, u32[]{:S(2)}) collective-permute-start(f32[64,256]{1,0:T(8,128)S(1)} %slice.38.a), channel_id=1, source_target_pairs={{0,16},{8,24},{16,0},{24,8},{1,17},{9,25},{17,1},{25,9},{2,18},{10... | collective-permute-start | bytes 196616 | tf_op jit(solution)/shard_map/ppermute | solution.py:170
  176.4 1.9 %collective-permute-start.11 = (f32[64,256]{1,0:T(8,128)S(1)}, f32[64,256]{1,0:T(8,128)S(1)}, u32[]{:S(2)}, u32[]{:S(2)}) collective-permute-start(f32[64,256]{1,0:T(8,128)S(1)} %slice.38.a), channel_id=1, source_target_pairs={{0,8},{8,16},{16,24},{24,0},{1,9},{9,17},{17,25},{25,1},{2,10},{10... | collective-permute-start | bytes 196616 | tf_op jit(solution)/shard_map/ppermute | solution.py:170
  179.7 7.6 %collective-permute-done.12.c = f32[64,256]{1,0:T(8,128)S(1)} collective-permute-done((f32[64,256]{1,0:T(8,128)S(1)}, f32[64,256]{1,0:T(8,128)S(1)}, u32[]{:S(2)}, u32[]{:S(2)}) %collective-permute-start.12) | collective-permute-done | bytes 65568 | tf_op jit(solution)/shard_map/ppermute | solution.py:170
  188.5 1.7 place_pieces.1
  (58 shorter events, 7.5 us)
Async XLA Ops:
  0.6 87.0 %copy-start = (bf16[256,256]{1,0:T(8,128)(2,1)S(1)}, bf16[256,256]{1,0:T(8,128)(2,1)}, u32[]{:S(2)}) copy-start(bf16[256,256]{1,0:T(8,128)(2,1)} %param.9) | copy-start | bytes 393220
  0.6 41.6 %copy-start.3 = (s32[1,1,128]{2,1,0:T(1,128)S(1)}, s32[1,1,128]{2,1,0:T(1,128)}, u32[]{:S(2)}) copy-start(s32[1,1,128]{2,1,0:T(1,128)} %param.13) | copy-start | bytes 1540
  0.7 41.6 %copy-start.2 = (s32[1,1,128]{2,1,0:T(1,128)S(1)}, s32[1,1,128]{2,1,0:T(1,128)}, u32[]{:S(2)}) copy-start(s32[1,1,128]{2,1,0:T(1,128)} %param.12) | copy-start | bytes 1540
  2.6 39.6 %all-to-all-start = ((bf16[16,128,256]{2,1,0:T(8,128)(2,1)}), bf16[16,128,256]{2,1,0:T(8,128)(2,1)S(1)}, u32[]{:S(2)}, u32[]{:S(2)}) async-start(bf16[16,128,256]{2,1,0:T(8,128)(2,1)} %broadcast_in_dim.65), calls=%async_computation | async-start | bytes 2097152 | tf_op jit(solution)/shard_map/all_to_all | solution.py:178
  19.6 118.7 %copy-start.1 = (s32[3]{0:T(128)}, s32[3]{0:T(128)S(1)}, u32[]{:S(2)}) copy-start(s32[3]{0:T(128)S(1)} %pad_add_fusion.core_ref.place) | copy-start | bytes 40
  45.2 8.6 %collective-permute-start = (bf16[16,128,256]{2,1,0:T(8,128)(2,1)S(1)}, bf16[16,128,256]{2,1,0:T(8,128)(2,1)S(1)}, u32[]{:S(2)}, u32[]{:S(2)}) collective-permute-start(bf16[16,128,256]{2,1,0:T(8,128)(2,1)S(1)} %get-tuple-element.7), channel_id=1, source_target_pairs={{0,1},{1,0},{2,3},{3,2},{4,5},{5,4},{6,7},{7,6},{8,9},{9,8},{10,11... | collective-permute-start | bytes 3145736 | tf_op jit(solution)/shard_map/ppermute | solution.py:174
  54.2 33.5 %copy-start.8 = (bf16[128,256]{1,0:T(8,128)(2,1)S(1)}, bf16[128,256]{1,0:T(8,128)(2,1)}, u32[]{:S(2)}) copy-start(bf16[128,256]{1,0:T(8,128)(2,1)} %param.11) | copy-start | bytes 196612
  54.2 33.5 %copy-start.9 = (f32[256]{0:T(256)S(1)}, f32[256]{0:T(256)}, u32[]{:S(2)}) copy-start(f32[256]{0:T(256)} %param.10) | copy-start | bytes 3076
  73.3 14.3 %all-to-all-start.2 = ((bf16[4,128,256]{2,1,0:T(8,128)(2,1)}), bf16[4,128,256]{2,1,0:T(8,128)(2,1)S(1)}, u32[]{:S(2)}, u32[]{:S(2)}) async-start(bf16[4,128,256]{2,1,0:T(8,128)(2,1)} %reduce_sum.60), calls=%async_computation.2 | async-start | bytes 524288 | tf_op jit(solution)/shard_map/all_to_all | solution.py:178
  106.6 35.7 %all-to-all-start.5 = ((bf16[16,72,256]{2,1,0:T(8,128)(2,1)}), bf16[16,72,256]{2,1,0:T(8,128)(2,1)S(1)}, u32[]{:S(2)}, u32[]{:S(2)}) async-start(bf16[16,72,256]{2,1,0:T(8,128)(2,1)} %broadcast_in_dim.76), calls=%async_computation.5 | async-start | bytes 1179648 | tf_op jit(solution)/shard_map/all_to_all | solution.py:178
  114.7 12.4 %collective-permute-start.3 = (bf16[4,128,256]{2,1,0:T(8,128)(2,1)S(1)}, bf16[4,128,256]{2,1,0:T(8,128)(2,1)S(1)}, u32[]{:S(2)}, u32[]{:S(2)}) collective-permute-start(bf16[4,128,256]{2,1,0:T(8,128)(2,1)S(1)} %slice.33.refs_0_), channel_id=1, source_target_pairs={{0,6},{2,0},{4,2},{6,4},{1,7},{3,1},{5,3},{7,5},{8,14},{10,8},{12,... | collective-permute-start | bytes 786440 | tf_op jit(solution)/shard_map/ppermute | solution.py:170
  117.5 12.3 %collective-permute-start.2 = (bf16[4,128,256]{2,1,0:T(8,128)(2,1)S(1)}, bf16[4,128,256]{2,1,0:T(8,128)(2,1)S(1)}, u32[]{:S(2)}, u32[]{:S(2)}) collective-permute-start(bf16[4,128,256]{2,1,0:T(8,128)(2,1)S(1)} %slice.33.refs_0_), channel_id=1, source_target_pairs={{0,4},{2,6},{4,0},{6,2},{1,5},{3,7},{5,1},{7,3},{8,12},{10,14},{12... | collective-permute-start | bytes 786440 | tf_op jit(solution)/shard_map/ppermute | solution.py:170
  120.6 13.4 %collective-permute-start.1 = (bf16[4,128,256]{2,1,0:T(8,128)(2,1)S(1)}, bf16[4,128,256]{2,1,0:T(8,128)(2,1)S(1)}, u32[]{:S(2)}, u32[]{:S(2)}) collective-permute-start(bf16[4,128,256]{2,1,0:T(8,128)(2,1)S(1)} %slice.33.refs_0_), channel_id=1, source_target_pairs={{0,2},{2,4},{4,6},{6,0},{1,3},{3,5},{5,7},{7,1},{8,10},{10,12},{12... | collective-permute-start | bytes 786440 | tf_op jit(solution)/shard_map/ppermute | solution.py:170
  122.5 14.6 %collective-permute-start.4 = (bf16[4,128,256]{2,1,0:T(8,128)(2,1)S(1)}, bf16[4,128,256]{2,1,0:T(8,128)(2,1)S(1)}, u32[]{:S(2)}, u32[]{:S(2)}) collective-permute-start(bf16[4,128,256]{2,1,0:T(8,128)(2,1)S(1)} %slice.33.refs_0_), channel_id=1, source_target_pairs={{0,1},{1,0},{2,3},{3,2},{4,5},{5,4},{6,7},{7,6},{8,9},{9,8},{10,11... | collective-permute-start | bytes 786440 | tf_op jit(solution)/shard_map/ppermute | solution.py:174
  127.0 10.1 %collective-permute-start.7 = (bf16[4,128,256]{2,1,0:T(8,128)(2,1)S(1)}, bf16[4,128,256]{2,1,0:T(8,128)(2,1)S(1)}, u32[]{:S(2)}, u32[]{:S(2)}) collective-permute-start(bf16[4,128,256]{2,1,0:T(8,128)(2,1)S(1)} %collective-permute-done.3.refs_3_), channel_id=1, source_target_pairs={{0,1},{1,0},{2,3},{3,2},{4,5},{5,4},{6,7},{7,6},{8,9},{9,8},{10,11... | collective-permute-start | bytes 786440 | tf_op jit(solution)/shard_map/ppermute | solution.py:174
  129.8 7.4 %collective-permute-start.6 = (bf16[4,128,256]{2,1,0:T(8,128)(2,1)S(1)}, bf16[4,128,256]{2,1,0:T(8,128)(2,1)S(1)}, u32[]{:S(2)}, u32[]{:S(2)}) collective-permute-start(bf16[4,128,256]{2,1,0:T(8,128)(2,1)S(1)} %collective-permute-done.2.refs_2_), channel_id=1, source_target_pairs={{0,1},{1,0},{2,3},{3,2},{4,5},{5,4},{6,7},{7,6},{8,9},{9,8},{10,11... | collective-permute-start | bytes 786440 | tf_op jit(solution)/shard_map/ppermute | solution.py:174
  134.0 4.2 %collective-permute-start.5 = (bf16[4,128,256]{2,1,0:T(8,128)(2,1)S(1)}, bf16[4,128,256]{2,1,0:T(8,128)(2,1)S(1)}, u32[]{:S(2)}, u32[]{:S(2)}) collective-permute-start(bf16[4,128,256]{2,1,0:T(8,128)(2,1)S(1)} %collective-permute-done.1.refs_1_), channel_id=1, source_target_pairs={{0,1},{1,0},{2,3},{3,2},{4,5},{5,4},{6,7},{7,6},{8,9},{9,8},{10,11... | collective-permute-start | bytes 786440 | tf_op jit(solution)/shard_map/ppermute | solution.py:174
  142.3 47.8 %all-to-all-start.4 = ((bf16[16,128,256]{2,1,0:T(8,128)(2,1)}), bf16[16,128,256]{2,1,0:T(8,128)(2,1)S(1)}, u32[]{:S(2)}, u32[]{:S(2)}) async-start(bf16[16,128,256]{2,1,0:T(8,128)(2,1)} %backward_tiles.1), calls=%async_computation.4 | async-start | bytes 2097152 | tf_op jit(solution)/shard_map/all_to_all | solution.py:178
  154.8 3.2 %collective-permute-start.8 = (f32[72,256]{1,0:T(8,128)S(1)}, f32[72,256]{1,0:T(8,128)S(1)}, u32[]{:S(2)}, u32[]{:S(2)}) collective-permute-start(f32[72,256]{1,0:T(8,128)S(1)} %convert_reduce_fusion), channel_id=1, source_target_pairs={{0,1},{1,0},{2,3},{3,2},{4,5},{5,4},{6,7},{7,6},{8,9},{9,8},{10,11... | collective-permute-start | bytes 221192 | tf_op jit(solution)/shard_map/ppermute | solution.py:174
  158.0 5.4 %collective-permute-start.9 = (f32[72,256]{1,0:T(8,128)S(1)}, f32[72,256]{1,0:T(8,128)S(1)}, u32[]{:S(2)}, u32[]{:S(2)}) collective-permute-start(f32[72,256]{1,0:T(8,128)S(1)} %add.33), channel_id=1, source_target_pairs={{0,2},{2,0},{4,6},{6,4},{1,3},{3,1},{5,7},{7,5},{8,10},{10,8},{12,... | collective-permute-start | bytes 221192 | tf_op jit(solution)/shard_map/ppermute | solution.py:246
  163.4 6.9 %collective-permute-start.10 = (f32[72,256]{1,0:T(8,128)S(1)}, f32[72,256]{1,0:T(8,128)S(1)}, u32[]{:S(2)}, u32[]{:S(2)}) collective-permute-start(f32[72,256]{1,0:T(8,128)S(1)} %add.34), channel_id=1, source_target_pairs={{0,4},{2,6},{4,0},{6,2},{1,5},{3,7},{5,1},{7,3},{8,12},{10,14},{12... | collective-permute-start | bytes 221192 | tf_op jit(solution)/shard_map/ppermute | solution.py:246
  170.3 16.9 %copy-start.4 = (f32[64,256]{1,0:T(8,128)}, f32[64,256]{1,0:T(8,128)S(1)}, u32[]{:S(2)}) copy-start(f32[64,256]{1,0:T(8,128)S(1)} %slice.38.a) | copy-start | bytes 196612
  170.3 9.3 %collective-permute-start.13 = (f32[64,256]{1,0:T(8,128)S(1)}, f32[64,256]{1,0:T(8,128)S(1)}, u32[]{:S(2)}, u32[]{:S(2)}) collective-permute-start(f32[64,256]{1,0:T(8,128)S(1)} %slice.38.a), channel_id=1, source_target_pairs={{0,24},{8,0},{16,8},{24,16},{1,25},{9,1},{17,9},{25,17},{2,26},{10... | collective-permute-start | bytes 196616 | tf_op jit(solution)/shard_map/ppermute | solution.py:170
  174.1 13.2 %collective-permute-start.12 = (f32[64,256]{1,0:T(8,128)S(1)}, f32[64,256]{1,0:T(8,128)S(1)}, u32[]{:S(2)}, u32[]{:S(2)}) collective-permute-start(f32[64,256]{1,0:T(8,128)S(1)} %slice.38.a), channel_id=1, source_target_pairs={{0,16},{8,24},{16,0},{24,8},{1,17},{9,25},{17,1},{25,9},{2,18},{10... | collective-permute-start | bytes 196616 | tf_op jit(solution)/shard_map/ppermute | solution.py:170
  176.4 10.9 %collective-permute-start.11 = (f32[64,256]{1,0:T(8,128)S(1)}, f32[64,256]{1,0:T(8,128)S(1)}, u32[]{:S(2)}, u32[]{:S(2)}) collective-permute-start(f32[64,256]{1,0:T(8,128)S(1)} %slice.38.a), channel_id=1, source_target_pairs={{0,8},{8,16},{16,24},{24,0},{1,9},{9,17},{17,25},{25,1},{2,10},{10... | collective-permute-start | bytes 196616 | tf_op jit(solution)/shard_map/ppermute | solution.py:170
  179.7 7.6 %copy-start.5 = (f32[64,256]{1,0:T(8,128)}, f32[64,256]{1,0:T(8,128)S(1)}, u32[]{:S(2)}) copy-start(f32[64,256]{1,0:T(8,128)S(1)} %collective-permute-done.13.d) | copy-start | bytes 196612
  187.2 0.6 copy-start.6
  187.9 0.6 copy-start.7

commit v6 on v4

--- a/solution.py
+++ b/solution.py
@@ -192,27 +192,32 @@
     row_tiles, col_tiles = 32, 16
     bf16 = jnp.bfloat16
     core = lax.axis_index("core").astype(jnp.int32).reshape(1)
-
-    block = gather(features, ROW, col_tiles)
+    line = lax.axis_index("yl")
+    around = [grad_out] + [lax.ppermute(grad_out, "yl", [(i, (i + k) % 4) for i in range(4)]) for k in range(1, 4)]
+    grad_line = jnp.stack([lax.select_n((line - t) & 3, *around) for t in range(4)])
+
+    block, grad_line = lax.optimization_barrier((gather(features, ROW, col_tiles), grad_line))
     kept, sent = spread_forward(rows, cols, live, core, values, block, row_tiles)
     by_core = (kept.astype(jnp.float32) + swap(sent).astype(jnp.float32)).astype(bf16)
     by_x = add_up(exchange(by_core.reshape(4, 4, side, width), "x")).astype(bf16)
-    mean = add_up(exchange(by_x, "yl"))
+    mean = add_up(gather(by_x, "yl", 4)).reshape(4 * side, width)
     pre = (
         jnp.dot(mean, weight.astype(jnp.float32), precision=lax.Precision.HIGHEST, preferred_element_type=jnp.float32)
         + bias[None, :]
     )
-    grad_pre = (grad_out.astype(jnp.float32) * elu_slope(pre)).astype(bf16)
-    output = elu_value(pre).astype(bf16)
-
-    grad32 = grad_pre.astype(jnp.float32)
+    grad_pre = (grad_line.reshape(4 * side, width).astype(jnp.float32) * elu_slope(pre)).astype(bf16)
+    output = elu_value(lax.dynamic_slice_in_dim(pre, line * side, side, 0)).astype(bf16)
+
+    mine = lax.dynamic_slice_in_dim(mean, line * (width // 4), width // 4, 1)
     weight_term = lax.dot_general(
-        mean, grad32, (((0,), (0,)), ((), ())), precision=lax.Precision.HIGHEST, preferred_element_type=jnp.float32
-    )
-    terms = weight_term.astype(bf16).reshape(4, width // 4, width)
-    along_y = gather_and_scatter(grad_pre, terms, "yl")
-    terms = add_up(along_y[:, side:]).astype(bf16).reshape(4, width // 16, width)
-    own = gather_and_scatter(along_y[:, :side].reshape(4 * side, width), terms, "x")
+        mine,
+        grad_pre.astype(jnp.float32),
+        (((0,), (0,)), ((), ())),
+        precision=lax.Precision.HIGHEST,
+        preferred_element_type=jnp.float32,
+    )
+    terms = weight_term.astype(bf16).reshape(4, width // 16, width)
+    own = gather_and_scatter(grad_pre, terms, "x")
     back = spread_backward(rows, cols, live, core, values, own, swap(own), col_tiles)
 
     reduced = add_up(exchange(back, ROW))

time: 192 us -> 200 us (1.042)
  blocking collectives: 99.4 us -> 34.2 us
  waiting for transfers between devices: 37 us -> 91.2 us
  starting transfers between devices: 40.2 us -> 56.8 us
    all_to_all x5 -> x2, blocking collectives: 99.4 us -> 34.2 us  [exchange(): return lax.all_to_all(x, axes, 0, 0, tiled=True)]
    all_to_all x2 -> x4, waiting for transfers between devices: 32.5 us -> 67.5 us  [exchange(): return lax.all_to_all(x, axes, 0, 0, tiled=True)]
    ppermute x0 -> x3, waiting for transfers between devices: none -> 19.2 us  [body(): lax.ppermute(grad_out, 'yl', [(i, (i + k) % 4) for i in range(4)])]
    all_to_all x2 -> x4, starting transfers between devices: 28 us -> 38.1 us  [exchange(): return lax.all_to_all(x, axes, 0, 0, tiled=True)]
    ppermute x0 -> x3, starting transfers between devices: none -> 8.22 us  [body(): lax.ppermute(grad_out, 'yl', [(i, (i + k) % 4) for i in range(4)])]
  transfers between devices with their start and end apart: 4 -> 9, of which waited for: 4 -> 7; matrix products, arithmetic and copies ran while one was open for 1% -> 1% of each run, Pallas kernels for 0% -> 0%
where the time goes in v6:
time: 200 us
  waiting for transfers between devices  91.2 us (46%)
  starting transfers between devices  56.8 us (28%)
  blocking collectives  34.2 us (17%)
  Pallas kernels  7.38 us (4%)
  local copies, waits for them, and re-layouts  4.55 us (2%)
  other arithmetic  2.29 us (1%)
    all_to_all x4, waiting for transfers between devices, exchange(): return lax.all_to_all(x, axes, 0, 0, tiled=True)  67.5 us
    all_to_all x4, starting transfers between devices, exchange(): return lax.all_to_all(x, axes, 0, 0, tiled=True)  38.1 us
    all_to_all x2, blocking collectives, exchange(): return lax.all_to_all(x, axes, 0, 0, tiled=True)  34.2 us
    ppermute x3, waiting for transfers between devices, body(): lax.ppermute(grad_out, 'yl', [(i, (i + k) % 4) for i in range(4)])  19.2 us
    ppermute x2, starting transfers between devices, swap(): return lax.ppermute(x, 'core', [(0, 1), (1, 0)])  10.5 us
    ppermute x3, starting transfers between devices, body(): lax.ppermute(grad_out, 'yl', [(i, (i + k) % 4) for i in range(4)])  8.22 us
    ppermute x2, waiting for transfers between devices, swap(): return lax.ppermute(x, 'core', [(0, 1), (1, 0)])  4.58 us
    pallas_call x1, Pallas kernels, spread_backward(): pl.pallas_call(backward_kernel, out_shape=jax.ShapeDtypeStruct((col_tiles...  4.41 us
  transfers between devices with their start and end apart: 9, of which 7 were waited for; matrix products, arithmetic and copies ran while one was open for 1% of the time, Pallas kernels for 0%

profile of v6, /device:TPU:1, one launch (start us, length us, event | category | flops | bytes accessed | tf_op | source)
XLA Modules:
  0.0 199.8 jit_solution(10723399621948753473)
XLA Ops:
  0.7 2.0 broadcast_in_dim.12
  2.6 16.2 %all-to-all-start = ((bf16[16,128,256]{2,1,0:T(8,128)(2,1)}), bf16[16,128,256]{2,1,0:T(8,128)(2,1)S(1)}, u32[]{:S(2)}, u32[]{:S(2)}) async-start(bf16[16,128,256]{2,1,0:T(8,128)(2,1)} %broadcast_in_dim.12), calls=%async_computation | async-start | bytes 2097152 | tf_op jit(solution)/shard_map/all_to_all | solution.py:171
  18.9 2.4 %collective-permute-start.1 = (bf16[128,256]{1,0:T(8,128)(2,1)S(1)}, bf16[128,256]{1,0:T(8,128)(2,1)S(1)}, u32[]{:S(2)}, u32[]{:S(2)}) collective-permute-start(bf16[128,256]{1,0:T(8,128)(2,1)S(1)} %copy-done.3), channel_id=1, source_target_pairs={{0,16},{8,24},{16,0},{24,8},{1,17},{9,25},{17,1},{25,9},{2,18},{10... | collective-permute-start | bytes 196616 | tf_op jit(solution)/shard_map/ppermute | solution.py:196
  21.3 3.9 %collective-permute-start.2 = (bf16[128,256]{1,0:T(8,128)(2,1)S(1)}, bf16[128,256]{1,0:T(8,128)(2,1)S(1)}, u32[]{:S(2)}, u32[]{:S(2)}) collective-permute-start(bf16[128,256]{1,0:T(8,128)(2,1)S(1)} %copy-done.3), channel_id=1, source_target_pairs={{0,24},{8,0},{16,8},{24,16},{1,25},{9,1},{17,9},{25,17},{2,26},{10... | collective-permute-start | bytes 196616 | tf_op jit(solution)/shard_map/ppermute | solution.py:196
  25.2 1.9 collective-permute-start
  27.8 8.6 %collective-permute-done.1 = bf16[128,256]{1,0:T(8,128)(2,1)S(1)} collective-permute-done((bf16[128,256]{1,0:T(8,128)(2,1)S(1)}, bf16[128,256]{1,0:T(8,128)(2,1)S(1)}, u32[]{:S(2)}, u32[]{:S(2)}) %collective-permute-start.1) | collective-permute-done | bytes 65568 | tf_op jit(solution)/shard_map/ppermute | solution.py:196
  36.4 10.5 %collective-permute-done.2 = bf16[128,256]{1,0:T(8,128)(2,1)S(1)} collective-permute-done((bf16[128,256]{1,0:T(8,128)(2,1)S(1)}, bf16[128,256]{1,0:T(8,128)(2,1)S(1)}, u32[]{:S(2)}, u32[]{:S(2)}) %collective-permute-start.2) | collective-permute-done | bytes 65568 | tf_op jit(solution)/shard_map/ppermute | solution.py:196
  47.1 3.0 %forward_tiles.1 = (bf16[16,128,256]{2,1,0:T(8,128)(2,1)S(1)}, bf16[16,128,256]{2,1,0:T(8,128)(2,1)S(1)}) custom-call(s32[128]{0:T(128)S(1)} %bitcast.27, s32[128]{0:T(128)S(1)} %bitcast.29, s32[1]{0:T(128)} %bitcast.25.live_ref, s32[1]{0:T(128)} %bitcast.3.core_ref, bf16[128,128,128]{2,1,0:T(8,128)(2,1)} %bitcast.31, bf16[16,128,256]{2,1,0:T(8,128)(2,1)S(1)} %all-to-all-done.src), custom_call_target="tpu_custom_call" | custom-call | flops 1073741824 | bytes 4194304 | tf_op jit(solution)/shard_map/forward_tiles/pallas_call | solution.py:129
  50.1 6.0 %collective-permute-start.3 = (bf16[16,128,256]{2,1,0:T(8,128)(2,1)S(1)}, bf16[16,128,256]{2,1,0:T(8,128)(2,1)S(1)}, u32[]{:S(2)}, u32[]{:S(2)}) collective-permute-start(bf16[16,128,256]{2,1,0:T(8,128)(2,1)S(1)} %get-tuple-element.10), channel_id=1, source_target_pairs={{0,1},{1,0},{2,3},{3,2},{4,5},{5,4},{6,7},{7,6},{8,9},{9,8},{10,11... | collective-permute-start | bytes 3145736 | tf_op jit(solution)/shard_map/ppermute | solution.py:167
  56.0 2.3 %collective-permute-done.3 = bf16[16,128,256]{2,1,0:T(8,128)(2,1)S(1)} collective-permute-done((bf16[16,128,256]{2,1,0:T(8,128)(2,1)S(1)}, bf16[16,128,256]{2,1,0:T(8,128)(2,1)S(1)}, u32[]{:S(2)}, u32[]{:S(2)}) %collective-permute-start.3) | collective-permute-done | bytes 1048608 | tf_op jit(solution)/shard_map/ppermute | solution.py:167
  58.3 0.4 add_convert_fusion
  58.7 18.0 %all_to_all.30 = bf16[4,4,128,256]{3,2,1,0:T(8,128)(2,1)S(1)} all-to-all(bf16[4,4,128,256]{3,2,1,0:T(8,128)(2,1)S(1)} %bitcast.33), channel_id=1, replica_groups=mesh['yh'=2,'z'=8,'yl'=4,'x'=4,'core'=2] {'x'}, dimensions={0} | all-to-all | bytes 2097152 | tf_op jit(solution)/shard_map/all_to_all | solution.py:171
  76.7 0.2 reduce_sum.30
  76.9 1.1 broadcast_in_dim.13
  78.0 6.0 %all-to-all-start.2 = ((bf16[4,4,128,256]{3,2,1,0:T(8,128)(2,1)}), bf16[4,4,128,256]{3,2,1,0:T(8,128)(2,1)S(1)}, u32[]{:S(2)}, u32[]{:S(2)}) async-start(bf16[4,4,128,256]{3,2,1,0:T(8,128)(2,1)} %broadcast_in_dim.13), calls=%async_computation.2 | async-start | bytes 2097152 | tf_op jit(solution)/shard_map/all_to_all | solution.py:171
  84.1 25.2 %all-to-all-done.2 = bf16[4,4,128,256]{3,2,1,0:T(8,128)(2,1)S(1)} async-done(((bf16[4,4,128,256]{3,2,1,0:T(8,128)(2,1)}), bf16[4,4,128,256]{3,2,1,0:T(8,128)(2,1)S(1)}, u32[]{:S(2)}, u32[]{:S(2)}) %all-to-all-start.2) | async-done | bytes 1048608 | tf_op jit(solution)/shard_map/all_to_all | solution.py:171
  109.5 0.5 fusion
  109.9 0.5 convolution_convert_fusion.1
  110.6 16.1 %all_to_all.31.own = bf16[4,528,256]{2,1,0:T(8,128)(2,1)S(1)} all-to-all(bf16[4,528,256]{2,1,0:T(8,128)(2,1)S(1)} %pad_maximum_fusion), channel_id=1, replica_groups=mesh['yh'=2,'z'=8,'yl'=4,'x'=4,'core'=2] {'x'}, dimensions={0} | all-to-all | bytes 2162688 | tf_op jit(solution)/shard_map/all_to_all | solution.py:171
  126.7 4.6 %collective-permute-start.4 = (bf16[4,528,256]{2,1,0:T(8,128)(2,1)S(1)}, bf16[4,528,256]{2,1,0:T(8,128)(2,1)S(1)}, u32[]{:S(2)}, u32[]{:S(2)}) collective-permute-start(bf16[4,528,256]{2,1,0:T(8,128)(2,1)S(1)} %all_to_all.31.own), channel_id=1, source_target_pairs={{0,1},{1,0},{2,3},{3,2},{4,5},{5,4},{6,7},{7,6},{8,9},{9,8},{10,11... | collective-permute-start | bytes 3244040 | tf_op jit(solution)/shard_map/ppermute | solution.py:167
  131.3 2.3 %collective-permute-done.4.other = bf16[4,528,256]{2,1,0:T(8,128)(2,1)S(1)} collective-permute-done((bf16[4,528,256]{2,1,0:T(8,128)(2,1)S(1)}, bf16[4,528,256]{2,1,0:T(8,128)(2,1)S(1)}, u32[]{:S(2)}, u32[]{:S(2)}) %collective-permute-start.4) | collective-permute-done | bytes 1081376 | tf_op jit(solution)/shard_map/ppermute | solution.py:167
  133.6 4.4 %backward_tiles.1 = bf16[16,144,256]{2,1,0:T(8,128)(2,1)} custom-call(s32[128]{0:T(128)S(1)} %bitcast.28, s32[128]{0:T(128)S(1)} %bitcast.30, s32[1]{0:T(128)} %bitcast.26.live_ref, s32[1]{0:T(128)} %bitcast.3.core_ref, bf16[128,128,128]{2,1,0:T(8,128)(2,1)} %bitcast.32, bf16[4,528,256]{2,1,0:T(8,128)(2,1)S(1)} %all_to_all.31.own, ...), custom_call_target="tpu_custom_call" | custom-call | flops 1073741824 | bytes 4194304 | tf_op jit(solution)/shard_map/backward_tiles/pallas_call | solution.py:148
  138.0 10.5 %all-to-all-start.4 = ((bf16[16,144,256]{2,1,0:T(8,128)(2,1)}), bf16[16,144,256]{2,1,0:T(8,128)(2,1)S(1)}, u32[]{:S(2)}, u32[]{:S(2)}) async-start(bf16[16,144,256]{2,1,0:T(8,128)(2,1)} %backward_tiles.1), calls=%async_computation.4 | async-start | bytes 2359296 | tf_op jit(solution)/shard_map/all_to_all | solution.py:171
  148.6 33.2 %all-to-all-done.4 = bf16[16,144,256]{2,1,0:T(8,128)(2,1)S(1)} async-done(((bf16[16,144,256]{2,1,0:T(8,128)(2,1)}), bf16[16,144,256]{2,1,0:T(8,128)(2,1)S(1)}, u32[]{:S(2)}, u32[]{:S(2)}) %all-to-all-start.4) | async-done | bytes 1179680 | tf_op jit(solution)/shard_map/all_to_all | solution.py:171
  181.8 0.2 convert_reduce_fusion
  182.0 0.7 broadcast_in_dim.16
  182.7 5.3 %all-to-all-start.5 = ((f32[32,8,256]{2,1,0:T(8,128)}), f32[32,8,256]{2,1,0:T(8,128)S(1)}, u32[]{:S(2)}, u32[]{:S(2)}) async-start(f32[32,8,256]{2,1,0:T(8,128)} %broadcast_in_dim.16), calls=%async_computation.5 | async-start | bytes 524288 | tf_op jit(solution)/shard_map/all_to_all | solution.py:171
  188.0 0.7 fusion.2
  188.7 0.6 slice_add_fusion
  189.2 0.8 convolution_convert_fusion
  190.0 9.0 %all-to-all-done.5 = f32[32,8,256]{2,1,0:T(8,128)S(1)} async-done(((f32[32,8,256]{2,1,0:T(8,128)}), f32[32,8,256]{2,1,0:T(8,128)S(1)}, u32[]{:S(2)}, u32[]{:S(2)}) %all-to-all-start.5) | async-done | bytes 262176 | tf_op jit(solution)/shard_map/all_to_all | solution.py:171
  199.1 0.7 copy.14
  (18 shorter events, 0.4 us)
Async XLA Ops:
  0.6 108.8 %copy-start = (bf16[256,256]{1,0:T(8,128)(2,1)S(1)}, bf16[256,256]{1,0:T(8,128)(2,1)}, u32[]{:S(2)}) copy-start(bf16[256,256]{1,0:T(8,128)(2,1)} %param.9) | copy-start | bytes 393220
  0.6 18.2 %copy-start.3 = (bf16[128,256]{1,0:T(8,128)(2,1)S(1)}, bf16[128,256]{1,0:T(8,128)(2,1)}, u32[]{:S(2)}) copy-start(bf16[128,256]{1,0:T(8,128)(2,1)} %param.11) | copy-start | bytes 196612
  0.7 46.4 %copy-start.1 = (s32[1,1,128]{2,1,0:T(1,128)S(1)}, s32[1,1,128]{2,1,0:T(1,128)}, u32[]{:S(2)}) copy-start(s32[1,1,128]{2,1,0:T(1,128)} %param.12) | copy-start | bytes 1540
  0.7 46.4 %copy-start.2 = (s32[1,1,128]{2,1,0:T(1,128)S(1)}, s32[1,1,128]{2,1,0:T(1,128)}, u32[]{:S(2)}) copy-start(s32[1,1,128]{2,1,0:T(1,128)} %param.13) | copy-start | bytes 1540
  2.6 44.4 %all-to-all-start = ((bf16[16,128,256]{2,1,0:T(8,128)(2,1)}), bf16[16,128,256]{2,1,0:T(8,128)(2,1)S(1)}, u32[]{:S(2)}, u32[]{:S(2)}) async-start(bf16[16,128,256]{2,1,0:T(8,128)(2,1)} %broadcast_in_dim.12), calls=%async_computation | async-start | bytes 2097152 | tf_op jit(solution)/shard_map/all_to_all | solution.py:171
  18.9 17.6 %collective-permute-start.1 = (bf16[128,256]{1,0:T(8,128)(2,1)S(1)}, bf16[128,256]{1,0:T(8,128)(2,1)S(1)}, u32[]{:S(2)}, u32[]{:S(2)}) collective-permute-start(bf16[128,256]{1,0:T(8,128)(2,1)S(1)} %copy-done.3), channel_id=1, source_target_pairs={{0,16},{8,24},{16,0},{24,8},{1,17},{9,25},{17,1},{25,9},{2,18},{10... | collective-permute-start | bytes 196616 | tf_op jit(solution)/shard_map/ppermute | solution.py:196
  21.3 25.7 %collective-permute-start.2 = (bf16[128,256]{1,0:T(8,128)(2,1)S(1)}, bf16[128,256]{1,0:T(8,128)(2,1)S(1)}, u32[]{:S(2)}, u32[]{:S(2)}) collective-permute-start(bf16[128,256]{1,0:T(8,128)(2,1)S(1)} %copy-done.3), channel_id=1, source_target_pairs={{0,24},{8,0},{16,8},{24,16},{1,25},{9,1},{17,9},{25,17},{2,26},{10... | collective-permute-start | bytes 196616 | tf_op jit(solution)/shard_map/ppermute | solution.py:196
  25.2 21.8 %collective-permute-start = (bf16[128,256]{1,0:T(8,128)(2,1)S(1)}, bf16[128,256]{1,0:T(8,128)(2,1)S(1)}, u32[]{:S(2)}, u32[]{:S(2)}) collective-permute-start(bf16[128,256]{1,0:T(8,128)(2,1)S(1)} %copy-done.3), channel_id=1, source_target_pairs={{0,8},{8,16},{16,24},{24,0},{1,9},{9,17},{17,25},{25,1},{2,10},{10... | collective-permute-start | bytes 196616 | tf_op jit(solution)/shard_map/ppermute | solution.py:196
  50.1 8.2 %collective-permute-start.3 = (bf16[16,128,256]{2,1,0:T(8,128)(2,1)S(1)}, bf16[16,128,256]{2,1,0:T(8,128)(2,1)S(1)}, u32[]{:S(2)}, u32[]{:S(2)}) collective-permute-start(bf16[16,128,256]{2,1,0:T(8,128)(2,1)S(1)} %get-tuple-element.10), channel_id=1, source_target_pairs={{0,1},{1,0},{2,3},{3,2},{4,5},{5,4},{6,7},{7,6},{8,9},{9,8},{10,11... | collective-permute-start | bytes 3145736 | tf_op jit(solution)/shard_map/ppermute | solution.py:167
  78.0 31.4 %copy-start.4 = (f32[256]{0:T(256)S(1)}, f32[256]{0:T(256)}, u32[]{:S(2)}) copy-start(f32[256]{0:T(256)} %param.10) | copy-start | bytes 3076
  78.0 31.3 %all-to-all-start.2 = ((bf16[4,4,128,256]{3,2,1,0:T(8,128)(2,1)}), bf16[4,4,128,256]{3,2,1,0:T(8,128)(2,1)S(1)}, u32[]{:S(2)}, u32[]{:S(2)}) async-start(bf16[4,4,128,256]{3,2,1,0:T(8,128)(2,1)} %broadcast_in_dim.13), calls=%async_computation.2 | async-start | bytes 2097152 | tf_op jit(solution)/shard_map/all_to_all | solution.py:171
  126.7 6.9 %collective-permute-start.4 = (bf16[4,528,256]{2,1,0:T(8,128)(2,1)S(1)}, bf16[4,528,256]{2,1,0:T(8,128)(2,1)S(1)}, u32[]{:S(2)}, u32[]{:S(2)}) collective-permute-start(bf16[4,528,256]{2,1,0:T(8,128)(2,1)S(1)} %all_to_all.31.own), channel_id=1, source_target_pairs={{0,1},{1,0},{2,3},{3,2},{4,5},{5,4},{6,7},{7,6},{8,9},{9,8},{10,11... | collective-permute-start | bytes 3244040 | tf_op jit(solution)/shard_map/ppermute | solution.py:167
  138.0 43.7 %all-to-all-start.4 = ((bf16[16,144,256]{2,1,0:T(8,128)(2,1)}), bf16[16,144,256]{2,1,0:T(8,128)(2,1)S(1)}, u32[]{:S(2)}, u32[]{:S(2)}) async-start(bf16[16,144,256]{2,1,0:T(8,128)(2,1)} %backward_tiles.1), calls=%async_computation.4 | async-start | bytes 2359296 | tf_op jit(solution)/shard_map/all_to_all | solution.py:171
  182.7 16.4 %all-to-all-start.5 = ((f32[32,8,256]{2,1,0:T(8,128)}), f32[32,8,256]{2,1,0:T(8,128)S(1)}, u32[]{:S(2)}, u32[]{:S(2)}) async-start(f32[32,8,256]{2,1,0:T(8,128)} %broadcast_in_dim.16), calls=%async_computation.5 | async-start | bytes 524288 | tf_op jit(solution)/shard_map/all_to_all | solution.py:171

commit v7 on v4

--- a/solution.py
+++ b/solution.py
@@ -45,8 +45,12 @@
         lax.fori_loop(0, (left + GROUP - 1) // GROUP, one, 0)
 
 
-def forward_kernel(rows, cols, live_ref, core_ref, values_hbm, src, kept, sent, values, acc, sems):
-    live, core = live_ref[0], core_ref[0]
+def pair_slot(t, half):
+    return (t & 7) * 2 + (t // 8 ^ half)
+
+
+def forward_kernel(rows, cols, live_ref, place, values_hbm, src, kept, sent, values, acc, sems):
+    live, core, yh = live_ref[0], place[0], place[1]
     copies = start_values(values_hbm, values, sems)
     half = kept.shape[0]
     acc[...] = jnp.zeros_like(acc)
@@ -58,15 +62,15 @@
         for u in range(GROUP):
             s = first + u
             dest = jnp.where(s < live, slot(rows[s]), 2 * half)
-            acc[dest] += jnp.dot(values[s], src[cols[s]], preferred_element_type=jnp.float32)
+            acc[dest] += jnp.dot(values[s], src[pair_slot(cols[s], yh)], preferred_element_type=jnp.float32)
 
     walk(copies, live, step)
     sent[...] = acc[half : 2 * half].astype(sent.dtype)
     kept[...] = acc[:half].astype(kept.dtype)
 
 
-def backward_kernel(rows, cols, live_ref, core_ref, values_hbm, own, other, out, values, src, acc, sems, src_sems):
-    live, core = live_ref[0], core_ref[0]
+def backward_kernel(rows, cols, live_ref, place, values_hbm, own, other, out, values, src, acc, sems, src_sems):
+    live, core, yh = live_ref[0], place[0], place[1]
     fetch = [
         pltpu.make_async_copy(own, src.at[pl.ds(core * 4, 4)], src_sems.at[0]),
         pltpu.make_async_copy(other, src.at[pl.ds((1 - core) * 4, 4)], src_sems.at[1]),
@@ -74,23 +78,12 @@
     for copy in fetch:
         copy.start()
     copies = start_values(values_hbm, values, sems)
-    tiles, side = out.shape[0], values.shape[1]
+    side = values.shape[1]
+    tiles = acc.shape[0] - 1
     gathered = 4 * side
     acc[...] = jnp.zeros_like(acc)
     for copy in fetch:
         copy.wait()
-
-    def step(first):
-        for u in range(GROUP):
-            s = first + u
-            dest = jnp.where(s < live, cols[s], tiles)
-            t = rows[s]
-            block = src[lax.rem(t, 2) * 4 + ((t // 2) & 3), pl.ds(pl.multiple_of(t // 8 * side, side), side), :]
-            acc[dest] += lax.dot_general(
-                values[s], block, (((0,), (0,)), ((), ())), preferred_element_type=jnp.float32
-            )
-
-    walk(copies, live, step)
 
     terms = jnp.zeros((16, out.shape[-1]), jnp.float32)
     bias = jnp.zeros((8, out.shape[-1]), jnp.float32)
@@ -105,9 +98,23 @@
     tail = jnp.where(row == 0, high, jnp.where(row == 1, bias - high, 0.0))
     mine = jnp.where(core == 0, terms[:8], terms[8:])
     tail = jnp.concatenate([mine, tail]).astype(out.dtype)
-    for t in range(tiles):
-        out[t, :side, :] = acc[t].astype(out.dtype)
-        out[t, side:, :] = tail
+    for z in range(out.shape[0]):
+        out[z, 2 * side :, :] = tail
+
+    def step(first):
+        for u in range(GROUP):
+            s = first + u
+            dest = jnp.where(s < live, pair_slot(cols[s], yh), tiles)
+            t = rows[s]
+            block = src[lax.rem(t, 2) * 4 + ((t // 2) & 3), pl.ds(pl.multiple_of(t // 8 * side, side), side), :]
+            acc[dest] += lax.dot_general(
+                values[s], block, (((0,), (0,)), ((), ())), preferred_element_type=jnp.float32
+            )
+
+    walk(copies, live, step)
+    for z in range(out.shape[0]):
+        out[z, :side, :] = acc[2 * z].astype(out.dtype)
+        out[z, side : 2 * side, :] = acc[2 * z + 1].astype(out.dtype)
 
 
 SMEM = pl.BlockSpec(memory_space=pltpu.SMEM)
@@ -122,7 +129,7 @@
     )
 
 
-def spread_forward(rows, cols, live, core, values, src, row_tiles):
+def spread_forward(rows, cols, live, place, values, src, row_tiles):
     slots, side, _ = values.shape
     width = src.shape[-1]
     half = jax.ShapeDtypeStruct((row_tiles // 2, side, width), jnp.bfloat16)
@@ -139,15 +146,15 @@
         compiler_params=pltpu.CompilerParams(vmem_limit_bytes=40 << 20),
         cost_estimate=cost(slots, side, width),
         name="forward_tiles",
-    )(rows, cols, live, core, values, src)
-
-
-def spread_backward(rows, cols, live, core, values, own, other, col_tiles):
+    )(rows, cols, live, place, values, src)
+
+
+def spread_backward(rows, cols, live, place, values, own, other, col_tiles):
     slots, side, _ = values.shape
     width = own.shape[-1]
     return pl.pallas_call(
         backward_kernel,
-        out_shape=jax.ShapeDtypeStruct((col_tiles, side + 16, width), jnp.bfloat16),
+        out_shape=jax.ShapeDtypeStruct((col_tiles // 2, 2 * side + 16, width), jnp.bfloat16),
         in_specs=[SMEM, SMEM, SMEM, SMEM, HBM, ANY, ANY],
         out_specs=VMEM,
         scratch_shapes=[
@@ -160,7 +167,7 @@
         compiler_params=pltpu.CompilerParams(vmem_limit_bytes=40 << 20),
         cost_estimate=cost(slots, side, width),
         name="backward_tiles",
-    )(rows, cols, live, core, values, own, other)
+    )(rows, cols, live, place, values, own, other)
 
 
 def swap(x):
@@ -183,6 +190,11 @@
 
 def add_up(x):
     return jnp.sum(x.astype(jnp.float32), axis=0)
+
+
+def in_two(x):
+    high = lax.reduce_precision(x, 8, 7)
+    return jnp.concatenate([high, lax.reduce_precision(x - high, 8, 7)])
 
 
 def body(features, weight, bias, grad_out, tile_rows, tile_cols, tile_counts, tile_values):
@@ -191,10 +203,11 @@
     side, width = features.shape
     row_tiles, col_tiles = 32, 16
     bf16 = jnp.bfloat16
-    core = lax.axis_index("core").astype(jnp.int32).reshape(1)
-
-    block = gather(features, ROW, col_tiles)
-    kept, sent = spread_forward(rows, cols, live, core, values, block, row_tiles)
+    place = jnp.stack([lax.axis_index(axis) for axis in ("core", "yh")]).astype(jnp.int32)
+
+    pair = jnp.stack([features, lax.ppermute(features, "yh", [(0, 1), (1, 0)])])
+    block = gather(pair, "z", 8).reshape(col_tiles, side, width)
+    kept, sent = spread_forward(rows, cols, live, place, values, block, row_tiles)
     by_core = (kept.astype(jnp.float32) + swap(sent).astype(jnp.float32)).astype(bf16)
     by_x = add_up(exchange(by_core.reshape(4, 4, side, width), "x")).astype(bf16)
     mean = add_up(exchange(by_x, "yl"))
@@ -213,12 +226,17 @@
     along_y = gather_and_scatter(grad_pre, terms, "yl")
     terms = add_up(along_y[:, side:]).astype(bf16).reshape(4, width // 16, width)
     own = gather_and_scatter(along_y[:, :side].reshape(4 * side, width), terms, "x")
-    back = spread_backward(rows, cols, live, core, values, own, swap(own), col_tiles)
-
-    reduced = add_up(exchange(back, ROW))
-    grad_mixed = reduced[:side].astype(bf16)
-    grad_weight = gather(reduced[side : side + 8], COL, 32).reshape(width, width)
-    grad_bias = reduced[side + 8] + reduced[side + 9]
+    back = spread_backward(rows, cols, live, place, values, own, swap(own), col_tiles)
+
+    reduced = add_up(exchange(back, "z"))
+    mine = in_two(reduced[2 * side :])
+    sent = jnp.concatenate([reduced[side : 2 * side].astype(bf16), mine.astype(bf16)])
+    sent = lax.ppermute(sent, "yh", [(0, 1), (1, 0)]).astype(jnp.float32)
+    grad_mixed = (reduced[:side] + sent[:side]).astype(bf16)
+    theirs = sent[side:]
+    total = (mine[:16] + mine[16:]) + (theirs[:16] + theirs[16:])
+    grad_weight = gather(total[:8], COL, 32).reshape(width, width)
+    grad_bias = total[8] + total[9]
     grad_features = lax.dot_general(
         grad_mixed, weight, (((1,), (1,)), ((), ())), preferred_element_type=jnp.float32
     ).astype(bf16)

time: 192 us -> 198 us (1.031)
  waiting for transfers between devices: 37 us -> 52 us
  starting transfers between devices: 40.2 us -> 33.9 us
  blocking collectives: 99.4 us -> 94.6 us
    all_to_all x2, starting transfers between devices: 28 us -> 14.9 us  [exchange(): return lax.all_to_all(x, axes, 0, 0, tiled=True)]
    ppermute x0 -> x2, waiting for transfers between devices: none -> 11 us  [the longest x1 9.08 us: body(): sent = lax.ppermute(sent, 'yh', [(0, 1), (1, 0)]).astype(jnp.float32)]
    ppermute x0 -> x2, starting transfers between devices: none -> 10.3 us  [the longest x1 8.41 us: body(): pair = jnp.stack([features, lax.ppermute(features, 'yh', [(0, 1), (1, 0)])])]
    all_to_all x5, blocking collectives: 99.4 us -> 94.6 us  [exchange(): return lax.all_to_all(x, axes, 0, 0, tiled=True)]
    all_to_all x2, waiting for transfers between devices: 32.5 us -> 36.4 us  [exchange(): return lax.all_to_all(x, axes, 0, 0, tiled=True)]
    ppermute x2, starting transfers between devices: 12.2 us -> 8.69 us  [swap(): return lax.ppermute(x, 'core', [(0, 1), (1, 0)])]
  transfers between devices with their start and end apart: 4 -> 6, of which waited for: 4 -> 6; matrix products, arithmetic and copies ran while one was open for 1% -> 1% of each run, Pallas kernels for 0% -> 0%
where the time goes in v7:
time: 198 us; the launch traced here: 197 us
  blocking collectives  94.6 us (48%)
  waiting for transfers between devices  52 us (26%)
  starting transfers between devices  33.9 us (17%)
  Pallas kernels  8.05 us (4%)
  local copies, waits for them, and re-layouts  2.63 us (1%)
  other arithmetic  2.41 us (1%)
  matrix products  2.06 us (1%)
    all_to_all x5, blocking collectives, exchange(): return lax.all_to_all(x, axes, 0, 0, tiled=True)  94.6 us
    all_to_all x2, waiting for transfers between devices, exchange(): return lax.all_to_all(x, axes, 0, 0, tiled=True)  36.4 us
    all_to_all x2, starting transfers between devices, exchange(): return lax.all_to_all(x, axes, 0, 0, tiled=True)  14.9 us
    ppermute x1, waiting for transfers between devices, body(): sent = lax.ppermute(sent, 'yh', [(0, 1), (1, 0)]).astype(jnp.float32)  9.08 us
    ppermute x2, starting transfers between devices, swap(): return lax.ppermute(x, 'core', [(0, 1), (1, 0)])  8.69 us
    ppermute x1, starting transfers between devices, body(): pair = jnp.stack([features, lax.ppermute(features, 'yh', [(0, 1), (1, 0)])])  8.41 us
    ppermute x2, waiting for transfers between devices, swap(): return lax.ppermute(x, 'core', [(0, 1), (1, 0)])  4.58 us
    pallas_call x1, Pallas kernels, spread_backward(): pl.pallas_call(backward_kernel, out_shape=jax.ShapeDtypeStruct((col_tiles...  4.14 us
  transfers between devices with their start and end apart: 6, of which 6 were waited for; matrix products, arithmetic and copies ran while one was open for 1% of the time, Pallas kernels for 0%

profile of v7, /device:TPU:1, one launch (start us, length us, event | category | flops | bytes accessed | tf_op | source)
XLA Modules:
  0.0 197.2 jit_solution(11350398143028661789)
XLA Ops:
  0.6 8.4 %collective-permute-start = (bf16[128,256]{1,0:T(8,128)(2,1)}, bf16[128,256]{1,0:T(8,128)(2,1)S(1)}, u32[]{:S(2)}, u32[]{:S(2)}) collective-permute-start(bf16[128,256]{1,0:T(8,128)(2,1)} %param.8), channel_id=1, source_target_pairs={{0,256},{256,0},{1,257},{257,1},{2,258},{258,2},{3,259},{259,3},{4... | collective-permute-start | bytes 196616 | tf_op jit(solution)/shard_map/ppermute | solution.py:208
  9.1 1.9 collective-permute-done
  11.0 0.9 pad_maximum_fusion.2
  11.8 1.1 broadcast_in_dim.14
  12.9 10.2 %all-to-all-start = ((bf16[8,2,128,256]{3,2,1,0:T(8,128)(2,1)}), bf16[8,2,128,256]{3,2,1,0:T(8,128)(2,1)S(1)}, u32[]{:S(2)}, u32[]{:S(2)}) async-start(bf16[8,2,128,256]{3,2,1,0:T(8,128)(2,1)} %broadcast_in_dim.14), calls=%async_computation | async-start | bytes 2097152 | tf_op jit(solution)/shard_map/all_to_all | solution.py:178
  23.7 0.1 pad_add_fusion.place
  23.8 26.6 %all-to-all-done = bf16[8,2,128,256]{3,2,1,0:T(8,128)(2,1)S(1)} async-done(((bf16[8,2,128,256]{3,2,1,0:T(8,128)(2,1)}), bf16[8,2,128,256]{3,2,1,0:T(8,128)(2,1)S(1)}, u32[]{:S(2)}, u32[]{:S(2)}) %all-to-all-start) | async-done | bytes 1048608 | tf_op jit(solution)/shard_map/all_to_all | solution.py:178
  50.4 3.9 %forward_tiles.1 = (bf16[16,128,256]{2,1,0:T(8,128)(2,1)S(1)}, bf16[16,128,256]{2,1,0:T(8,128)(2,1)S(1)}) custom-call(s32[128]{0:T(128)S(1)} %bitcast.23, s32[128]{0:T(128)S(1)} %bitcast.25, s32[1]{0:T(128)} %bitcast.20.live_ref, s32[2]{0:T(128)S(1)} %pad_add_fusion.place, bf16[128,128,128]{2,1,0:T(8,128)(2,1)} %bitcast.27, bf16[16,128,256]{2,1,0:T(8,128)(2,1)S(1)} %bitcast.22), custom_call_target="tpu_custom_call" | custom-call | flops 1073741824 | bytes 4194304 | tf_op jit(solution)/shard_map/forward_tiles/pallas_call | solution.py:136
  54.3 3.3 %collective-permute-start.1 = (bf16[16,128,256]{2,1,0:T(8,128)(2,1)S(1)}, bf16[16,128,256]{2,1,0:T(8,128)(2,1)S(1)}, u32[]{:S(2)}, u32[]{:S(2)}) collective-permute-start(bf16[16,128,256]{2,1,0:T(8,128)(2,1)S(1)} %get-tuple-element.7), channel_id=1, source_target_pairs={{0,1},{1,0},{2,3},{3,2},{4,5},{5,4},{6,7},{7,6},{8,9},{9,8},{10,11... | collective-permute-start | bytes 3145736 | tf_op jit(solution)/shard_map/ppermute | solution.py:174
  57.7 2.3 %collective-permute-done.1 = bf16[16,128,256]{2,1,0:T(8,128)(2,1)S(1)} collective-permute-done((bf16[16,128,256]{2,1,0:T(8,128)(2,1)S(1)}, bf16[16,128,256]{2,1,0:T(8,128)(2,1)S(1)}, u32[]{:S(2)}, u32[]{:S(2)}) %collective-permute-start.1) | collective-permute-done | bytes 1048608 | tf_op jit(solution)/shard_map/ppermute | solution.py:174
  59.9 0.4 add_convert_fusion
  60.3 20.7 %all_to_all.35 = bf16[4,4,128,256]{3,2,1,0:T(8,128)(2,1)S(1)} all-to-all(bf16[4,4,128,256]{3,2,1,0:T(8,128)(2,1)S(1)} %bitcast.29), channel_id=1, replica_groups=mesh['yh'=2,'z'=8,'yl'=4,'x'=4,'core'=2] {'x'}, dimensions={0} | all-to-all | bytes 2097152 | tf_op jit(solution)/shard_map/all_to_all | solution.py:178
  81.0 0.2 reduce_sum.42
  81.2 10.5 %all_to_all.36 = bf16[4,128,256]{2,1,0:T(8,128)(2,1)S(1)} all-to-all(bf16[4,128,256]{2,1,0:T(8,128)(2,1)S(1)} %reduce_sum.42), channel_id=1, replica_groups=mesh['yh'=2,'z'=8,'yl'=4,'x'=4,'core'=2] {'yl'}, dimensions={0} | all-to-all | bytes 524288 | tf_op jit(solution)/shard_map/all_to_all | solution.py:178
  91.7 0.9 fusion.2
  92.6 0.3 convolution_convert_fusion
  93.0 15.3 %all_to_all.37 = bf16[4,192,256]{2,1,0:T(8,128)(2,1)S(1)} all-to-all(bf16[4,192,256]{2,1,0:T(8,128)(2,1)S(1)} %pad_maximum_fusion.1), channel_id=1, replica_groups=mesh['yh'=2,'z'=8,'yl'=4,'x'=4,'core'=2] {'yl'}, dimensions={0} | all-to-all | bytes 786432 | tf_op jit(solution)/shard_map/all_to_all | solution.py:178
  108.4 0.1 pad_maximum_fusion
  108.5 15.3 %all_to_all.38.own = bf16[4,528,256]{2,1,0:T(8,128)(2,1)S(1)} all-to-all(bf16[4,528,256]{2,1,0:T(8,128)(2,1)S(1)} %pad_maximum_fusion), channel_id=1, replica_groups=mesh['yh'=2,'z'=8,'yl'=4,'x'=4,'core'=2] {'x'}, dimensions={0} | all-to-all | bytes 2162688 | tf_op jit(solution)/shard_map/all_to_all | solution.py:178
  123.9 5.4 %collective-permute-start.2 = (bf16[4,528,256]{2,1,0:T(8,128)(2,1)S(1)}, bf16[4,528,256]{2,1,0:T(8,128)(2,1)S(1)}, u32[]{:S(2)}, u32[]{:S(2)}) collective-permute-start(bf16[4,528,256]{2,1,0:T(8,128)(2,1)S(1)} %all_to_all.38.own), channel_id=1, source_target_pairs={{0,1},{1,0},{2,3},{3,2},{4,5},{5,4},{6,7},{7,6},{8,9},{9,8},{10,11... | collective-permute-start | bytes 3244040 | tf_op jit(solution)/shard_map/ppermute | solution.py:174
  129.2 2.3 %collective-permute-done.2.other = bf16[4,528,256]{2,1,0:T(8,128)(2,1)S(1)} collective-permute-done((bf16[4,528,256]{2,1,0:T(8,128)(2,1)S(1)}, bf16[4,528,256]{2,1,0:T(8,128)(2,1)S(1)}, u32[]{:S(2)}, u32[]{:S(2)}) %collective-permute-start.2) | collective-permute-done | bytes 1081376 | tf_op jit(solution)/shard_map/ppermute | solution.py:174
  131.5 4.1 %backward_tiles.1 = bf16[8,272,256]{2,1,0:T(8,128)(2,1)S(1)} custom-call(s32[128]{0:T(128)S(1)} %bitcast.24, s32[128]{0:T(128)S(1)} %bitcast.26, s32[1]{0:T(128)} %bitcast.21.live_ref, s32[2]{0:T(128)S(1)} %pad_add_fusion.place, bf16[128,128,128]{2,1,0:T(8,128)(2,1)} %bitcast.28, bf16[4,528,256]{2,1,0:T(8,128)(2,1)S(1)} %all_to_all.38.own, ...), custom_call_target="tpu_custom_call" | custom-call | flops 1073741824 | bytes 4194304 | tf_op jit(solution)/shard_map/backward_tiles/pallas_call | solution.py:155
  135.7 32.9 %all_to_all.39 = bf16[8,272,256]{2,1,0:T(8,128)(2,1)S(1)} all-to-all(bf16[8,272,256]{2,1,0:T(8,128)(2,1)S(1)} %backward_tiles.1), channel_id=1, replica_groups=mesh['yh'=2,'z'=8,'yl'=4,'x'=4,'core'=2] {'z'}, dimensions={0} | all-to-all | bytes 2228224 | tf_op jit(solution)/shard_map/all_to_all | solution.py:178
  168.6 0.2 convert_reduce_fusion
  168.8 1.9 collective-permute-start.3
  170.7 9.1 %collective-permute-done.3 = bf16[160,256]{1,0:T(8,128)(2,1)S(1)} collective-permute-done((bf16[160,256]{1,0:T(8,128)(2,1)S(1)}, bf16[160,256]{1,0:T(8,128)(2,1)S(1)}, u32[]{:S(2)}, u32[]{:S(2)}) %collective-permute-start.3) | collective-permute-done | bytes 81952 | tf_op jit(solution)/shard_map/ppermute | solution.py:234
  179.8 0.7 broadcast_in_dim.35
  180.5 4.7 %all-to-all-start.6 = ((f32[32,8,256]{2,1,0:T(8,128)}), f32[32,8,256]{2,1,0:T(8,128)S(1)}, u32[]{:S(2)}, u32[]{:S(2)}) async-start(f32[32,8,256]{2,1,0:T(8,128)} %broadcast_in_dim.35), calls=%async_computation.6 | async-start | bytes 524288 | tf_op jit(solution)/shard_map/all_to_all | solution.py:178
  185.2 0.6 slice_add_fusion.2
  185.8 0.8 convolution_convert_fusion.1
  186.6 9.8 %all-to-all-done.6 = f32[32,8,256]{2,1,0:T(8,128)S(1)} async-done(((f32[32,8,256]{2,1,0:T(8,128)}), f32[32,8,256]{2,1,0:T(8,128)S(1)}, u32[]{:S(2)}, u32[]{:S(2)}) %all-to-all-start.6) | async-done | bytes 262176 | tf_op jit(solution)/shard_map/all_to_all | solution.py:178
  196.5 0.7 copy.14
  (22 shorter events, 0.3 us)
Async XLA Ops:
  0.6 91.1 %copy-start = (bf16[256,256]{1,0:T(8,128)(2,1)S(1)}, bf16[256,256]{1,0:T(8,128)(2,1)}, u32[]{:S(2)}) copy-start(bf16[256,256]{1,0:T(8,128)(2,1)} %param.9) | copy-start | bytes 393220
  0.6 10.3 %collective-permute-start = (bf16[128,256]{1,0:T(8,128)(2,1)}, bf16[128,256]{1,0:T(8,128)(2,1)S(1)}, u32[]{:S(2)}, u32[]{:S(2)}) collective-permute-start(bf16[128,256]{1,0:T(8,128)(2,1)} %param.8), channel_id=1, source_target_pairs={{0,256},{256,0},{1,257},{257,1},{2,258},{258,2},{3,259},{259,3},{4... | collective-permute-start | bytes 196616 | tf_op jit(solution)/shard_map/ppermute | solution.py:208
  12.9 37.5 %copy-start.1 = (s32[1,1,128]{2,1,0:T(1,128)S(1)}, s32[1,1,128]{2,1,0:T(1,128)}, u32[]{:S(2)}) copy-start(s32[1,1,128]{2,1,0:T(1,128)} %param.12) | copy-start | bytes 1540
  12.9 37.5 %copy-start.2 = (s32[1,1,128]{2,1,0:T(1,128)S(1)}, s32[1,1,128]{2,1,0:T(1,128)}, u32[]{:S(2)}) copy-start(s32[1,1,128]{2,1,0:T(1,128)} %param.13) | copy-start | bytes 1540
  12.9 37.5 %all-to-all-start = ((bf16[8,2,128,256]{3,2,1,0:T(8,128)(2,1)}), bf16[8,2,128,256]{3,2,1,0:T(8,128)(2,1)S(1)}, u32[]{:S(2)}, u32[]{:S(2)}) async-start(bf16[8,2,128,256]{3,2,1,0:T(8,128)(2,1)} %broadcast_in_dim.14), calls=%async_computation | async-start | bytes 2097152 | tf_op jit(solution)/shard_map/all_to_all | solution.py:178
  54.3 5.6 %collective-permute-start.1 = (bf16[16,128,256]{2,1,0:T(8,128)(2,1)S(1)}, bf16[16,128,256]{2,1,0:T(8,128)(2,1)S(1)}, u32[]{:S(2)}, u32[]{:S(2)}) collective-permute-start(bf16[16,128,256]{2,1,0:T(8,128)(2,1)S(1)} %get-tuple-element.7), channel_id=1, source_target_pairs={{0,1},{1,0},{2,3},{3,2},{4,5},{5,4},{6,7},{7,6},{8,9},{9,8},{10,11... | collective-permute-start | bytes 3145736 | tf_op jit(solution)/shard_map/ppermute | solution.py:174
  81.0 10.7 %copy-start.3 = (bf16[128,256]{1,0:T(8,128)(2,1)S(1)}, bf16[128,256]{1,0:T(8,128)(2,1)}, u32[]{:S(2)}) copy-start(bf16[128,256]{1,0:T(8,128)(2,1)} %param.11) | copy-start | bytes 196612
  81.0 10.7 %copy-start.4 = (f32[256]{0:T(256)S(1)}, f32[256]{0:T(256)}, u32[]{:S(2)}) copy-start(f32[256]{0:T(256)} %param.10) | copy-start | bytes 3076
  123.9 7.7 %collective-permute-start.2 = (bf16[4,528,256]{2,1,0:T(8,128)(2,1)S(1)}, bf16[4,528,256]{2,1,0:T(8,128)(2,1)S(1)}, u32[]{:S(2)}, u32[]{:S(2)}) collective-permute-start(bf16[4,528,256]{2,1,0:T(8,128)(2,1)S(1)} %all_to_all.38.own), channel_id=1, source_target_pairs={{0,1},{1,0},{2,3},{3,2},{4,5},{5,4},{6,7},{7,6},{8,9},{9,8},{10,11... | collective-permute-start | bytes 3244040 | tf_op jit(solution)/shard_map/ppermute | solution.py:174
  168.8 11.0 %collective-permute-start.3 = (bf16[160,256]{1,0:T(8,128)(2,1)S(1)}, bf16[160,256]{1,0:T(8,128)(2,1)S(1)}, u32[]{:S(2)}, u32[]{:S(2)}) collective-permute-start(bf16[160,256]{1,0:T(8,128)(2,1)S(1)} %pad_maximum_fusion.3), channel_id=1, source_target_pairs={{0,256},{256,0},{1,257},{257,1},{2,258},{258,2},{3,259},{259,3},{4... | collective-permute-start | bytes 245768 | tf_op jit(solution)/shard_map/ppermute | solution.py:234
  180.5 15.9 %all-to-all-start.6 = ((f32[32,8,256]{2,1,0:T(8,128)}), f32[32,8,256]{2,1,0:T(8,128)S(1)}, u32[]{:S(2)}, u32[]{:S(2)}) async-start(f32[32,8,256]{2,1,0:T(8,128)} %broadcast_in_dim.35), calls=%async_computation.6 | async-start | bytes 524288 | tf_op jit(solution)/shard_map/all_to_all | solution.py:178

commit v8 on v5

--- a/solution.py
+++ b/solution.py
@@ -65,10 +65,10 @@
     kept[...] = acc[:half].astype(kept.dtype)
 
 
-def backward_kernel(rows, cols, live_ref, place, values_hbm, *refs):
+def backward_kernel(rows, cols, live_ref, place, weight_rows, values_hbm, *refs):
     blocks, (out, values, src, acc, sems, src_sems) = refs[:8], refs[8:]
     live = live_ref[0]
-    core, x = place[0], place[1]
+    core, x, y = place[0], place[1], place[2]
     depth = blocks[0].shape[0]
     fetch = [
         pltpu.make_async_copy(block, src.at[pl.ds(k * depth, depth)], src_sems.at[k]) for k, block in enumerate(blocks)
@@ -76,13 +76,27 @@
     for copy in fetch:
         copy.start()
     copies = start_values(values_hbm, values, sems)
-    tiles = out.shape[0]
+    tiles, width = out.shape[0], out.shape[-1]
+    side = values.shape[1]
     acc[...] = jnp.zeros_like(acc)
     for copy in fetch:
         copy.wait()
 
     def slot(t):
-        return (lax.rem(t, 2) ^ core) * 16 + ((x - t // 2) & 3) * 4 + t // 8
+        return (lax.rem(t, 2) ^ core) * 16 + ((x - t // 2) & 3) * 4 + ((y - t // 8) & 3)
+
+    bias = jnp.zeros((8, width), jnp.float32)
+    for t in range(2 * tiles):
+        block = src[slot(jnp.int32(t))].astype(jnp.float32)
+        bias += jnp.sum(block.reshape(side // 8, 8, width), axis=0)
+    bias = jnp.sum(bias, axis=0, keepdims=True)
+    high = bias.astype(jnp.bfloat16).astype(jnp.float32)
+    row = lax.broadcasted_iota(jnp.int32, (8, width), 0)
+    tail = jnp.where(row == 0, high, jnp.where(row == 1, bias - high, 0.0)).astype(out.dtype)
+    piece = weight_rows[...].astype(out.dtype)
+    for t in range(tiles):
+        out[t, side : side + 16, :] = piece
+        out[t, side + 16 :, :] = tail
 
     def step(first):
         for u in range(GROUP):
@@ -93,13 +107,8 @@
             )
 
     walk(copies, live, step)
-    out[...] = acc[:tiles].astype(out.dtype)
-
-
-def place_kernel(place, a, b, c, d, out):
-    per = a.shape[0]
-    for k, piece in enumerate((a, b, c, d)):
-        out[pl.ds(((place[2] - k) & 3) * per, per), :] = piece[...]
+    for t in range(tiles):
+        out[t, :side, :] = acc[t].astype(out.dtype)
 
 
 SMEM = pl.BlockSpec(memory_space=pltpu.SMEM)
@@ -134,13 +143,13 @@
     )(rows, cols, live, place, values, src)
 
 
-def spread_backward(rows, cols, live, place, values, blocks, col_tiles):
+def spread_backward(rows, cols, live, place, weight_rows, values, blocks, col_tiles):
     slots, side, _ = values.shape
     depth, _, width = blocks[0].shape
     return pl.pallas_call(
         backward_kernel,
-        out_shape=jax.ShapeDtypeStruct((col_tiles, side, width), jnp.bfloat16),
-        in_specs=[SMEM, SMEM, SMEM, SMEM, HBM] + [ANY] * len(blocks),
+        out_shape=jax.ShapeDtypeStruct((col_tiles, side + 24, width), jnp.bfloat16),
+        in_specs=[SMEM, SMEM, SMEM, SMEM, VMEM, HBM] + [ANY] * len(blocks),
         out_specs=VMEM,
         scratch_shapes=[
             pltpu.VMEM((slots, side, side), jnp.bfloat16),
@@ -152,18 +161,7 @@
         compiler_params=pltpu.CompilerParams(vmem_limit_bytes=40 << 20),
         cost_estimate=cost(slots, side, width),
         name="backward_tiles",
-    )(rows, cols, live, place, values, *blocks)
-
-
-def put_in_place(place, pieces):
-    per, width = pieces[0].shape
-    return pl.pallas_call(
-        place_kernel,
-        out_shape=jax.ShapeDtypeStruct((len(pieces) * per, width), pieces[0].dtype),
-        in_specs=[SMEM] + [VMEM] * len(pieces),
-        out_specs=VMEM,
-        name="place_pieces",
-    )(place, *pieces)
+    )(rows, cols, live, place, weight_rows, values, *blocks)
 
 
 def around(x, axis, size):
@@ -183,19 +181,8 @@
     return exchange(copies, axes)
 
 
-def gather_and_scatter(x, pieces, axes):
-    copies = jnp.broadcast_to(x[None], pieces.shape[:1] + x.shape)
-    return exchange(lax.optimization_barrier(jnp.concatenate([copies, pieces], axis=1)), axes)
-
-
 def add_up(x):
     return jnp.sum(x.astype(jnp.float32), axis=0)
-
-
-def two_rows(x):
-    high = x.astype(jnp.bfloat16).astype(jnp.float32)
-    row = lax.broadcasted_iota(jnp.int32, (8, x.shape[-1]), 0)
-    return jnp.where(row == 0, high, jnp.where(row == 1, x - high, 0.0)).astype(jnp.bfloat16)
 
 
 def body(features, weight, bias, grad_out, tile_rows, tile_cols, tile_counts, tile_values):
@@ -222,30 +209,18 @@
     weight_term = lax.dot_general(
         mean, grad32, (((0,), (0,)), ((), ())), precision=lax.Precision.HIGHEST, preferred_element_type=jnp.float32
     )
-    bias_term = jnp.sum(grad32, axis=0, keepdims=True)
-    terms = weight_term.astype(bf16).reshape(4, width // 4, width)
-    tail = jnp.broadcast_to(two_rows(bias_term)[None], (4, 8, width))
-    along_y = gather_and_scatter(grad_pre, jnp.concatenate([terms, tail], axis=1), "yl")
-
-    own = around(along_y[:, :side], "x", 4)
+    along_y = jnp.stack(around(grad_pre, "yl", 4))
+    own = around(along_y, "x", 4)
     blocks = own + [swap(block) for block in own]
-    terms = add_up(along_y[:, side:])
-    rows_of_weight = width // 4
-    terms = jnp.concatenate(
-        [
-            terms[:rows_of_weight].astype(bf16),
-            two_rows(terms[rows_of_weight : rows_of_weight + 1] + terms[rows_of_weight + 1 : rows_of_weight + 2]),
-        ]
-    )
-    terms = add_up(gather(terms, ROW, 16))
-    back = spread_backward(rows, cols, live, place, values, blocks, col_tiles)
-    grad_mixed = add_up(exchange(back, ROW)).astype(bf16)
-
-    terms = terms + swap(terms)
-    for bit in (1, 2):
-        terms = terms + lax.ppermute(terms, "x", [(i, i ^ bit) for i in range(4)])
-    grad_bias = terms[rows_of_weight] + terms[rows_of_weight + 1]
-    grad_weight = put_in_place(place, around(terms[:rows_of_weight], "yl", 4))
+
+    pieces = exchange(weight_term.astype(bf16).reshape(16, width // 16, width), ROW)
+    pieces, _ = lax.optimization_barrier((pieces, own[3]))
+    weight_rows = add_up(gather(add_up(pieces).astype(bf16), COL, 32))
+    back = exchange(spread_backward(rows, cols, live, place, weight_rows, values, blocks, col_tiles), ROW)
+    grad_mixed = add_up(back[:, :side]).astype(bf16)
+    grad_weight = back[:, side : side + 16].reshape(width, width).astype(jnp.float32)
+    bias_rows = add_up(back[:, side + 16 :])
+    grad_bias = bias_rows[0] + bias_rows[1]
     grad_features = lax.dot_general(
         grad_mixed, weight, (((1,), (1,)), ((), ())), preferred_element_type=jnp.float32
     ).astype(bf16)

time: 194 us -> 206 us (1.062)
  the two profiles are of different devices: /device:TPU:1 before, /device:TPU:16 now
where the time goes in v8:
time: 206 us; the launch traced here: 205 us
  blocking collectives  92.4 us (45%)
  starting transfers between devices  50.9 us (25%)
  waiting for transfers between devices  46.3 us (22%)
  Pallas kernels  6.78 us (3%)
  local copies, waits for them, and re-layouts  2.7 us (1%)
  other arithmetic  2.25 us (1%)
  matrix products  2.06 us (1%)
    all_to_all x4, blocking collectives, exchange(): return lax.all_to_all(x, axes, 0, 0, tiled=True)  92.4 us
    all_to_all x2, waiting for transfers between devices, exchange(): return lax.all_to_all(x, axes, 0, 0, tiled=True)  31.4 us
    ppermute x6, starting transfers between devices, around(): lax.ppermute(x, axis, [(i, (i + k) % size) for i in range(size)])  21 us
    all_to_all x2, starting transfers between devices, exchange(): return lax.all_to_all(x, axes, 0, 0, tiled=True)  19.8 us
    ppermute x6, waiting for transfers between devices, around(): lax.ppermute(x, axis, [(i, (i + k) % size) for i in range(size)])  11.2 us
    ppermute x5, starting transfers between devices, swap(): return lax.ppermute(x, 'core', [(0, 1), (1, 0)])  10.1 us
  transfers between devices with their start and end apart: 13, of which 7 were waited for; matrix products, arithmetic and copies ran while one was open for 0% of the time, Pallas kernels for 0%

profile of v8, /device:TPU:16, one launch (start us, length us, event | category | flops | bytes accessed | tf_op | source)
XLA Modules:
  0.0 204.9 jit_solution(13891139172233189266)
XLA Ops:
  0.7 1.9 broadcast_in_dim.8
  2.6 13.9 %all-to-all-start = ((bf16[16,128,256]{2,1,0:T(8,128)(2,1)}), bf16[16,128,256]{2,1,0:T(8,128)(2,1)S(1)}, u32[]{:S(2)}, u32[]{:S(2)}) async-start(bf16[16,128,256]{2,1,0:T(8,128)(2,1)} %broadcast_in_dim.8), calls=%async_computation | async-start | bytes 2097152 | tf_op jit(solution)/shard_map/all_to_all | solution.py:176
  17.2 31.4 %all-to-all-done.src = bf16[16,128,256]{2,1,0:T(8,128)(2,1)S(1)} async-done(((bf16[16,128,256]{2,1,0:T(8,128)(2,1)}), bf16[16,128,256]{2,1,0:T(8,128)(2,1)S(1)}, u32[]{:S(2)}, u32[]{:S(2)}) %all-to-all-start) | async-done | bytes 1048608 | tf_op jit(solution)/shard_map/all_to_all | solution.py:176
  48.6 3.3 %forward_tiles.1 = (bf16[16,128,256]{2,1,0:T(8,128)(2,1)S(1)}, bf16[16,128,256]{2,1,0:T(8,128)(2,1)S(1)}) custom-call(s32[128]{0:T(128)S(1)} %bitcast.25, s32[128]{0:T(128)S(1)} %bitcast.27, s32[1]{0:T(128)} %bitcast.23.live_ref, s32[3]{0:T(128)S(1)} %pad_add_fusion.core_ref.place, bf16[128,128,128]{2,1,0:T(8,128)(2,1)} %bitcast.29, ...), custom_call_target="tpu_custom_call" | custom-call | flops 1073741824 | bytes 4194304 | tf_op jit(solution)/shard_map/forward_tiles/pallas_call | solution.py:130
  51.9 1.9 collective-permute-start
  53.9 2.6 %collective-permute-done = bf16[16,128,256]{2,1,0:T(8,128)(2,1)S(1)} collective-permute-done((bf16[16,128,256]{2,1,0:T(8,128)(2,1)S(1)}, bf16[16,128,256]{2,1,0:T(8,128)(2,1)S(1)}, u32[]{:S(2)}, u32[]{:S(2)}) %collective-permute-start) | collective-permute-done | bytes 1048608 | tf_op jit(solution)/shard_map/ppermute | solution.py:172
  56.9 21.8 %all_to_all.30 = bf16[4,4,128,256]{3,2,1,0:T(8,128)(2,1)S(1)} all-to-all(bf16[4,4,128,256]{3,2,1,0:T(8,128)(2,1)S(1)} %bitcast.31), channel_id=1, replica_groups=mesh['yh'=2,'z'=8,'yl'=4,'x'=4,'core'=2] {'x'}, dimensions={0} | all-to-all | bytes 2097152 | tf_op jit(solution)/shard_map/all_to_all | solution.py:176
  78.9 9.0 %all_to_all.31 = bf16[4,128,256]{2,1,0:T(8,128)(2,1)S(1)} all-to-all(bf16[4,128,256]{2,1,0:T(8,128)(2,1)S(1)} %reduce_sum.63), channel_id=1, replica_groups=mesh['yh'=2,'z'=8,'yl'=4,'x'=4,'core'=2] {'yl'}, dimensions={0} | all-to-all | bytes 524288 | tf_op jit(solution)/shard_map/all_to_all | solution.py:176
  88.0 0.9 fusion.2
  88.9 3.7 %collective-permute-start.3 = (bf16[128,256]{1,0:T(8,128)(2,1)S(1)}, bf16[128,256]{1,0:T(8,128)(2,1)S(1)}, u32[]{:S(2)}, u32[]{:S(2)}) collective-permute-start(bf16[128,256]{1,0:T(8,128)(2,1)S(1)} %get-tuple-element.10), channel_id=1, source_target_pairs={{0,24},{8,0},{16,8},{24,16},{1,25},{9,1},{17,9},{25,17},{2,26},{10... | collective-permute-start | bytes 196616 | tf_op jit(solution)/shard_map/ppermute | solution.py:168
  92.6 4.3 %collective-permute-start.2 = (bf16[128,256]{1,0:T(8,128)(2,1)S(1)}, bf16[128,256]{1,0:T(8,128)(2,1)S(1)}, u32[]{:S(2)}, u32[]{:S(2)}) collective-permute-start(bf16[128,256]{1,0:T(8,128)(2,1)S(1)} %get-tuple-element.10), channel_id=1, source_target_pairs={{0,16},{8,24},{16,0},{24,8},{1,17},{9,25},{17,1},{25,9},{2,18},{10... | collective-permute-start | bytes 196616 | tf_op jit(solution)/shard_map/ppermute | solution.py:168
  96.9 2.6 %collective-permute-start.1 = (bf16[128,256]{1,0:T(8,128)(2,1)S(1)}, bf16[128,256]{1,0:T(8,128)(2,1)S(1)}, u32[]{:S(2)}, u32[]{:S(2)}) collective-permute-start(bf16[128,256]{1,0:T(8,128)(2,1)S(1)} %get-tuple-element.10), channel_id=1, source_target_pairs={{0,8},{8,16},{16,24},{24,0},{1,9},{9,17},{17,25},{25,1},{2,10},{10... | collective-permute-start | bytes 196616 | tf_op jit(solution)/shard_map/ppermute | solution.py:168
  99.5 0.6 collective-permute-done.2
  100.1 3.0 %collective-permute-done.1 = bf16[128,256]{1,0:T(8,128)(2,1)S(1)} collective-permute-done((bf16[128,256]{1,0:T(8,128)(2,1)S(1)}, bf16[128,256]{1,0:T(8,128)(2,1)S(1)}, u32[]{:S(2)}, u32[]{:S(2)}) %collective-permute-start.1) | collective-permute-done | bytes 65568 | tf_op jit(solution)/shard_map/ppermute | solution.py:168
  103.1 3.1 %collective-permute-start.4 = (bf16[4,128,256]{2,1,0:T(8,128)(2,1)S(1)}, bf16[4,128,256]{2,1,0:T(8,128)(2,1)S(1)}, u32[]{:S(2)}, u32[]{:S(2)}) collective-permute-start(bf16[4,128,256]{2,1,0:T(8,128)(2,1)S(1)} %pad_maximum_fusion.refs_0_), channel_id=1, source_target_pairs={{0,6},{2,0},{4,2},{6,4},{1,7},{3,1},{5,3},{7,5},{8,14},{10,8},{12,... | collective-permute-start | bytes 786440 | tf_op jit(solution)/shard_map/ppermute | solution.py:168
  106.5 17.9 %all_to_all.32 = bf16[16,16,256]{2,1,0:T(8,128)(2,1)S(1)} all-to-all(bf16[16,16,256]{2,1,0:T(8,128)(2,1)S(1)} %bitcast.32), channel_id=1, replica_groups=mesh['yh'=2,'z'=8,'yl'=4,'x'=4,'core'=2] {'yh','z'}, dimensions={0} | all-to-all | bytes 262144 | tf_op jit(solution)/shard_map/all_to_all | solution.py:176
  124.5 0.7 broadcast_in_dim.10
  125.2 5.9 %all-to-all-start.4 = ((bf16[32,16,256]{2,1,0:T(8,128)(2,1)}), bf16[32,16,256]{2,1,0:T(8,128)(2,1)S(1)}, u32[]{:S(2)}, u32[]{:S(2)}) async-start(bf16[32,16,256]{2,1,0:T(8,128)(2,1)} %broadcast_in_dim.10), calls=%async_computation.4 | async-start | bytes 524288 | tf_op jit(solution)/shard_map/all_to_all | solution.py:176
  131.1 4.9 %collective-permute-start.6 = (bf16[4,128,256]{2,1,0:T(8,128)(2,1)S(1)}, bf16[4,128,256]{2,1,0:T(8,128)(2,1)S(1)}, u32[]{:S(2)}, u32[]{:S(2)}) collective-permute-start(bf16[4,128,256]{2,1,0:T(8,128)(2,1)S(1)} %pad_maximum_fusion.refs_0_), channel_id=1, source_target_pairs={{0,4},{2,6},{4,0},{6,2},{1,5},{3,7},{5,1},{7,3},{8,12},{10,14},{12... | collective-permute-start | bytes 786440 | tf_op jit(solution)/shard_map/ppermute | solution.py:168
  136.0 2.5 %collective-permute-start.5 = (bf16[4,128,256]{2,1,0:T(8,128)(2,1)S(1)}, bf16[4,128,256]{2,1,0:T(8,128)(2,1)S(1)}, u32[]{:S(2)}, u32[]{:S(2)}) collective-permute-start(bf16[4,128,256]{2,1,0:T(8,128)(2,1)S(1)} %pad_maximum_fusion.refs_0_), channel_id=1, source_target_pairs={{0,2},{2,4},{4,6},{6,0},{1,3},{3,5},{5,7},{7,1},{8,10},{10,12},{12... | collective-permute-start | bytes 786440 | tf_op jit(solution)/shard_map/ppermute | solution.py:168
  138.5 1.9 collective-permute-start.7
  140.5 4.2 %collective-permute-done.6.refs_2_ = bf16[4,128,256]{2,1,0:T(8,128)(2,1)S(1)} collective-permute-done((bf16[4,128,256]{2,1,0:T(8,128)(2,1)S(1)}, bf16[4,128,256]{2,1,0:T(8,128)(2,1)S(1)}, u32[]{:S(2)}, u32[]{:S(2)}) %collective-permute-start.6) | collective-permute-done | bytes 262176 | tf_op jit(solution)/shard_map/ppermute | solution.py:168
  144.7 1.9 collective-permute-start.9
  146.6 3.4 %collective-permute-done.5.refs_1_ = bf16[4,128,256]{2,1,0:T(8,128)(2,1)S(1)} collective-permute-done((bf16[4,128,256]{2,1,0:T(8,128)(2,1)S(1)}, bf16[4,128,256]{2,1,0:T(8,128)(2,1)S(1)}, u32[]{:S(2)}, u32[]{:S(2)}) %collective-permute-start.5) | collective-permute-done | bytes 262176 | tf_op jit(solution)/shard_map/ppermute | solution.py:168
  150.0 2.0 collective-permute-start.8
  152.0 2.3 %collective-permute-start.10 = (bf16[4,128,256]{2,1,0:T(8,128)(2,1)S(1)}, bf16[4,128,256]{2,1,0:T(8,128)(2,1)S(1)}, u32[]{:S(2)}, u32[]{:S(2)}) collective-permute-start(bf16[4,128,256]{2,1,0:T(8,128)(2,1)S(1)} %collective-permute-done.4.refs_3_), channel_id=1, source_target_pairs={{0,1},{1,0},{2,3},{3,2},{4,5},{5,4},{6,7},{7,6},{8,9},{9,8},{10,11... | collective-permute-start | bytes 786440 | tf_op jit(solution)/shard_map/ppermute | solution.py:172
  154.4 1.0 collective-permute-done.10.refs_7_
  155.5 3.5 %backward_tiles.1 = bf16[16,152,256]{2,1,0:T(8,128)(2,1)S(1)} custom-call(s32[128]{0:T(128)S(1)} %bitcast.26, s32[128]{0:T(128)S(1)} %bitcast.28, s32[1]{0:T(128)} %bitcast.24.live_ref, s32[3]{0:T(128)S(1)} %pad_add_fusion.core_ref.place, f32[16,256]{1,0:T(8,128)S(1)} %convert_reduce_fusion.weight_rows, bf16[128,128,128]{2,1,0:T(8,128)(2,1)} %bitcast.30, ...), custom_call_target="tpu_custom_call" | custom-call | flops 1073741824 | bytes 4194304 | tf_op jit(solution)/shard_map/backward_tiles/pallas_call | solution.py:149
  159.0 43.7 %all_to_all.33 = bf16[16,152,256]{2,1,0:T(8,128)(2,1)S(1)} all-to-all(bf16[16,152,256]{2,1,0:T(8,128)(2,1)S(1)} %backward_tiles.1), channel_id=1, replica_groups=mesh['yh'=2,'z'=8,'yl'=4,'x'=4,'core'=2] {'yh','z'}, dimensions={0} | all-to-all | bytes 2490368 | tf_op jit(solution)/shard_map/all_to_all | solution.py:176
  202.7 0.6 slice_add_fusion
  203.4 0.8 convolution_convert_fusion.1
  204.2 0.7 bitcast_convert_fusion
  (27 shorter events, 1.3 us)
Async XLA Ops:
  0.6 87.3 %copy-start = (bf16[256,256]{1,0:T(8,128)(2,1)S(1)}, bf16[256,256]{1,0:T(8,128)(2,1)}, u32[]{:S(2)}) copy-start(bf16[256,256]{1,0:T(8,128)(2,1)} %param.9) | copy-start | bytes 393220
  0.6 48.0 %copy-start.2 = (s32[1,1,128]{2,1,0:T(1,128)S(1)}, s32[1,1,128]{2,1,0:T(1,128)}, u32[]{:S(2)}) copy-start(s32[1,1,128]{2,1,0:T(1,128)} %param.13) | copy-start | bytes 1540
  0.7 48.0 %copy-start.1 = (s32[1,1,128]{2,1,0:T(1,128)S(1)}, s32[1,1,128]{2,1,0:T(1,128)}, u32[]{:S(2)}) copy-start(s32[1,1,128]{2,1,0:T(1,128)} %param.12) | copy-start | bytes 1540
  2.6 46.0 %all-to-all-start = ((bf16[16,128,256]{2,1,0:T(8,128)(2,1)}), bf16[16,128,256]{2,1,0:T(8,128)(2,1)S(1)}, u32[]{:S(2)}, u32[]{:S(2)}) async-start(bf16[16,128,256]{2,1,0:T(8,128)(2,1)} %broadcast_in_dim.8), calls=%async_computation | async-start | bytes 2097152 | tf_op jit(solution)/shard_map/all_to_all | solution.py:176
  51.9 4.6 %collective-permute-start = (bf16[16,128,256]{2,1,0:T(8,128)(2,1)S(1)}, bf16[16,128,256]{2,1,0:T(8,128)(2,1)S(1)}, u32[]{:S(2)}, u32[]{:S(2)}) collective-permute-start(bf16[16,128,256]{2,1,0:T(8,128)(2,1)S(1)} %get-tuple-element.8), channel_id=1, source_target_pairs={{0,1},{1,0},{2,3},{3,2},{4,5},{5,4},{6,7},{7,6},{8,9},{9,8},{10,11... | collective-permute-start | bytes 3145736 | tf_op jit(solution)/shard_map/ppermute | solution.py:172
  56.8 31.1 %copy-start.3 = (bf16[128,256]{1,0:T(8,128)(2,1)S(1)}, bf16[128,256]{1,0:T(8,128)(2,1)}, u32[]{:S(2)}) copy-start(bf16[128,256]{1,0:T(8,128)(2,1)} %param.11) | copy-start | bytes 196612
  56.9 31.1 %copy-start.4 = (f32[256]{0:T(256)S(1)}, f32[256]{0:T(256)}, u32[]{:S(2)}) copy-start(f32[256]{0:T(256)} %param.10) | copy-start | bytes 3076
  88.9 10.6 %collective-permute-start.3 = (bf16[128,256]{1,0:T(8,128)(2,1)S(1)}, bf16[128,256]{1,0:T(8,128)(2,1)S(1)}, u32[]{:S(2)}, u32[]{:S(2)}) collective-permute-start(bf16[128,256]{1,0:T(8,128)(2,1)S(1)} %get-tuple-element.10), channel_id=1, source_target_pairs={{0,24},{8,0},{16,8},{24,16},{1,25},{9,1},{17,9},{25,17},{2,26},{10... | collective-permute-start | bytes 196616 | tf_op jit(solution)/shard_map/ppermute | solution.py:168
  92.6 7.5 %collective-permute-start.2 = (bf16[128,256]{1,0:T(8,128)(2,1)S(1)}, bf16[128,256]{1,0:T(8,128)(2,1)S(1)}, u32[]{:S(2)}, u32[]{:S(2)}) collective-permute-start(bf16[128,256]{1,0:T(8,128)(2,1)S(1)} %get-tuple-element.10), channel_id=1, source_target_pairs={{0,16},{8,24},{16,0},{24,8},{1,17},{9,25},{17,1},{25,9},{2,18},{10... | collective-permute-start | bytes 196616 | tf_op jit(solution)/shard_map/ppermute | solution.py:168
  96.9 6.2 %collective-permute-start.1 = (bf16[128,256]{1,0:T(8,128)(2,1)S(1)}, bf16[128,256]{1,0:T(8,128)(2,1)S(1)}, u32[]{:S(2)}, u32[]{:S(2)}) collective-permute-start(bf16[128,256]{1,0:T(8,128)(2,1)S(1)} %get-tuple-element.10), channel_id=1, source_target_pairs={{0,8},{8,16},{16,24},{24,0},{1,9},{9,17},{17,25},{25,1},{2,10},{10... | collective-permute-start | bytes 196616 | tf_op jit(solution)/shard_map/ppermute | solution.py:168
  103.1 21.3 %collective-permute-start.4 = (bf16[4,128,256]{2,1,0:T(8,128)(2,1)S(1)}, bf16[4,128,256]{2,1,0:T(8,128)(2,1)S(1)}, u32[]{:S(2)}, u32[]{:S(2)}) collective-permute-start(bf16[4,128,256]{2,1,0:T(8,128)(2,1)S(1)} %pad_maximum_fusion.refs_0_), channel_id=1, source_target_pairs={{0,6},{2,0},{4,2},{6,4},{1,7},{3,1},{5,3},{7,5},{8,14},{10,8},{12,... | collective-permute-start | bytes 786440 | tf_op jit(solution)/shard_map/ppermute | solution.py:168
  125.2 29.1 %all-to-all-start.4 = ((bf16[32,16,256]{2,1,0:T(8,128)(2,1)}), bf16[32,16,256]{2,1,0:T(8,128)(2,1)S(1)}, u32[]{:S(2)}, u32[]{:S(2)}) async-start(bf16[32,16,256]{2,1,0:T(8,128)(2,1)} %broadcast_in_dim.10), calls=%async_computation.4 | async-start | bytes 524288 | tf_op jit(solution)/shard_map/all_to_all | solution.py:176
  131.1 13.5 %collective-permute-start.6 = (bf16[4,128,256]{2,1,0:T(8,128)(2,1)S(1)}, bf16[4,128,256]{2,1,0:T(8,128)(2,1)S(1)}, u32[]{:S(2)}, u32[]{:S(2)}) collective-permute-start(bf16[4,128,256]{2,1,0:T(8,128)(2,1)S(1)} %pad_maximum_fusion.refs_0_), channel_id=1, source_target_pairs={{0,4},{2,6},{4,0},{6,2},{1,5},{3,7},{5,1},{7,3},{8,12},{10,14},{12... | collective-permute-start | bytes 786440 | tf_op jit(solution)/shard_map/ppermute | solution.py:168
  136.0 14.0 %collective-permute-start.5 = (bf16[4,128,256]{2,1,0:T(8,128)(2,1)S(1)}, bf16[4,128,256]{2,1,0:T(8,128)(2,1)S(1)}, u32[]{:S(2)}, u32[]{:S(2)}) collective-permute-start(bf16[4,128,256]{2,1,0:T(8,128)(2,1)S(1)} %pad_maximum_fusion.refs_0_), channel_id=1, source_target_pairs={{0,2},{2,4},{4,6},{6,0},{1,3},{3,5},{5,7},{7,1},{8,10},{10,12},{12... | collective-permute-start | bytes 786440 | tf_op jit(solution)/shard_map/ppermute | solution.py:168
  138.5 15.9 %collective-permute-start.7 = (bf16[4,128,256]{2,1,0:T(8,128)(2,1)S(1)}, bf16[4,128,256]{2,1,0:T(8,128)(2,1)S(1)}, u32[]{:S(2)}, u32[]{:S(2)}) collective-permute-start(bf16[4,128,256]{2,1,0:T(8,128)(2,1)S(1)} %pad_maximum_fusion.refs_0_), channel_id=1, source_target_pairs={{0,1},{1,0},{2,3},{3,2},{4,5},{5,4},{6,7},{7,6},{8,9},{9,8},{10,11... | collective-permute-start | bytes 786440 | tf_op jit(solution)/shard_map/ppermute | solution.py:172
  144.7 9.7 %collective-permute-start.9 = (bf16[4,128,256]{2,1,0:T(8,128)(2,1)S(1)}, bf16[4,128,256]{2,1,0:T(8,128)(2,1)S(1)}, u32[]{:S(2)}, u32[]{:S(2)}) collective-permute-start(bf16[4,128,256]{2,1,0:T(8,128)(2,1)S(1)} %collective-permute-done.6.refs_2_), channel_id=1, source_target_pairs={{0,1},{1,0},{2,3},{3,2},{4,5},{5,4},{6,7},{7,6},{8,9},{9,8},{10,11... | collective-permute-start | bytes 786440 | tf_op jit(solution)/shard_map/ppermute | solution.py:172
  150.0 4.4 %collective-permute-start.8 = (bf16[4,128,256]{2,1,0:T(8,128)(2,1)S(1)}, bf16[4,128,256]{2,1,0:T(8,128)(2,1)S(1)}, u32[]{:S(2)}, u32[]{:S(2)}) collective-permute-start(bf16[4,128,256]{2,1,0:T(8,128)(2,1)S(1)} %collective-permute-done.5.refs_1_), channel_id=1, source_target_pairs={{0,1},{1,0},{2,3},{3,2},{4,5},{5,4},{6,7},{7,6},{8,9},{9,8},{10,11... | collective-permute-start | bytes 786440 | tf_op jit(solution)/shard_map/ppermute | solution.py:172
  152.0 3.5 %collective-permute-start.10 = (bf16[4,128,256]{2,1,0:T(8,128)(2,1)S(1)}, bf16[4,128,256]{2,1,0:T(8,128)(2,1)S(1)}, u32[]{:S(2)}, u32[]{:S(2)}) collective-permute-start(bf16[4,128,256]{2,1,0:T(8,128)(2,1)S(1)} %collective-permute-done.4.refs_3_), channel_id=1, source_target_pairs={{0,1},{1,0},{2,3},{3,2},{4,5},{5,4},{6,7},{7,6},{8,9},{9,8},{10,11... | collective-permute-start | bytes 786440 | tf_op jit(solution)/shard_map/ppermute | solution.py:172

commit v9 on v8

--- a/solution.py
+++ b/solution.py
@@ -214,7 +214,7 @@
     blocks = own + [swap(block) for block in own]
 
     pieces = exchange(weight_term.astype(bf16).reshape(16, width // 16, width), ROW)
-    pieces, _ = lax.optimization_barrier((pieces, own[3]))
+    pieces, _ = lax.optimization_barrier((pieces, along_y))
     weight_rows = add_up(gather(add_up(pieces).astype(bf16), COL, 32))
     back = exchange(spread_backward(rows, cols, live, place, weight_rows, values, blocks, col_tiles), ROW)
     grad_mixed = add_up(back[:, :side]).astype(bf16)

time: 206 us -> 199 us (0.966)
  the two profiles are of different devices: /device:TPU:16 before, /device:TPU:22 now
where the time goes in v9:
time: 199 us; the launch traced here: 198 us
  blocking collectives  80.2 us (40%)
  starting transfers between devices  57.9 us (29%)
  waiting for transfers between devices  45 us (23%)
  Pallas kernels  6.06 us (3%)
  matrix products  2.72 us (1%)
  local copies, waits for them, and re-layouts  2.71 us (1%)
  other arithmetic  2.25 us (1%)
    all_to_all x3, blocking collectives, exchange(): return lax.all_to_all(x, axes, 0, 0, tiled=True)  80.2 us
    all_to_all x3, waiting for transfers between devices, exchange(): return lax.all_to_all(x, axes, 0, 0, tiled=True)  31.4 us
    all_to_all x3, starting transfers between devices, exchange(): return lax.all_to_all(x, axes, 0, 0, tiled=True)  27.4 us
    ppermute x6, starting transfers between devices, around(): lax.ppermute(x, axis, [(i, (i + k) % size) for i in range(size)])  20.4 us
    ppermute x5, starting transfers between devices, swap(): return lax.ppermute(x, 'core', [(0, 1), (1, 0)])  10.1 us
    ppermute x6, waiting for transfers between devices, around(): lax.ppermute(x, axis, [(i, (i + k) % size) for i in range(size)])  9.51 us
    ppermute x5, waiting for transfers between devices, swap(): return lax.ppermute(x, 'core', [(0, 1), (1, 0)])  4.04 us
  transfers between devices with their start and end apart: 14, of which 6 were waited for; matrix products, arithmetic and copies ran while one was open for 0% of the time, Pallas kernels for 0%

profile of v9, /device:TPU:22, one launch (start us, length us, event | category | flops | bytes accessed | tf_op | source)
XLA Modules:
  0.0 198.4 jit_solution(10277039177507761484)
XLA Ops:
  0.7 1.9 broadcast_in_dim.8
  2.6 13.9 %all-to-all-start = ((bf16[16,128,256]{2,1,0:T(8,128)(2,1)}), bf16[16,128,256]{2,1,0:T(8,128)(2,1)S(1)}, u32[]{:S(2)}, u32[]{:S(2)}) async-start(bf16[16,128,256]{2,1,0:T(8,128)(2,1)} %broadcast_in_dim.8), calls=%async_computation | async-start | bytes 2097152 | tf_op jit(solution)/shard_map/all_to_all | solution.py:176
  17.2 31.4 %all-to-all-done.src = bf16[16,128,256]{2,1,0:T(8,128)(2,1)S(1)} async-done(((bf16[16,128,256]{2,1,0:T(8,128)(2,1)}), bf16[16,128,256]{2,1,0:T(8,128)(2,1)S(1)}, u32[]{:S(2)}, u32[]{:S(2)}) %all-to-all-start) | async-done | bytes 1048608 | tf_op jit(solution)/shard_map/all_to_all | solution.py:176
  48.6 3.0 %forward_tiles.1 = (bf16[16,128,256]{2,1,0:T(8,128)(2,1)S(1)}, bf16[16,128,256]{2,1,0:T(8,128)(2,1)S(1)}) custom-call(s32[128]{0:T(128)S(1)} %bitcast.25, s32[128]{0:T(128)S(1)} %bitcast.27, s32[1]{0:T(128)} %bitcast.23.live_ref, s32[3]{0:T(128)S(1)} %pad_add_fusion.core_ref.place, bf16[128,128,128]{2,1,0:T(8,128)(2,1)} %bitcast.29, ...), custom_call_target="tpu_custom_call" | custom-call | flops 1073741824 | bytes 4194304 | tf_op jit(solution)/shard_map/forward_tiles/pallas_call | solution.py:130
  51.6 1.9 collective-permute-start
  53.6 2.6 %collective-permute-done = bf16[16,128,256]{2,1,0:T(8,128)(2,1)S(1)} collective-permute-done((bf16[16,128,256]{2,1,0:T(8,128)(2,1)S(1)}, bf16[16,128,256]{2,1,0:T(8,128)(2,1)S(1)}, u32[]{:S(2)}, u32[]{:S(2)}) %collective-permute-start) | collective-permute-done | bytes 1048608 | tf_op jit(solution)/shard_map/ppermute | solution.py:172
  56.6 18.8 %all_to_all.30 = bf16[4,4,128,256]{3,2,1,0:T(8,128)(2,1)S(1)} all-to-all(bf16[4,4,128,256]{3,2,1,0:T(8,128)(2,1)S(1)} %bitcast.31), channel_id=1, replica_groups=mesh['yh'=2,'z'=8,'yl'=4,'x'=4,'core'=2] {'x'}, dimensions={0} | all-to-all | bytes 2097152 | tf_op jit(solution)/shard_map/all_to_all | solution.py:176
  75.6 10.3 %all_to_all.31 = bf16[4,128,256]{2,1,0:T(8,128)(2,1)S(1)} all-to-all(bf16[4,128,256]{2,1,0:T(8,128)(2,1)S(1)} %reduce_sum.63), channel_id=1, replica_groups=mesh['yh'=2,'z'=8,'yl'=4,'x'=4,'core'=2] {'yl'}, dimensions={0} | all-to-all | bytes 524288 | tf_op jit(solution)/shard_map/all_to_all | solution.py:176
  86.0 0.9 fusion.2
  86.9 1.0 convolution_convert_fusion
  87.9 6.1 %all-to-all-start.3 = ((bf16[16,16,256]{2,1,0:T(8,128)(2,1)}), bf16[16,16,256]{2,1,0:T(8,128)(2,1)S(1)}, u32[]{:S(2)}, u32[]{:S(2)}) async-start(bf16[16,16,256]{2,1,0:T(8,128)(2,1)} %bitcast.8), calls=%async_computation.3 | async-start | bytes 262144 | tf_op jit(solution)/shard_map/all_to_all | solution.py:176
  94.0 3.7 %collective-permute-start.3 = (bf16[128,256]{1,0:T(8,128)(2,1)S(1)}, bf16[128,256]{1,0:T(8,128)(2,1)S(1)}, u32[]{:S(2)}, u32[]{:S(2)}) collective-permute-start(bf16[128,256]{1,0:T(8,128)(2,1)S(1)} %get-tuple-element.10), channel_id=1, source_target_pairs={{0,24},{8,0},{16,8},{24,16},{1,25},{9,1},{17,9},{25,17},{2,26},{10... | collective-permute-start | bytes 196616 | tf_op jit(solution)/shard_map/ppermute | solution.py:168
  97.6 4.3 %collective-permute-start.2 = (bf16[128,256]{1,0:T(8,128)(2,1)S(1)}, bf16[128,256]{1,0:T(8,128)(2,1)S(1)}, u32[]{:S(2)}, u32[]{:S(2)}) collective-permute-start(bf16[128,256]{1,0:T(8,128)(2,1)S(1)} %get-tuple-element.10), channel_id=1, source_target_pairs={{0,16},{8,24},{16,0},{24,8},{1,17},{9,25},{17,1},{25,9},{2,18},{10... | collective-permute-start | bytes 196616 | tf_op jit(solution)/shard_map/ppermute | solution.py:168
  102.0 2.6 %collective-permute-start.1 = (bf16[128,256]{1,0:T(8,128)(2,1)S(1)}, bf16[128,256]{1,0:T(8,128)(2,1)S(1)}, u32[]{:S(2)}, u32[]{:S(2)}) collective-permute-start(bf16[128,256]{1,0:T(8,128)(2,1)S(1)} %get-tuple-element.10), channel_id=1, source_target_pairs={{0,8},{8,16},{16,24},{24,0},{1,9},{9,17},{17,25},{25,1},{2,10},{10... | collective-permute-start | bytes 196616 | tf_op jit(solution)/shard_map/ppermute | solution.py:168
  104.6 0.6 collective-permute-done.2
  105.2 3.0 %collective-permute-done.1 = bf16[128,256]{1,0:T(8,128)(2,1)S(1)} collective-permute-done((bf16[128,256]{1,0:T(8,128)(2,1)S(1)}, bf16[128,256]{1,0:T(8,128)(2,1)S(1)}, u32[]{:S(2)}, u32[]{:S(2)}) %collective-permute-start.1) | collective-permute-done | bytes 65568 | tf_op jit(solution)/shard_map/ppermute | solution.py:168
  108.2 0.7 broadcast_in_dim.10
  108.9 7.5 %all-to-all-start.4 = ((bf16[32,16,256]{2,1,0:T(8,128)(2,1)}), bf16[32,16,256]{2,1,0:T(8,128)(2,1)S(1)}, u32[]{:S(2)}, u32[]{:S(2)}) async-start(bf16[32,16,256]{2,1,0:T(8,128)(2,1)} %broadcast_in_dim.10), calls=%async_computation.4 | async-start | bytes 524288 | tf_op jit(solution)/shard_map/all_to_all | solution.py:176
  116.4 2.8 %collective-permute-start.6 = (bf16[4,128,256]{2,1,0:T(8,128)(2,1)S(1)}, bf16[4,128,256]{2,1,0:T(8,128)(2,1)S(1)}, u32[]{:S(2)}, u32[]{:S(2)}) collective-permute-start(bf16[4,128,256]{2,1,0:T(8,128)(2,1)S(1)} %pad_maximum_fusion.refs_0_), channel_id=1, source_target_pairs={{0,6},{2,0},{4,2},{6,4},{1,7},{3,1},{5,3},{7,5},{8,14},{10,8},{12,... | collective-permute-start | bytes 786440 | tf_op jit(solution)/shard_map/ppermute | solution.py:168
  119.2 3.0 %collective-permute-start.5 = (bf16[4,128,256]{2,1,0:T(8,128)(2,1)S(1)}, bf16[4,128,256]{2,1,0:T(8,128)(2,1)S(1)}, u32[]{:S(2)}, u32[]{:S(2)}) collective-permute-start(bf16[4,128,256]{2,1,0:T(8,128)(2,1)S(1)} %pad_maximum_fusion.refs_0_), channel_id=1, source_target_pairs={{0,4},{2,6},{4,0},{6,2},{1,5},{3,7},{5,1},{7,3},{8,12},{10,14},{12... | collective-permute-start | bytes 786440 | tf_op jit(solution)/shard_map/ppermute | solution.py:168
  122.2 4.0 %collective-permute-start.4 = (bf16[4,128,256]{2,1,0:T(8,128)(2,1)S(1)}, bf16[4,128,256]{2,1,0:T(8,128)(2,1)S(1)}, u32[]{:S(2)}, u32[]{:S(2)}) collective-permute-start(bf16[4,128,256]{2,1,0:T(8,128)(2,1)S(1)} %pad_maximum_fusion.refs_0_), channel_id=1, source_target_pairs={{0,2},{2,4},{4,6},{6,0},{1,3},{3,5},{5,7},{7,1},{8,10},{10,12},{12... | collective-permute-start | bytes 786440 | tf_op jit(solution)/shard_map/ppermute | solution.py:168
  126.2 1.9 collective-permute-start.7
  128.2 5.9 %collective-permute-done.6.refs_3_ = bf16[4,128,256]{2,1,0:T(8,128)(2,1)S(1)} collective-permute-done((bf16[4,128,256]{2,1,0:T(8,128)(2,1)S(1)}, bf16[4,128,256]{2,1,0:T(8,128)(2,1)S(1)}, u32[]{:S(2)}, u32[]{:S(2)}) %collective-permute-start.6) | collective-permute-done | bytes 262176 | tf_op jit(solution)/shard_map/ppermute | solution.py:168
  134.1 1.9 collective-permute-start.10
  136.0 2.4 %collective-permute-start.9 = (bf16[4,128,256]{2,1,0:T(8,128)(2,1)S(1)}, bf16[4,128,256]{2,1,0:T(8,128)(2,1)S(1)}, u32[]{:S(2)}, u32[]{:S(2)}) collective-permute-start(bf16[4,128,256]{2,1,0:T(8,128)(2,1)S(1)} %collective-permute-done.5.refs_2_), channel_id=1, source_target_pairs={{0,1},{1,0},{2,3},{3,2},{4,5},{5,4},{6,7},{7,6},{8,9},{9,8},{10,11... | collective-permute-start | bytes 786440 | tf_op jit(solution)/shard_map/ppermute | solution.py:172
  138.5 1.9 collective-permute-start.8
  140.5 1.4 collective-permute-done.8.refs_5_
  141.9 3.1 %backward_tiles.1 = bf16[16,152,256]{2,1,0:T(8,128)(2,1)S(1)} custom-call(s32[128]{0:T(128)S(1)} %bitcast.26, s32[128]{0:T(128)S(1)} %bitcast.28, s32[1]{0:T(128)} %bitcast.24.live_ref, s32[3]{0:T(128)S(1)} %pad_add_fusion.core_ref.place, f32[16,256]{1,0:T(8,128)S(1)} %convert_reduce_fusion.weight_rows, bf16[128,128,128]{2,1,0:T(8,128)(2,1)} %bitcast.30, ...), custom_call_target="tpu_custom_call" | custom-call | flops 1073741824 | bytes 4194304 | tf_op jit(solution)/shard_map/backward_tiles/pallas_call | solution.py:149
  145.0 51.1 %all_to_all.32 = bf16[16,152,256]{2,1,0:T(8,128)(2,1)S(1)} all-to-all(bf16[16,152,256]{2,1,0:T(8,128)(2,1)S(1)} %backward_tiles.1), channel_id=1, replica_groups=mesh['yh'=2,'z'=8,'yl'=4,'x'=4,'core'=2] {'yh','z'}, dimensions={0} | all-to-all | bytes 2490368 | tf_op jit(solution)/shard_map/all_to_all | solution.py:176
  196.1 0.6 slice_add_fusion
  196.8 0.8 convolution_convert_fusion.1
  197.6 0.7 bitcast_convert_fusion
  (28 shorter events, 1.0 us)
Async XLA Ops:
  0.6 85.3 %copy-start = (bf16[256,256]{1,0:T(8,128)(2,1)S(1)}, bf16[256,256]{1,0:T(8,128)(2,1)}, u32[]{:S(2)}) copy-start(bf16[256,256]{1,0:T(8,128)(2,1)} %param.9) | copy-start | bytes 393220
  0.6 48.0 %copy-start.2 = (s32[1,1,128]{2,1,0:T(1,128)S(1)}, s32[1,1,128]{2,1,0:T(1,128)}, u32[]{:S(2)}) copy-start(s32[1,1,128]{2,1,0:T(1,128)} %param.13) | copy-start | bytes 1540
  0.7 48.0 %copy-start.1 = (s32[1,1,128]{2,1,0:T(1,128)S(1)}, s32[1,1,128]{2,1,0:T(1,128)}, u32[]{:S(2)}) copy-start(s32[1,1,128]{2,1,0:T(1,128)} %param.12) | copy-start | bytes 1540
  2.6 46.0 %all-to-all-start = ((bf16[16,128,256]{2,1,0:T(8,128)(2,1)}), bf16[16,128,256]{2,1,0:T(8,128)(2,1)S(1)}, u32[]{:S(2)}, u32[]{:S(2)}) async-start(bf16[16,128,256]{2,1,0:T(8,128)(2,1)} %broadcast_in_dim.8), calls=%async_computation | async-start | bytes 2097152 | tf_op jit(solution)/shard_map/all_to_all | solution.py:176
  51.6 4.6 %collective-permute-start = (bf16[16,128,256]{2,1,0:T(8,128)(2,1)S(1)}, bf16[16,128,256]{2,1,0:T(8,128)(2,1)S(1)}, u32[]{:S(2)}, u32[]{:S(2)}) collective-permute-start(bf16[16,128,256]{2,1,0:T(8,128)(2,1)S(1)} %get-tuple-element.8), channel_id=1, source_target_pairs={{0,1},{1,0},{2,3},{3,2},{4,5},{5,4},{6,7},{7,6},{8,9},{9,8},{10,11... | collective-permute-start | bytes 3145736 | tf_op jit(solution)/shard_map/ppermute | solution.py:172
  56.5 29.4 %copy-start.3 = (bf16[128,256]{1,0:T(8,128)(2,1)S(1)}, bf16[128,256]{1,0:T(8,128)(2,1)}, u32[]{:S(2)}) copy-start(bf16[128,256]{1,0:T(8,128)(2,1)} %param.11) | copy-start | bytes 196612
  56.6 29.4 %copy-start.4 = (f32[256]{0:T(256)S(1)}, f32[256]{0:T(256)}, u32[]{:S(2)}) copy-start(f32[256]{0:T(256)} %param.10) | copy-start | bytes 3076
  87.9 20.3 %all-to-all-start.3 = ((bf16[16,16,256]{2,1,0:T(8,128)(2,1)}), bf16[16,16,256]{2,1,0:T(8,128)(2,1)S(1)}, u32[]{:S(2)}, u32[]{:S(2)}) async-start(bf16[16,16,256]{2,1,0:T(8,128)(2,1)} %bitcast.8), calls=%async_computation.3 | async-start | bytes 262144 | tf_op jit(solution)/shard_map/all_to_all | solution.py:176
  94.0 10.6 %collective-permute-start.3 = (bf16[128,256]{1,0:T(8,128)(2,1)S(1)}, bf16[128,256]{1,0:T(8,128)(2,1)S(1)}, u32[]{:S(2)}, u32[]{:S(2)}) collective-permute-start(bf16[128,256]{1,0:T(8,128)(2,1)S(1)} %get-tuple-element.10), channel_id=1, source_target_pairs={{0,24},{8,0},{16,8},{24,16},{1,25},{9,1},{17,9},{25,17},{2,26},{10... | collective-permute-start | bytes 196616 | tf_op jit(solution)/shard_map/ppermute | solution.py:168
  97.6 7.5 %collective-permute-start.2 = (bf16[128,256]{1,0:T(8,128)(2,1)S(1)}, bf16[128,256]{1,0:T(8,128)(2,1)S(1)}, u32[]{:S(2)}, u32[]{:S(2)}) collective-permute-start(bf16[128,256]{1,0:T(8,128)(2,1)S(1)} %get-tuple-element.10), channel_id=1, source_target_pairs={{0,16},{8,24},{16,0},{24,8},{1,17},{9,25},{17,1},{25,9},{2,18},{10... | collective-permute-start | bytes 196616 | tf_op jit(solution)/shard_map/ppermute | solution.py:168
  102.0 6.2 %collective-permute-start.1 = (bf16[128,256]{1,0:T(8,128)(2,1)S(1)}, bf16[128,256]{1,0:T(8,128)(2,1)S(1)}, u32[]{:S(2)}, u32[]{:S(2)}) collective-permute-start(bf16[128,256]{1,0:T(8,128)(2,1)S(1)} %get-tuple-element.10), channel_id=1, source_target_pairs={{0,8},{8,16},{16,24},{24,0},{1,9},{9,17},{17,25},{25,1},{2,10},{10... | collective-permute-start | bytes 196616 | tf_op jit(solution)/shard_map/ppermute | solution.py:168
  108.9 31.5 %all-to-all-start.4 = ((bf16[32,16,256]{2,1,0:T(8,128)(2,1)}), bf16[32,16,256]{2,1,0:T(8,128)(2,1)S(1)}, u32[]{:S(2)}, u32[]{:S(2)}) async-start(bf16[32,16,256]{2,1,0:T(8,128)(2,1)} %broadcast_in_dim.10), calls=%async_computation.4 | async-start | bytes 524288 | tf_op jit(solution)/shard_map/all_to_all | solution.py:176
  116.4 17.7 %collective-permute-start.6 = (bf16[4,128,256]{2,1,0:T(8,128)(2,1)S(1)}, bf16[4,128,256]{2,1,0:T(8,128)(2,1)S(1)}, u32[]{:S(2)}, u32[]{:S(2)}) collective-permute-start(bf16[4,128,256]{2,1,0:T(8,128)(2,1)S(1)} %pad_maximum_fusion.refs_0_), channel_id=1, source_target_pairs={{0,6},{2,0},{4,2},{6,4},{1,7},{3,1},{5,3},{7,5},{8,14},{10,8},{12,... | collective-permute-start | bytes 786440 | tf_op jit(solution)/shard_map/ppermute | solution.py:168
  119.2 16.8 %collective-permute-start.5 = (bf16[4,128,256]{2,1,0:T(8,128)(2,1)S(1)}, bf16[4,128,256]{2,1,0:T(8,128)(2,1)S(1)}, u32[]{:S(2)}, u32[]{:S(2)}) collective-permute-start(bf16[4,128,256]{2,1,0:T(8,128)(2,1)S(1)} %pad_maximum_fusion.refs_0_), channel_id=1, source_target_pairs={{0,4},{2,6},{4,0},{6,2},{1,5},{3,7},{5,1},{7,3},{8,12},{10,14},{12... | collective-permute-start | bytes 786440 | tf_op jit(solution)/shard_map/ppermute | solution.py:168
  122.2 16.2 %collective-permute-start.4 = (bf16[4,128,256]{2,1,0:T(8,128)(2,1)S(1)}, bf16[4,128,256]{2,1,0:T(8,128)(2,1)S(1)}, u32[]{:S(2)}, u32[]{:S(2)}) collective-permute-start(bf16[4,128,256]{2,1,0:T(8,128)(2,1)S(1)} %pad_maximum_fusion.refs_0_), channel_id=1, source_target_pairs={{0,2},{2,4},{4,6},{6,0},{1,3},{3,5},{5,7},{7,1},{8,10},{10,12},{12... | collective-permute-start | bytes 786440 | tf_op jit(solution)/shard_map/ppermute | solution.py:168
  126.2 14.2 %collective-permute-start.7 = (bf16[4,128,256]{2,1,0:T(8,128)(2,1)S(1)}, bf16[4,128,256]{2,1,0:T(8,128)(2,1)S(1)}, u32[]{:S(2)}, u32[]{:S(2)}) collective-permute-start(bf16[4,128,256]{2,1,0:T(8,128)(2,1)S(1)} %pad_maximum_fusion.refs_0_), channel_id=1, source_target_pairs={{0,1},{1,0},{2,3},{3,2},{4,5},{5,4},{6,7},{7,6},{8,9},{9,8},{10,11... | collective-permute-start | bytes 786440 | tf_op jit(solution)/shard_map/ppermute | solution.py:172
  134.1 6.4 %collective-permute-start.10 = (bf16[4,128,256]{2,1,0:T(8,128)(2,1)S(1)}, bf16[4,128,256]{2,1,0:T(8,128)(2,1)S(1)}, u32[]{:S(2)}, u32[]{:S(2)}) collective-permute-start(bf16[4,128,256]{2,1,0:T(8,128)(2,1)S(1)} %collective-permute-done.6.refs_3_), channel_id=1, source_target_pairs={{0,1},{1,0},{2,3},{3,2},{4,5},{5,4},{6,7},{7,6},{8,9},{9,8},{10,11... | collective-permute-start | bytes 786440 | tf_op jit(solution)/shard_map/ppermute | solution.py:172
  136.0 4.4 %collective-permute-start.9 = (bf16[4,128,256]{2,1,0:T(8,128)(2,1)S(1)}, bf16[4,128,256]{2,1,0:T(8,128)(2,1)S(1)}, u32[]{:S(2)}, u32[]{:S(2)}) collective-permute-start(bf16[4,128,256]{2,1,0:T(8,128)(2,1)S(1)} %collective-permute-done.5.refs_2_), channel_id=1, source_target_pairs={{0,1},{1,0},{2,3},{3,2},{4,5},{5,4},{6,7},{7,6},{8,9},{9,8},{10,11... | collective-permute-start | bytes 786440 | tf_op jit(solution)/shard_map/ppermute | solution.py:172
  138.5 3.4 %collective-permute-start.8 = (bf16[4,128,256]{2,1,0:T(8,128)(2,1)S(1)}, bf16[4,128,256]{2,1,0:T(8,128)(2,1)S(1)}, u32[]{:S(2)}, u32[]{:S(2)}) collective-permute-start(bf16[4,128,256]{2,1,0:T(8,128)(2,1)S(1)} %collective-permute-done.4.refs_1_), channel_id=1, source_target_pairs={{0,1},{1,0},{2,3},{3,2},{4,5},{5,4},{6,7},{7,6},{8,9},{9,8},{10,11... | collective-permute-start | bytes 786440 | tf_op jit(solution)/shard_map/ppermute | solution.py:172

commit v10 on v4

--- a/solution.py
+++ b/solution.py
@@ -9,8 +9,7 @@
 ROW = ("yh", "z")
 COL = ("yl", "x", "core")
 ALL = ROW + COL
-CHUNK = 16
-GROUP = 16
+GROUP = 32
 
 
 def elu_value(pre):
@@ -24,25 +23,26 @@
 def start_values(values_hbm, values, sems):
     copies = [
         pltpu.make_async_copy(
-            values_hbm.at[pl.ds(c * CHUNK, CHUNK)], values.at[pl.ds(c * CHUNK, CHUNK)], sems.at[c]
+            values_hbm.at[pl.ds(c * GROUP, GROUP)], values.at[pl.ds(c * GROUP, GROUP)], sems.at[c]
         )
-        for c in range(values.shape[0] // CHUNK)
+        for c in range(values.shape[0] // GROUP)
     ]
     for copy in copies:
         copy.start()
     return copies
 
 
-def walk(copies, live, step):
+def walk(live, step, copies=()):
+    if not copies:
+
+        def one(g, carry):
+            step(g * GROUP)
+            return carry
+
+        lax.fori_loop(0, (live + GROUP - 1) // GROUP, one, 0)
     for c, copy in enumerate(copies):
         copy.wait()
-        left = jnp.clip(live - c * CHUNK, 0, CHUNK)
-
-        def one(g, carry, c=c):
-            step(c * CHUNK + g * GROUP)
-            return carry
-
-        lax.fori_loop(0, (left + GROUP - 1) // GROUP, one, 0)
+        pl.when(c * GROUP < live)(lambda c=c: step(c * GROUP))
 
 
 def forward_kernel(rows, cols, live_ref, core_ref, values_hbm, src, kept, sent, values, acc, sems):
@@ -60,12 +60,12 @@
             dest = jnp.where(s < live, slot(rows[s]), 2 * half)
             acc[dest] += jnp.dot(values[s], src[cols[s]], preferred_element_type=jnp.float32)
 
-    walk(copies, live, step)
+    walk(live, step, copies)
     sent[...] = acc[half : 2 * half].astype(sent.dtype)
     kept[...] = acc[:half].astype(kept.dtype)
 
 
-def backward_kernel(rows, cols, live_ref, core_ref, values_hbm, own, other, out, values, src, acc, sems, src_sems):
+def backward_kernel(rows, cols, live_ref, core_ref, values, own, other, out, src, acc, src_sems):
     live, core = live_ref[0], core_ref[0]
     fetch = [
         pltpu.make_async_copy(own, src.at[pl.ds(core * 4, 4)], src_sems.at[0]),
@@ -73,24 +73,11 @@
     ]
     for copy in fetch:
         copy.start()
-    copies = start_values(values_hbm, values, sems)
     tiles, side = out.shape[0], values.shape[1]
     gathered = 4 * side
     acc[...] = jnp.zeros_like(acc)
     for copy in fetch:
         copy.wait()
-
-    def step(first):
-        for u in range(GROUP):
-            s = first + u
-            dest = jnp.where(s < live, cols[s], tiles)
-            t = rows[s]
-            block = src[lax.rem(t, 2) * 4 + ((t // 2) & 3), pl.ds(pl.multiple_of(t // 8 * side, side), side), :]
-            acc[dest] += lax.dot_general(
-                values[s], block, (((0,), (0,)), ((), ())), preferred_element_type=jnp.float32
-            )
-
-    walk(copies, live, step)
 
     terms = jnp.zeros((16, out.shape[-1]), jnp.float32)
     bias = jnp.zeros((8, out.shape[-1]), jnp.float32)
@@ -106,8 +93,21 @@
     mine = jnp.where(core == 0, terms[:8], terms[8:])
     tail = jnp.concatenate([mine, tail]).astype(out.dtype)
     for t in range(tiles):
+        out[t, side:, :] = tail
+
+    def step(first):
+        for u in range(GROUP):
+            s = first + u
+            dest = jnp.where(s < live, cols[s], tiles)
+            t = rows[s]
+            block = src[lax.rem(t, 2) * 4 + ((t // 2) & 3), pl.ds(pl.multiple_of(t // 8 * side, side), side), :]
+            acc[dest] += lax.dot_general(
+                values[s], block, (((0,), (0,)), ((), ())), preferred_element_type=jnp.float32
+            )
+
+    walk(live, step)
+    for t in range(tiles):
         out[t, :side, :] = acc[t].astype(out.dtype)
-        out[t, side:, :] = tail
 
 
 SMEM = pl.BlockSpec(memory_space=pltpu.SMEM)
@@ -134,7 +134,7 @@
         scratch_shapes=[
             pltpu.VMEM((slots, side, side), jnp.bfloat16),
             pltpu.VMEM((row_tiles + 1, side, width), jnp.float32),
-            pltpu.SemaphoreType.DMA((slots // CHUNK,)),
+            pltpu.SemaphoreType.DMA((slots // GROUP,)),
         ],
         compiler_params=pltpu.CompilerParams(vmem_limit_bytes=40 << 20),
         cost_estimate=cost(slots, side, width),
@@ -148,16 +148,14 @@
     return pl.pallas_call(
         backward_kernel,
         out_shape=jax.ShapeDtypeStruct((col_tiles, side + 16, width), jnp.bfloat16),
-        in_specs=[SMEM, SMEM, SMEM, SMEM, HBM, ANY, ANY],
+        in_specs=[SMEM, SMEM, SMEM, SMEM, VMEM, ANY, ANY],
         out_specs=VMEM,
         scratch_shapes=[
-            pltpu.VMEM((slots, side, side), jnp.bfloat16),
             pltpu.VMEM((2 * own.shape[0],) + own.shape[1:], jnp.bfloat16),
             pltpu.VMEM((col_tiles + 1, side, width), jnp.float32),
-            pltpu.SemaphoreType.DMA((slots // CHUNK,)),
             pltpu.SemaphoreType.DMA((2,)),
         ],
-        compiler_params=pltpu.CompilerParams(vmem_limit_bytes=40 << 20),
+        compiler_params=pltpu.CompilerParams(vmem_limit_bytes=32 << 20),
         cost_estimate=cost(slots, side, width),
         name="backward_tiles",
     )(rows, cols, live, core, values, own, other)
@@ -186,7 +184,8 @@
 
 
 def body(features, weight, bias, grad_out, tile_rows, tile_cols, tile_counts, tile_values):
-    values = pltpu.with_memory_space_constraint(tile_values[0, 0], pltpu.HBM)
+    values = tile_values[0, 0]
+    in_hbm = pltpu.with_memory_space_constraint(values, pltpu.HBM)
     rows, cols, live = tile_rows[0, 0], tile_cols[0, 0], tile_counts[0]
     side, width = features.shape
     row_tiles, col_tiles = 32, 16
@@ -194,7 +193,7 @@
     core = lax.axis_index("core").astype(jnp.int32).reshape(1)
 
     block = gather(features, ROW, col_tiles)
-    kept, sent = spread_forward(rows, cols, live, core, values, block, row_tiles)
+    kept, sent = spread_forward(rows, cols, live, core, in_hbm, block, row_tiles)
     by_core = (kept.astype(jnp.float32) + swap(sent).astype(jnp.float32)).astype(bf16)
     by_x = add_up(exchange(by_core.reshape(4, 4, side, width), "x")).astype(bf16)
     mean = add_up(exchange(by_x, "yl"))

time: 192 us -> 190 us (0.990)
  blocking collectives: 99.4 us -> 94.8 us
  starting transfers between devices: 40.2 us -> 43.9 us
    all_to_all x5, blocking collectives: 99.4 us -> 94.8 us  [exchange(): return lax.all_to_all(x, axes, 0, 0, tiled=True)]
    all_to_all x2, starting transfers between devices: 28 us -> 32 us  [exchange(): return lax.all_to_all(x, axes, 0, 0, tiled=True)]
where the time goes in v10:
time: 190 us; the launch traced here: 189 us
  blocking collectives  94.8 us (50%)
  starting transfers between devices  43.9 us (23%)
  waiting for transfers between devices  37 us (19%)
  Pallas kernels  5.1 us (3%)
  local copies, waits for them, and re-layouts  3.51 us (2%)
  matrix products  2.06 us (1%)
    all_to_all x5, blocking collectives, exchange(): return lax.all_to_all(x, axes, 0, 0, tiled=True)  94.8 us
    all_to_all x2, waiting for transfers between devices, exchange(): return lax.all_to_all(x, axes, 0, 0, tiled=True)  32.4 us
    all_to_all x2, starting transfers between devices, exchange(): return lax.all_to_all(x, axes, 0, 0, tiled=True)  32 us
    ppermute x2, starting transfers between devices, swap(): return lax.ppermute(x, 'core', [(0, 1), (1, 0)])  11.9 us
    ppermute x2, waiting for transfers between devices, swap(): return lax.ppermute(x, 'core', [(0, 1), (1, 0)])  4.58 us
  transfers between devices with their start and end apart: 4, of which 4 were waited for; matrix products, arithmetic and copies ran while one was open for 1% of the time, Pallas kernels for 0%

profile of v10, /device:TPU:1, one launch (start us, length us, event | category | flops | bytes accessed | tf_op | source)
XLA Modules:
  0.0 189.3 jit_solution(9209568115804824123)
XLA Ops:
  0.6 0.0 copy-start
  0.6 1.9 %broadcast_in_dim.14 = bf16[16,128,256]{2,1,0:T(8,128)(2,1)} broadcast(bf16[128,256]{1,0:T(8,128)(2,1)} %param.8), dimensions={1,2} | broadcast | bytes 1114112 | tf_op jit(solution)/shard_map/broadcast_in_dim | solution.py:173
  2.6 16.4 %all-to-all-start = ((bf16[16,128,256]{2,1,0:T(8,128)(2,1)}), bf16[16,128,256]{2,1,0:T(8,128)(2,1)S(1)}, u32[]{:S(2)}, u32[]{:S(2)}) async-start(bf16[16,128,256]{2,1,0:T(8,128)(2,1)} %broadcast_in_dim.14), calls=%async_computation | async-start | bytes 2097152 | tf_op jit(solution)/shard_map/all_to_all | solution.py:169
  19.6 22.7 %all-to-all-done.src = bf16[16,128,256]{2,1,0:T(8,128)(2,1)S(1)} async-done(((bf16[16,128,256]{2,1,0:T(8,128)(2,1)}), bf16[16,128,256]{2,1,0:T(8,128)(2,1)S(1)}, u32[]{:S(2)}, u32[]{:S(2)}) %all-to-all-start) | async-done | bytes 1048608 | tf_op jit(solution)/shard_map/all_to_all | solution.py:169
  42.4 0.0 copy-done.2
  42.4 0.0 copy-done.3
  42.4 3.0 %forward_tiles.1 = (bf16[16,128,256]{2,1,0:T(8,128)(2,1)S(1)}, bf16[16,128,256]{2,1,0:T(8,128)(2,1)S(1)}) custom-call(s32[128]{0:T(128)S(1)} %bitcast.20, s32[128]{0:T(128)S(1)} %bitcast.22, s32[1]{0:T(128)} %bitcast.16.live_ref, s32[1]{0:T(128)} %bitcast.3.core_ref, bf16[128,128,128]{2,1,0:T(8,128)(2,1)} %bitcast.18, bf16[16,128,256]{2,1,0:T(8,128)(2,1)S(1)} %all-to-all-done.src), custom_call_target="tpu_custom_call" | custom-call | flops 1073741824 | bytes 4194304 | tf_op jit(solution)/shard_map/forward_tiles/pallas_call | solution.py:129
  45.3 6.5 %collective-permute-start = (bf16[16,128,256]{2,1,0:T(8,128)(2,1)S(1)}, bf16[16,128,256]{2,1,0:T(8,128)(2,1)S(1)}, u32[]{:S(2)}, u32[]{:S(2)}) collective-permute-start(bf16[16,128,256]{2,1,0:T(8,128)(2,1)S(1)} %get-tuple-element.7), channel_id=1, source_target_pairs={{0,1},{1,0},{2,3},{3,2},{4,5},{5,4},{6,7},{7,6},{8,9},{9,8},{10,11... | collective-permute-start | bytes 3145736 | tf_op jit(solution)/shard_map/ppermute | solution.py:165
  51.8 2.3 %collective-permute-done = bf16[16,128,256]{2,1,0:T(8,128)(2,1)S(1)} collective-permute-done((bf16[16,128,256]{2,1,0:T(8,128)(2,1)S(1)}, bf16[16,128,256]{2,1,0:T(8,128)(2,1)S(1)}, u32[]{:S(2)}, u32[]{:S(2)}) %collective-permute-start) | collective-permute-done | bytes 1048608 | tf_op jit(solution)/shard_map/ppermute | solution.py:165
  54.1 0.4 add_convert_fusion
  54.5 18.0 %all_to_all.35 = bf16[4,4,128,256]{3,2,1,0:T(8,128)(2,1)S(1)} all-to-all(bf16[4,4,128,256]{3,2,1,0:T(8,128)(2,1)S(1)} %bitcast.24), channel_id=1, replica_groups=mesh['yh'=2,'z'=8,'yl'=4,'x'=4,'core'=2] {'x'}, dimensions={0} | all-to-all | bytes 2097152 | tf_op jit(solution)/shard_map/all_to_all | solution.py:169
  72.5 0.2 reduce_sum.42
  72.7 14.4 %all_to_all.36 = bf16[4,128,256]{2,1,0:T(8,128)(2,1)S(1)} all-to-all(bf16[4,128,256]{2,1,0:T(8,128)(2,1)S(1)} %reduce_sum.42), channel_id=1, replica_groups=mesh['yh'=2,'z'=8,'yl'=4,'x'=4,'core'=2] {'yl'}, dimensions={0} | all-to-all | bytes 524288 | tf_op jit(solution)/shard_map/all_to_all | solution.py:169
  87.2 0.0 copy-done
  87.2 0.9 fusion.2
  88.1 0.3 convolution_convert_fusion
  88.5 14.5 %all_to_all.37 = bf16[4,192,256]{2,1,0:T(8,128)(2,1)S(1)} all-to-all(bf16[4,192,256]{2,1,0:T(8,128)(2,1)S(1)} %pad_maximum_fusion.1), channel_id=1, replica_groups=mesh['yh'=2,'z'=8,'yl'=4,'x'=4,'core'=2] {'yl'}, dimensions={0} | all-to-all | bytes 786432 | tf_op jit(solution)/shard_map/all_to_all | solution.py:169
  103.1 0.1 broadcast_in_dim.34
  103.2 0.0 copy-start.1
  103.2 0.1 pad_maximum_fusion
  103.2 15.5 %all_to_all.38.own = bf16[4,528,256]{2,1,0:T(8,128)(2,1)S(1)} all-to-all(bf16[4,528,256]{2,1,0:T(8,128)(2,1)S(1)} %pad_maximum_fusion), channel_id=1, replica_groups=mesh['yh'=2,'z'=8,'yl'=4,'x'=4,'core'=2] {'x'}, dimensions={0} | all-to-all | bytes 2162688 | tf_op jit(solution)/shard_map/all_to_all | solution.py:169
  118.8 5.4 %collective-permute-start.1 = (bf16[4,528,256]{2,1,0:T(8,128)(2,1)S(1)}, bf16[4,528,256]{2,1,0:T(8,128)(2,1)S(1)}, u32[]{:S(2)}, u32[]{:S(2)}) collective-permute-start(bf16[4,528,256]{2,1,0:T(8,128)(2,1)S(1)} %all_to_all.38.own), channel_id=1, source_target_pairs={{0,1},{1,0},{2,3},{3,2},{4,5},{5,4},{6,7},{7,6},{8,9},{9,8},{10,11... | collective-permute-start | bytes 3244040 | tf_op jit(solution)/shard_map/ppermute | solution.py:165
  124.2 2.3 %collective-permute-done.1.other = bf16[4,528,256]{2,1,0:T(8,128)(2,1)S(1)} collective-permute-done((bf16[4,528,256]{2,1,0:T(8,128)(2,1)S(1)}, bf16[4,528,256]{2,1,0:T(8,128)(2,1)S(1)}, u32[]{:S(2)}, u32[]{:S(2)}) %collective-permute-start.1) | collective-permute-done | bytes 1081376 | tf_op jit(solution)/shard_map/ppermute | solution.py:165
  126.5 2.1 %backward_tiles.1 = bf16[16,144,256]{2,1,0:T(8,128)(2,1)S(1)} custom-call(s32[128]{0:T(128)S(1)} %bitcast.21, s32[128]{0:T(128)S(1)} %bitcast.23, s32[1]{0:T(128)} %bitcast.17.live_ref, s32[1]{0:T(128)} %bitcast.3.core_ref, bf16[128,128,128]{2,1,0:T(8,128)(2,1)S(1)} %bitcast.19, bf16[4,528,256]{2,1,0:T(8,128)(2,1)S(1)} %all_to_all.38.own, ...), custom_call_target="tpu_custom_call" | custom-call | flops 1073741824 | bytes 4194304 | tf_op jit(solution)/shard_map/backward_tiles/pallas_call | solution.py:148
  128.7 32.3 %all_to_all.39 = bf16[16,144,256]{2,1,0:T(8,128)(2,1)S(1)} all-to-all(bf16[16,144,256]{2,1,0:T(8,128)(2,1)S(1)} %backward_tiles.1), channel_id=1, replica_groups=mesh['yh'=2,'z'=8,'yl'=4,'x'=4,'core'=2] {'yh','z'}, dimensions={0} | all-to-all | bytes 2359296 | tf_op jit(solution)/shard_map/all_to_all | solution.py:169
  161.0 0.2 convert_reduce_fusion
  161.1 0.7 broadcast_in_dim.35
  161.8 15.7 %all-to-all-start.6 = ((f32[32,8,256]{2,1,0:T(8,128)}), f32[32,8,256]{2,1,0:T(8,128)S(1)}, u32[]{:S(2)}, u32[]{:S(2)}) async-start(f32[32,8,256]{2,1,0:T(8,128)} %broadcast_in_dim.35), calls=%async_computation.6 | async-start | bytes 524288 | tf_op jit(solution)/shard_map/all_to_all | solution.py:169
  177.5 0.6 slice_add_fusion
  178.1 0.8 convolution_convert_fusion.1
  178.9 9.7 %all-to-all-done.6 = f32[32,8,256]{2,1,0:T(8,128)S(1)} async-done(((f32[32,8,256]{2,1,0:T(8,128)}), f32[32,8,256]{2,1,0:T(8,128)S(1)}, u32[]{:S(2)}, u32[]{:S(2)}) %all-to-all-start.6) | async-done | bytes 262176 | tf_op jit(solution)/shard_map/all_to_all | solution.py:169
  188.6 0.7 copy.14
  (13 shorter events, 0.1 us)
Async XLA Ops:
  0.6 86.5 %copy-start = (bf16[256,256]{1,0:T(8,128)(2,1)S(1)}, bf16[256,256]{1,0:T(8,128)(2,1)}, u32[]{:S(2)}) copy-start(bf16[256,256]{1,0:T(8,128)(2,1)} %param.9) | copy-start | bytes 393220
  2.6 39.8 %copy-start.2 = (s32[1,1,128]{2,1,0:T(1,128)S(1)}, s32[1,1,128]{2,1,0:T(1,128)}, u32[]{:S(2)}) copy-start(s32[1,1,128]{2,1,0:T(1,128)} %param.12) | copy-start | bytes 1540
  2.6 39.8 %copy-start.3 = (s32[1,1,128]{2,1,0:T(1,128)S(1)}, s32[1,1,128]{2,1,0:T(1,128)}, u32[]{:S(2)}) copy-start(s32[1,1,128]{2,1,0:T(1,128)} %param.13) | copy-start | bytes 1540
  2.6 39.8 %all-to-all-start = ((bf16[16,128,256]{2,1,0:T(8,128)(2,1)}), bf16[16,128,256]{2,1,0:T(8,128)(2,1)S(1)}, u32[]{:S(2)}, u32[]{:S(2)}) async-start(bf16[16,128,256]{2,1,0:T(8,128)(2,1)} %broadcast_in_dim.14), calls=%async_computation | async-start | bytes 2097152 | tf_op jit(solution)/shard_map/all_to_all | solution.py:169
  45.3 8.8 %collective-permute-start = (bf16[16,128,256]{2,1,0:T(8,128)(2,1)S(1)}, bf16[16,128,256]{2,1,0:T(8,128)(2,1)S(1)}, u32[]{:S(2)}, u32[]{:S(2)}) collective-permute-start(bf16[16,128,256]{2,1,0:T(8,128)(2,1)S(1)} %get-tuple-element.7), channel_id=1, source_target_pairs={{0,1},{1,0},{2,3},{3,2},{4,5},{5,4},{6,7},{7,6},{8,9},{9,8},{10,11... | collective-permute-start | bytes 3145736 | tf_op jit(solution)/shard_map/ppermute | solution.py:165
  72.5 14.7 %copy-start.4 = (bf16[128,256]{1,0:T(8,128)(2,1)S(1)}, bf16[128,256]{1,0:T(8,128)(2,1)}, u32[]{:S(2)}) copy-start(bf16[128,256]{1,0:T(8,128)(2,1)} %param.11) | copy-start | bytes 196612
  72.5 14.7 %copy-start.5 = (f32[256]{0:T(256)S(1)}, f32[256]{0:T(256)}, u32[]{:S(2)}) copy-start(f32[256]{0:T(256)} %param.10) | copy-start | bytes 3076
  103.2 23.4 %copy-start.1 = (bf16[1,1,128,128,128]{4,3,2,1,0:T(8,128)(2,1)S(1)}, bf16[1,1,128,128,128]{4,3,2,1,0:T(8,128)(2,1)}, u32[]{:S(2)}) copy-start(bf16[1,1,128,128,128]{4,3,2,1,0:T(8,128)(2,1)} %param.15) | copy-start | bytes 12582916
  118.8 7.7 %collective-permute-start.1 = (bf16[4,528,256]{2,1,0:T(8,128)(2,1)S(1)}, bf16[4,528,256]{2,1,0:T(8,128)(2,1)S(1)}, u32[]{:S(2)}, u32[]{:S(2)}) collective-permute-start(bf16[4,528,256]{2,1,0:T(8,128)(2,1)S(1)} %all_to_all.38.own), channel_id=1, source_target_pairs={{0,1},{1,0},{2,3},{3,2},{4,5},{5,4},{6,7},{7,6},{8,9},{9,8},{10,11... | collective-permute-start | bytes 3244040 | tf_op jit(solution)/shard_map/ppermute | solution.py:165
  161.8 26.8 %all-to-all-start.6 = ((f32[32,8,256]{2,1,0:T(8,128)}), f32[32,8,256]{2,1,0:T(8,128)S(1)}, u32[]{:S(2)}, u32[]{:S(2)}) async-start(f32[32,8,256]{2,1,0:T(8,128)} %broadcast_in_dim.35), calls=%async_computation.6 | async-start | bytes 524288 | tf_op jit(solution)/shard_map/all_to_all | solution.py:169

commit v11 on v10

--- a/solution.py
+++ b/solution.py
@@ -216,7 +216,7 @@
 
     reduced = add_up(exchange(back, ROW))
     grad_mixed = reduced[:side].astype(bf16)
-    grad_weight = gather(reduced[side : side + 8], COL, 32).reshape(width, width)
+    grad_weight = gather(reduced[side : side + 8].astype(bf16), COL, 32).reshape(width, width).astype(jnp.float32)
     grad_bias = reduced[side + 8] + reduced[side + 9]
     grad_features = lax.dot_general(
         grad_mixed, weight, (((1,), (1,)), ((), ())), preferred_element_type=jnp.float32

time: 190 us -> 188 us (0.989)
  starting transfers between devices: 43.9 us -> 34.8 us
  blocking collectives: 94.8 us -> 103 us
  waiting for transfers between devices: 37 us -> 34.5 us
    all_to_all x2, starting transfers between devices: 32 us -> 23.4 us  [exchange(): return lax.all_to_all(x, axes, 0, 0, tiled=True)]
    all_to_all x5, blocking collectives: 94.8 us -> 103 us  [exchange(): return lax.all_to_all(x, axes, 0, 0, tiled=True)]
    all_to_all x2, waiting for transfers between devices: 32.4 us -> 29.9 us  [exchange(): return lax.all_to_all(x, axes, 0, 0, tiled=True)]
where the time goes in v11:
time: 188 us; the launch traced here: 187 us
  blocking collectives  103 us (55%)
  starting transfers between devices  34.8 us (19%)
  waiting for transfers between devices  34.5 us (18%)
  Pallas kernels  6.39 us (3%)
  local copies, waits for them, and re-layouts  2.75 us (1%)
  other arithmetic  2.19 us (1%)
  matrix products  2.06 us (1%)
    all_to_all x5, blocking collectives, exchange(): return lax.all_to_all(x, axes, 0, 0, tiled=True)  103 us
    all_to_all x2, waiting for transfers between devices, exchange(): return lax.all_to_all(x, axes, 0, 0, tiled=True)  29.9 us
    all_to_all x2, starting transfers between devices, exchange(): return lax.all_to_all(x, axes, 0, 0, tiled=True)  23.4 us
    ppermute x2, starting transfers between devices, swap(): return lax.ppermute(x, 'core', [(0, 1), (1, 0)])  11.4 us
    ppermute x2, waiting for transfers between devices, swap(): return lax.ppermute(x, 'core', [(0, 1), (1, 0)])  4.58 us
  transfers between devices with their start and end apart: 4, of which 4 were waited for; matrix products, arithmetic and copies ran while one was open for 1% of the time, Pallas kernels for 0%

profile of v11, /device:TPU:1, one launch (start us, length us, event | category | flops | bytes accessed | tf_op | source)
XLA Modules:
  0.0 187.0 jit_solution(12704115247246859327)
XLA Ops:
  0.6 0.0 copy-start
  0.6 1.9 %broadcast_in_dim.14 = bf16[16,128,256]{2,1,0:T(8,128)(2,1)} broadcast(bf16[128,256]{1,0:T(8,128)(2,1)} %param.8), dimensions={1,2} | broadcast | bytes 1114112 | tf_op jit(solution)/shard_map/broadcast_in_dim | solution.py:173
  2.6 16.4 %all-to-all-start = ((bf16[16,128,256]{2,1,0:T(8,128)(2,1)}), bf16[16,128,256]{2,1,0:T(8,128)(2,1)S(1)}, u32[]{:S(2)}, u32[]{:S(2)}) async-start(bf16[16,128,256]{2,1,0:T(8,128)(2,1)} %broadcast_in_dim.14), calls=%async_computation | async-start | bytes 2097152 | tf_op jit(solution)/shard_map/all_to_all | solution.py:169
  19.6 22.7 %all-to-all-done.src = bf16[16,128,256]{2,1,0:T(8,128)(2,1)S(1)} async-done(((bf16[16,128,256]{2,1,0:T(8,128)(2,1)}), bf16[16,128,256]{2,1,0:T(8,128)(2,1)S(1)}, u32[]{:S(2)}, u32[]{:S(2)}) %all-to-all-start) | async-done | bytes 1048608 | tf_op jit(solution)/shard_map/all_to_all | solution.py:169
  42.4 0.0 copy-done.2
  42.4 0.0 copy-done.3
  42.4 3.5 %forward_tiles.1 = (bf16[16,128,256]{2,1,0:T(8,128)(2,1)S(1)}, bf16[16,128,256]{2,1,0:T(8,128)(2,1)S(1)}) custom-call(s32[128]{0:T(128)S(1)} %bitcast.22, s32[128]{0:T(128)S(1)} %bitcast.24, s32[1]{0:T(128)} %bitcast.18.live_ref, s32[1]{0:T(128)} %bitcast.3.core_ref, bf16[128,128,128]{2,1,0:T(8,128)(2,1)} %bitcast.20, bf16[16,128,256]{2,1,0:T(8,128)(2,1)S(1)} %all-to-all-done.src), custom_call_target="tpu_custom_call" | custom-call | flops 1073741824 | bytes 4194304 | tf_op jit(solution)/shard_map/forward_tiles/pallas_call | solution.py:129
  45.8 6.0 %collective-permute-start = (bf16[16,128,256]{2,1,0:T(8,128)(2,1)S(1)}, bf16[16,128,256]{2,1,0:T(8,128)(2,1)S(1)}, u32[]{:S(2)}, u32[]{:S(2)}) collective-permute-start(bf16[16,128,256]{2,1,0:T(8,128)(2,1)S(1)} %get-tuple-element.7), channel_id=1, source_target_pairs={{0,1},{1,0},{2,3},{3,2},{4,5},{5,4},{6,7},{7,6},{8,9},{9,8},{10,11... | collective-permute-start | bytes 3145736 | tf_op jit(solution)/shard_map/ppermute | solution.py:165
  51.8 2.3 %collective-permute-done = bf16[16,128,256]{2,1,0:T(8,128)(2,1)S(1)} collective-permute-done((bf16[16,128,256]{2,1,0:T(8,128)(2,1)S(1)}, bf16[16,128,256]{2,1,0:T(8,128)(2,1)S(1)}, u32[]{:S(2)}, u32[]{:S(2)}) %collective-permute-start) | collective-permute-done | bytes 1048608 | tf_op jit(solution)/shard_map/ppermute | solution.py:165
  54.1 0.4 add_convert_fusion
  54.5 18.0 %all_to_all.35 = bf16[4,4,128,256]{3,2,1,0:T(8,128)(2,1)S(1)} all-to-all(bf16[4,4,128,256]{3,2,1,0:T(8,128)(2,1)S(1)} %bitcast.26), channel_id=1, replica_groups=mesh['yh'=2,'z'=8,'yl'=4,'x'=4,'core'=2] {'x'}, dimensions={0} | all-to-all | bytes 2097152 | tf_op jit(solution)/shard_map/all_to_all | solution.py:169
  72.5 0.2 reduce_sum.42
  72.7 14.4 %all_to_all.36 = bf16[4,128,256]{2,1,0:T(8,128)(2,1)S(1)} all-to-all(bf16[4,128,256]{2,1,0:T(8,128)(2,1)S(1)} %reduce_sum.42), channel_id=1, replica_groups=mesh['yh'=2,'z'=8,'yl'=4,'x'=4,'core'=2] {'yl'}, dimensions={0} | all-to-all | bytes 524288 | tf_op jit(solution)/shard_map/all_to_all | solution.py:169
  87.2 0.0 copy-done
  87.2 0.9 fusion.2
  88.1 0.3 convolution_convert_fusion
  88.5 14.5 %all_to_all.37 = bf16[4,192,256]{2,1,0:T(8,128)(2,1)S(1)} all-to-all(bf16[4,192,256]{2,1,0:T(8,128)(2,1)S(1)} %pad_maximum_fusion.1), channel_id=1, replica_groups=mesh['yh'=2,'z'=8,'yl'=4,'x'=4,'core'=2] {'yl'}, dimensions={0} | all-to-all | bytes 786432 | tf_op jit(solution)/shard_map/all_to_all | solution.py:169
  103.1 0.1 broadcast_in_dim.34
  103.2 0.0 copy-start.1
  103.2 0.1 pad_maximum_fusion
  103.2 15.5 %all_to_all.38.own = bf16[4,528,256]{2,1,0:T(8,128)(2,1)S(1)} all-to-all(bf16[4,528,256]{2,1,0:T(8,128)(2,1)S(1)} %pad_maximum_fusion), channel_id=1, replica_groups=mesh['yh'=2,'z'=8,'yl'=4,'x'=4,'core'=2] {'x'}, dimensions={0} | all-to-all | bytes 2162688 | tf_op jit(solution)/shard_map/all_to_all | solution.py:169
  118.8 5.4 %collective-permute-start.1 = (bf16[4,528,256]{2,1,0:T(8,128)(2,1)S(1)}, bf16[4,528,256]{2,1,0:T(8,128)(2,1)S(1)}, u32[]{:S(2)}, u32[]{:S(2)}) collective-permute-start(bf16[4,528,256]{2,1,0:T(8,128)(2,1)S(1)} %all_to_all.38.own), channel_id=1, source_target_pairs={{0,1},{1,0},{2,3},{3,2},{4,5},{5,4},{6,7},{7,6},{8,9},{9,8},{10,11... | collective-permute-start | bytes 3244040 | tf_op jit(solution)/shard_map/ppermute | solution.py:165
  124.2 2.3 %collective-permute-done.1.other = bf16[4,528,256]{2,1,0:T(8,128)(2,1)S(1)} collective-permute-done((bf16[4,528,256]{2,1,0:T(8,128)(2,1)S(1)}, bf16[4,528,256]{2,1,0:T(8,128)(2,1)S(1)}, u32[]{:S(2)}, u32[]{:S(2)}) %collective-permute-start.1) | collective-permute-done | bytes 1081376 | tf_op jit(solution)/shard_map/ppermute | solution.py:165
  126.5 2.9 %backward_tiles.1 = bf16[16,144,256]{2,1,0:T(8,128)(2,1)S(1)} custom-call(s32[128]{0:T(128)S(1)} %bitcast.23, s32[128]{0:T(128)S(1)} %bitcast.25, s32[1]{0:T(128)} %bitcast.19.live_ref, s32[1]{0:T(128)} %bitcast.3.core_ref, bf16[128,128,128]{2,1,0:T(8,128)(2,1)S(1)} %bitcast.21, bf16[4,528,256]{2,1,0:T(8,128)(2,1)S(1)} %all_to_all.38.own, ...), custom_call_target="tpu_custom_call" | custom-call | flops 1073741824 | bytes 4194304 | tf_op jit(solution)/shard_map/backward_tiles/pallas_call | solution.py:148
  129.5 40.4 %all_to_all.39 = bf16[16,144,256]{2,1,0:T(8,128)(2,1)S(1)} all-to-all(bf16[16,144,256]{2,1,0:T(8,128)(2,1)S(1)} %backward_tiles.1), channel_id=1, replica_groups=mesh['yh'=2,'z'=8,'yl'=4,'x'=4,'core'=2] {'yh','z'}, dimensions={0} | all-to-all | bytes 2359296 | tf_op jit(solution)/shard_map/all_to_all | solution.py:169
  169.8 0.2 convert_reduce_fusion
  170.0 0.7 broadcast_in_dim.35
  170.7 7.0 %all-to-all-start.6 = ((bf16[32,8,256]{2,1,0:T(8,128)(2,1)}), bf16[32,8,256]{2,1,0:T(8,128)(2,1)S(1)}, u32[]{:S(2)}, u32[]{:S(2)}) async-start(bf16[32,8,256]{2,1,0:T(8,128)(2,1)} %broadcast_in_dim.35), calls=%async_computation.6 | async-start | bytes 262144 | tf_op jit(solution)/shard_map/all_to_all | solution.py:169
  177.7 0.6 slice_add_fusion
  178.3 0.8 convolution_convert_fusion.1
  179.1 7.1 %all-to-all-done.6 = bf16[32,8,256]{2,1,0:T(8,128)(2,1)S(1)} async-done(((bf16[32,8,256]{2,1,0:T(8,128)(2,1)}), bf16[32,8,256]{2,1,0:T(8,128)(2,1)S(1)}, u32[]{:S(2)}, u32[]{:S(2)}) %all-to-all-start.6) | async-done | bytes 131104 | tf_op jit(solution)/shard_map/all_to_all | solution.py:169
  186.2 0.7 bitcast_convert_fusion
  (14 shorter events, 0.1 us)
Async XLA Ops:
  0.6 86.5 %copy-start = (bf16[256,256]{1,0:T(8,128)(2,1)S(1)}, bf16[256,256]{1,0:T(8,128)(2,1)}, u32[]{:S(2)}) copy-start(bf16[256,256]{1,0:T(8,128)(2,1)} %param.9) | copy-start | bytes 393220
  2.6 39.8 %copy-start.2 = (s32[1,1,128]{2,1,0:T(1,128)S(1)}, s32[1,1,128]{2,1,0:T(1,128)}, u32[]{:S(2)}) copy-start(s32[1,1,128]{2,1,0:T(1,128)} %param.12) | copy-start | bytes 1540
  2.6 39.8 %copy-start.3 = (s32[1,1,128]{2,1,0:T(1,128)S(1)}, s32[1,1,128]{2,1,0:T(1,128)}, u32[]{:S(2)}) copy-start(s32[1,1,128]{2,1,0:T(1,128)} %param.13) | copy-start | bytes 1540
  2.6 39.8 %all-to-all-start = ((bf16[16,128,256]{2,1,0:T(8,128)(2,1)}), bf16[16,128,256]{2,1,0:T(8,128)(2,1)S(1)}, u32[]{:S(2)}, u32[]{:S(2)}) async-start(bf16[16,128,256]{2,1,0:T(8,128)(2,1)} %broadcast_in_dim.14), calls=%async_computation | async-start | bytes 2097152 | tf_op jit(solution)/shard_map/all_to_all | solution.py:169
  45.8 8.3 %collective-permute-start = (bf16[16,128,256]{2,1,0:T(8,128)(2,1)S(1)}, bf16[16,128,256]{2,1,0:T(8,128)(2,1)S(1)}, u32[]{:S(2)}, u32[]{:S(2)}) collective-permute-start(bf16[16,128,256]{2,1,0:T(8,128)(2,1)S(1)} %get-tuple-element.7), channel_id=1, source_target_pairs={{0,1},{1,0},{2,3},{3,2},{4,5},{5,4},{6,7},{7,6},{8,9},{9,8},{10,11... | collective-permute-start | bytes 3145736 | tf_op jit(solution)/shard_map/ppermute | solution.py:165
  72.5 14.7 %copy-start.4 = (bf16[128,256]{1,0:T(8,128)(2,1)S(1)}, bf16[128,256]{1,0:T(8,128)(2,1)}, u32[]{:S(2)}) copy-start(bf16[128,256]{1,0:T(8,128)(2,1)} %param.11) | copy-start | bytes 196612
  72.5 14.7 %copy-start.5 = (f32[256]{0:T(256)S(1)}, f32[256]{0:T(256)}, u32[]{:S(2)}) copy-start(f32[256]{0:T(256)} %param.10) | copy-start | bytes 3076
  103.2 23.4 %copy-start.1 = (bf16[1,1,128,128,128]{4,3,2,1,0:T(8,128)(2,1)S(1)}, bf16[1,1,128,128,128]{4,3,2,1,0:T(8,128)(2,1)}, u32[]{:S(2)}) copy-start(bf16[1,1,128,128,128]{4,3,2,1,0:T(8,128)(2,1)} %param.15) | copy-start | bytes 12582916
  118.8 7.7 %collective-permute-start.1 = (bf16[4,528,256]{2,1,0:T(8,128)(2,1)S(1)}, bf16[4,528,256]{2,1,0:T(8,128)(2,1)S(1)}, u32[]{:S(2)}, u32[]{:S(2)}) collective-permute-start(bf16[4,528,256]{2,1,0:T(8,128)(2,1)S(1)} %all_to_all.38.own), channel_id=1, source_target_pairs={{0,1},{1,0},{2,3},{3,2},{4,5},{5,4},{6,7},{7,6},{8,9},{9,8},{10,11... | collective-permute-start | bytes 3244040 | tf_op jit(solution)/shard_map/ppermute | solution.py:165
  170.7 15.6 %all-to-all-start.6 = ((bf16[32,8,256]{2,1,0:T(8,128)(2,1)}), bf16[32,8,256]{2,1,0:T(8,128)(2,1)S(1)}, u32[]{:S(2)}, u32[]{:S(2)}) async-start(bf16[32,8,256]{2,1,0:T(8,128)(2,1)} %broadcast_in_dim.35), calls=%async_computation.6 | async-start | bytes 262144 | tf_op jit(solution)/shard_map/all_to_all | solution.py:169

commit v12 on v11

--- a/solution.py
+++ b/solution.py
@@ -8,6 +8,7 @@
 
 ROW = ("yh", "z")
 COL = ("yl", "x", "core")
+PAIRS = ("z", "yh")
 ALL = ROW + COL
 GROUP = 32
 
@@ -18,6 +19,10 @@
 
 def elu_slope(pre):
     return jnp.where(pre > 0, jnp.float32(1.0), jnp.exp(jnp.minimum(pre, 0.0)))
+
+
+def pair_slot(t):
+    return (t & 7) * 2 + t // 8
 
 
 def start_values(values_hbm, values, sems):
@@ -58,7 +63,7 @@
         for u in range(GROUP):
             s = first + u
             dest = jnp.where(s < live, slot(rows[s]), 2 * half)
-            acc[dest] += jnp.dot(values[s], src[cols[s]], preferred_element_type=jnp.float32)
+            acc[dest] += jnp.dot(values[s], src[pair_slot(cols[s])], preferred_element_type=jnp.float32)
 
     walk(live, step, copies)
     sent[...] = acc[half : 2 * half].astype(sent.dtype)
@@ -98,7 +103,7 @@
     def step(first):
         for u in range(GROUP):
             s = first + u
-            dest = jnp.where(s < live, cols[s], tiles)
+            dest = jnp.where(s < live, pair_slot(cols[s]), tiles)
             t = rows[s]
             block = src[lax.rem(t, 2) * 4 + ((t // 2) & 3), pl.ds(pl.multiple_of(t // 8 * side, side), side), :]
             acc[dest] += lax.dot_general(
@@ -192,7 +197,7 @@
     bf16 = jnp.bfloat16
     core = lax.axis_index("core").astype(jnp.int32).reshape(1)
 
-    block = gather(features, ROW, col_tiles)
+    block = gather(features, PAIRS, col_tiles)
     kept, sent = spread_forward(rows, cols, live, core, in_hbm, block, row_tiles)
     by_core = (kept.astype(jnp.float32) + swap(sent).astype(jnp.float32)).astype(bf16)
     by_x = add_up(exchange(by_core.reshape(4, 4, side, width), "x")).astype(bf16)
@@ -214,7 +219,7 @@
     own = gather_and_scatter(along_y[:, :side].reshape(4 * side, width), terms, "x")
     back = spread_backward(rows, cols, live, core, values, own, swap(own), col_tiles)
 
-    reduced = add_up(exchange(back, ROW))
+    reduced = add_up(exchange(back, PAIRS))
     grad_mixed = reduced[:side].astype(bf16)
     grad_weight = gather(reduced[side : side + 8].astype(bf16), COL, 32).reshape(width, width).astype(jnp.float32)
     grad_bias = reduced[side + 8] + reduced[side + 9]

time: 188 us -> 202 us (1.074)
  starting transfers between devices: 34.8 us -> 41.4 us
  blocking collectives: 103 us -> 109 us
    all_to_all x2, starting transfers between devices: 23.4 us -> 31.1 us  [exchange(): return lax.all_to_all(x, axes, 0, 0, tiled=True)]
    all_to_all x5, blocking collectives: 103 us -> 109 us  [exchange(): return lax.all_to_all(x, axes, 0, 0, tiled=True)]
where the time goes in v12:
time: 202 us; the launch traced here: 201 us
  blocking collectives  109 us (54%)
  starting transfers between devices  41.4 us (20%)
  waiting for transfers between devices  36.1 us (18%)
  Pallas kernels  6.63 us (3%)
  local copies, waits for them, and re-layouts  2.75 us (1%)
  other arithmetic  2.19 us (1%)
  matrix products  2.06 us (1%)
    all_to_all x5, blocking collectives, exchange(): return lax.all_to_all(x, axes, 0, 0, tiled=True)  109 us
    all_to_all x2, waiting for transfers between devices, exchange(): return lax.all_to_all(x, axes, 0, 0, tiled=True)  31.5 us
    all_to_all x2, starting transfers between devices, exchange(): return lax.all_to_all(x, axes, 0, 0, tiled=True)  31.1 us
    ppermute x2, starting transfers between devices, swap(): return lax.ppermute(x, 'core', [(0, 1), (1, 0)])  10.3 us
    ppermute x2, waiting for transfers between devices, swap(): return lax.ppermute(x, 'core', [(0, 1), (1, 0)])  4.58 us
  transfers between devices with their start and end apart: 4, of which 4 were waited for; matrix products, arithmetic and copies ran while one was open for 1% of the time, Pallas kernels for 0%

profile of v12, /device:TPU:1, one launch (start us, length us, event | category | flops | bytes accessed | tf_op | source)
XLA Modules:
  0.0 201.5 jit_solution(3286447256448828949)
XLA Ops:
  0.6 0.0 copy-start
  0.6 1.9 broadcast_in_dim.14
  2.6 16.4 %all-to-all-start = ((bf16[16,128,256]{2,1,0:T(8,128)(2,1)}), bf16[16,128,256]{2,1,0:T(8,128)(2,1)S(1)}, u32[]{:S(2)}, u32[]{:S(2)}) async-start(bf16[16,128,256]{2,1,0:T(8,128)(2,1)} %broadcast_in_dim.14), calls=%async_computation | async-start | bytes 2097152 | tf_op jit(solution)/shard_map/all_to_all | solution.py:174
  19.6 24.3 %all-to-all-done.src = bf16[16,128,256]{2,1,0:T(8,128)(2,1)S(1)} async-done(((bf16[16,128,256]{2,1,0:T(8,128)(2,1)}), bf16[16,128,256]{2,1,0:T(8,128)(2,1)S(1)}, u32[]{:S(2)}, u32[]{:S(2)}) %all-to-all-start) | async-done | bytes 1048608 | tf_op jit(solution)/shard_map/all_to_all | solution.py:174
  44.0 0.0 copy-done.3
  44.0 3.6 %forward_tiles.1 = (bf16[16,128,256]{2,1,0:T(8,128)(2,1)S(1)}, bf16[16,128,256]{2,1,0:T(8,128)(2,1)S(1)}) custom-call(s32[128]{0:T(128)S(1)} %bitcast.22, s32[128]{0:T(128)S(1)} %bitcast.24, s32[1]{0:T(128)} %bitcast.18.live_ref, s32[1]{0:T(128)} %bitcast.3.core_ref, bf16[128,128,128]{2,1,0:T(8,128)(2,1)} %bitcast.20, bf16[16,128,256]{2,1,0:T(8,128)(2,1)S(1)} %all-to-all-done.src), custom_call_target="tpu_custom_call" | custom-call | flops 1073741824 | bytes 4194304 | tf_op jit(solution)/shard_map/forward_tiles/pallas_call | solution.py:134
  47.5 4.9 %collective-permute-start = (bf16[16,128,256]{2,1,0:T(8,128)(2,1)S(1)}, bf16[16,128,256]{2,1,0:T(8,128)(2,1)S(1)}, u32[]{:S(2)}, u32[]{:S(2)}) collective-permute-start(bf16[16,128,256]{2,1,0:T(8,128)(2,1)S(1)} %get-tuple-element.7), channel_id=1, source_target_pairs={{0,1},{1,0},{2,3},{3,2},{4,5},{5,4},{6,7},{7,6},{8,9},{9,8},{10,11... | collective-permute-start | bytes 3145736 | tf_op jit(solution)/shard_map/ppermute | solution.py:170
  52.5 2.3 %collective-permute-done = bf16[16,128,256]{2,1,0:T(8,128)(2,1)S(1)} collective-permute-done((bf16[16,128,256]{2,1,0:T(8,128)(2,1)S(1)}, bf16[16,128,256]{2,1,0:T(8,128)(2,1)S(1)}, u32[]{:S(2)}, u32[]{:S(2)}) %collective-permute-start) | collective-permute-done | bytes 1048608 | tf_op jit(solution)/shard_map/ppermute | solution.py:170
  54.7 0.4 add_convert_fusion
  55.1 18.4 %all_to_all.35 = bf16[4,4,128,256]{3,2,1,0:T(8,128)(2,1)S(1)} all-to-all(bf16[4,4,128,256]{3,2,1,0:T(8,128)(2,1)S(1)} %bitcast.26), channel_id=1, replica_groups=mesh['yh'=2,'z'=8,'yl'=4,'x'=4,'core'=2] {'x'}, dimensions={0} | all-to-all | bytes 2097152 | tf_op jit(solution)/shard_map/all_to_all | solution.py:174
  73.5 0.2 reduce_sum.42
  73.7 20.9 %all_to_all.36 = bf16[4,128,256]{2,1,0:T(8,128)(2,1)S(1)} all-to-all(bf16[4,128,256]{2,1,0:T(8,128)(2,1)S(1)} %reduce_sum.42), channel_id=1, replica_groups=mesh['yh'=2,'z'=8,'yl'=4,'x'=4,'core'=2] {'yl'}, dimensions={0} | all-to-all | bytes 524288 | tf_op jit(solution)/shard_map/all_to_all | solution.py:174
  94.6 0.0 copy-done
  94.7 0.0 copy-done.4
  94.7 0.9 fusion.2
  95.6 0.3 convolution_convert_fusion
  96.0 13.8 %all_to_all.37 = bf16[4,192,256]{2,1,0:T(8,128)(2,1)S(1)} all-to-all(bf16[4,192,256]{2,1,0:T(8,128)(2,1)S(1)} %pad_maximum_fusion.1), channel_id=1, replica_groups=mesh['yh'=2,'z'=8,'yl'=4,'x'=4,'core'=2] {'yl'}, dimensions={0} | all-to-all | bytes 786432 | tf_op jit(solution)/shard_map/all_to_all | solution.py:174
  109.9 0.1 broadcast_in_dim.34
  109.9 0.0 copy-start.1
  109.9 0.1 pad_maximum_fusion
  110.0 16.1 %all_to_all.38.own = bf16[4,528,256]{2,1,0:T(8,128)(2,1)S(1)} all-to-all(bf16[4,528,256]{2,1,0:T(8,128)(2,1)S(1)} %pad_maximum_fusion), channel_id=1, replica_groups=mesh['yh'=2,'z'=8,'yl'=4,'x'=4,'core'=2] {'x'}, dimensions={0} | all-to-all | bytes 2162688 | tf_op jit(solution)/shard_map/all_to_all | solution.py:174
  126.1 5.3 %collective-permute-start.1 = (bf16[4,528,256]{2,1,0:T(8,128)(2,1)S(1)}, bf16[4,528,256]{2,1,0:T(8,128)(2,1)S(1)}, u32[]{:S(2)}, u32[]{:S(2)}) collective-permute-start(bf16[4,528,256]{2,1,0:T(8,128)(2,1)S(1)} %all_to_all.38.own), channel_id=1, source_target_pairs={{0,1},{1,0},{2,3},{3,2},{4,5},{5,4},{6,7},{7,6},{8,9},{9,8},{10,11... | collective-permute-start | bytes 3244040 | tf_op jit(solution)/shard_map/ppermute | solution.py:170
  131.5 2.3 %collective-permute-done.1.other = bf16[4,528,256]{2,1,0:T(8,128)(2,1)S(1)} collective-permute-done((bf16[4,528,256]{2,1,0:T(8,128)(2,1)S(1)}, bf16[4,528,256]{2,1,0:T(8,128)(2,1)S(1)}, u32[]{:S(2)}, u32[]{:S(2)}) %collective-permute-start.1) | collective-permute-done | bytes 1081376 | tf_op jit(solution)/shard_map/ppermute | solution.py:170
  133.8 3.1 %backward_tiles.1 = bf16[16,144,256]{2,1,0:T(8,128)(2,1)S(1)} custom-call(s32[128]{0:T(128)S(1)} %bitcast.23, s32[128]{0:T(128)S(1)} %bitcast.25, s32[1]{0:T(128)} %bitcast.19.live_ref, s32[1]{0:T(128)} %bitcast.3.core_ref, bf16[128,128,128]{2,1,0:T(8,128)(2,1)S(1)} %bitcast.21, bf16[4,528,256]{2,1,0:T(8,128)(2,1)S(1)} %all_to_all.38.own, ...), custom_call_target="tpu_custom_call" | custom-call | flops 1073741824 | bytes 4194304 | tf_op jit(solution)/shard_map/backward_tiles/pallas_call | solution.py:153
  136.9 39.7 %all_to_all.39 = bf16[16,144,256]{2,1,0:T(8,128)(2,1)S(1)} all-to-all(bf16[16,144,256]{2,1,0:T(8,128)(2,1)S(1)} %backward_tiles.1), channel_id=1, replica_groups=mesh['yh'=2,'z'=8,'yl'=4,'x'=4,'core'=2] {'z','yh'}, dimensions={0} | all-to-all | bytes 2359296 | tf_op jit(solution)/shard_map/all_to_all | solution.py:174
  176.6 0.2 convert_reduce_fusion
  176.8 0.7 broadcast_in_dim.35
  177.4 14.8 %all-to-all-start.6 = ((bf16[32,8,256]{2,1,0:T(8,128)(2,1)}), bf16[32,8,256]{2,1,0:T(8,128)(2,1)S(1)}, u32[]{:S(2)}, u32[]{:S(2)}) async-start(bf16[32,8,256]{2,1,0:T(8,128)(2,1)} %broadcast_in_dim.35), calls=%async_computation.6 | async-start | bytes 262144 | tf_op jit(solution)/shard_map/all_to_all | solution.py:174
  192.2 0.6 slice_add_fusion
  192.8 0.8 convolution_convert_fusion.1
  193.6 7.2 %all-to-all-done.6 = bf16[32,8,256]{2,1,0:T(8,128)(2,1)S(1)} async-done(((bf16[32,8,256]{2,1,0:T(8,128)(2,1)}), bf16[32,8,256]{2,1,0:T(8,128)(2,1)S(1)}, u32[]{:S(2)}, u32[]{:S(2)}) %all-to-all-start.6) | async-done | bytes 131104 | tf_op jit(solution)/shard_map/all_to_all | solution.py:174
  200.8 0.7 bitcast_convert_fusion
  (14 shorter events, 0.1 us)
Async XLA Ops:
  0.6 94.0 %copy-start = (bf16[256,256]{1,0:T(8,128)(2,1)S(1)}, bf16[256,256]{1,0:T(8,128)(2,1)}, u32[]{:S(2)}) copy-start(bf16[256,256]{1,0:T(8,128)(2,1)} %param.9) | copy-start | bytes 393220
  2.6 41.4 %copy-start.2 = (s32[1,1,128]{2,1,0:T(1,128)S(1)}, s32[1,1,128]{2,1,0:T(1,128)}, u32[]{:S(2)}) copy-start(s32[1,1,128]{2,1,0:T(1,128)} %param.12) | copy-start | bytes 1540
  2.6 41.4 %copy-start.3 = (s32[1,1,128]{2,1,0:T(1,128)S(1)}, s32[1,1,128]{2,1,0:T(1,128)}, u32[]{:S(2)}) copy-start(s32[1,1,128]{2,1,0:T(1,128)} %param.13) | copy-start | bytes 1540
  2.6 41.3 %all-to-all-start = ((bf16[16,128,256]{2,1,0:T(8,128)(2,1)}), bf16[16,128,256]{2,1,0:T(8,128)(2,1)S(1)}, u32[]{:S(2)}, u32[]{:S(2)}) async-start(bf16[16,128,256]{2,1,0:T(8,128)(2,1)} %broadcast_in_dim.14), calls=%async_computation | async-start | bytes 2097152 | tf_op jit(solution)/shard_map/all_to_all | solution.py:174
  47.5 7.2 %collective-permute-start = (bf16[16,128,256]{2,1,0:T(8,128)(2,1)S(1)}, bf16[16,128,256]{2,1,0:T(8,128)(2,1)S(1)}, u32[]{:S(2)}, u32[]{:S(2)}) collective-permute-start(bf16[16,128,256]{2,1,0:T(8,128)(2,1)S(1)} %get-tuple-element.7), channel_id=1, source_target_pairs={{0,1},{1,0},{2,3},{3,2},{4,5},{5,4},{6,7},{7,6},{8,9},{9,8},{10,11... | collective-permute-start | bytes 3145736 | tf_op jit(solution)/shard_map/ppermute | solution.py:170
  73.5 21.2 %copy-start.4 = (bf16[128,256]{1,0:T(8,128)(2,1)S(1)}, bf16[128,256]{1,0:T(8,128)(2,1)}, u32[]{:S(2)}) copy-start(bf16[128,256]{1,0:T(8,128)(2,1)} %param.11) | copy-start | bytes 196612
  73.5 21.2 %copy-start.5 = (f32[256]{0:T(256)S(1)}, f32[256]{0:T(256)}, u32[]{:S(2)}) copy-start(f32[256]{0:T(256)} %param.10) | copy-start | bytes 3076
  109.9 23.9 %copy-start.1 = (bf16[1,1,128,128,128]{4,3,2,1,0:T(8,128)(2,1)S(1)}, bf16[1,1,128,128,128]{4,3,2,1,0:T(8,128)(2,1)}, u32[]{:S(2)}) copy-start(bf16[1,1,128,128,128]{4,3,2,1,0:T(8,128)(2,1)} %param.15) | copy-start | bytes 12582916
  126.1 7.7 %collective-permute-start.1 = (bf16[4,528,256]{2,1,0:T(8,128)(2,1)S(1)}, bf16[4,528,256]{2,1,0:T(8,128)(2,1)S(1)}, u32[]{:S(2)}, u32[]{:S(2)}) collective-permute-start(bf16[4,528,256]{2,1,0:T(8,128)(2,1)S(1)} %all_to_all.38.own), channel_id=1, source_target_pairs={{0,1},{1,0},{2,3},{3,2},{4,5},{5,4},{6,7},{7,6},{8,9},{9,8},{10,11... | collective-permute-start | bytes 3244040 | tf_op jit(solution)/shard_map/ppermute | solution.py:170
  177.4 23.3 %all-to-all-start.6 = ((bf16[32,8,256]{2,1,0:T(8,128)(2,1)}), bf16[32,8,256]{2,1,0:T(8,128)(2,1)S(1)}, u32[]{:S(2)}, u32[]{:S(2)}) async-start(bf16[32,8,256]{2,1,0:T(8,128)(2,1)} %broadcast_in_dim.35), calls=%async_computation.6 | async-start | bytes 262144 | tf_op jit(solution)/shard_map/all_to_all | solution.py:174

commit v13 on v11

--- a/solution.py
+++ b/solution.py
@@ -202,7 +202,6 @@
         + bias[None, :]
     )
     grad_pre = (grad_out.astype(jnp.float32) * elu_slope(pre)).astype(bf16)
-    output = elu_value(pre).astype(bf16)
 
     grad32 = grad_pre.astype(jnp.float32)
     weight_term = lax.dot_general(
@@ -214,6 +213,8 @@
     own = gather_and_scatter(along_y[:, :side].reshape(4 * side, width), terms, "x")
     back = spread_backward(rows, cols, live, core, values, own, swap(own), col_tiles)
 
+    late, back = lax.optimization_barrier((pre, back))
+    output = elu_value(late).astype(bf16)
     reduced = add_up(exchange(back, ROW))
     grad_mixed = reduced[:side].astype(bf16)
     grad_weight = gather(reduced[side : side + 8].astype(bf16), COL, 32).reshape(width, width).astype(jnp.float32)

time: 188 us -> 187 us (level)
  blocking collectives: 103 us -> 62.8 us
  waiting for transfers between devices: 34.5 us -> 66.5 us
  starting transfers between devices: 34.8 us -> 42.8 us
    all_to_all x5 -> x4, blocking collectives: 103 us -> 62.8 us  [exchange(): return lax.all_to_all(x, axes, 0, 0, tiled=True)]
    all_to_all x2 -> x3, waiting for transfers between devices: 29.9 us -> 61.9 us  [exchange(): return lax.all_to_all(x, axes, 0, 0, tiled=True)]
    all_to_all x2 -> x3, starting transfers between devices: 23.4 us -> 30.9 us  [exchange(): return lax.all_to_all(x, axes, 0, 0, tiled=True)]
  transfers between devices with their start and end apart: 4 -> 5, of which waited for: 4 -> 5; matrix products, arithmetic and copies ran while one was open for 1% -> 1% of each run, Pallas kernels for 0% -> 0%
where the time goes in v13:
time: 187 us
  waiting for transfers between devices  66.5 us (36%)
  blocking collectives  62.8 us (34%)
  starting transfers between devices  42.8 us (23%)
  Pallas kernels  6.1 us (3%)
  other arithmetic  2.87 us (2%)
  local copies, waits for them, and re-layouts  2.75 us (1%)
    all_to_all x4, blocking collectives, exchange(): return lax.all_to_all(x, axes, 0, 0, tiled=True)  62.8 us
    all_to_all x3, waiting for transfers between devices, exchange(): return lax.all_to_all(x, axes, 0, 0, tiled=True)  61.9 us
    all_to_all x3, starting transfers between devices, exchange(): return lax.all_to_all(x, axes, 0, 0, tiled=True)  30.9 us
    ppermute x2, starting transfers between devices, swap(): return lax.ppermute(x, 'core', [(0, 1), (1, 0)])  11.9 us
    ppermute x2, waiting for transfers between devices, swap(): return lax.ppermute(x, 'core', [(0, 1), (1, 0)])  4.58 us
  transfers between devices with their start and end apart: 5, of which 5 were waited for; matrix products, arithmetic and copies ran while one was open for 1% of the time, Pallas kernels for 0%

profile of v13, /device:TPU:1, one launch (start us, length us, event | category | flops | bytes accessed | tf_op | source)
XLA Modules:
  0.0 186.7 jit_solution(1923685110931241679)
XLA Ops:
  0.6 0.0 copy-start
  0.6 1.9 %broadcast_in_dim.14 = bf16[16,128,256]{2,1,0:T(8,128)(2,1)} broadcast(bf16[128,256]{1,0:T(8,128)(2,1)} %param.8), dimensions={1,2} | broadcast | bytes 1114112 | tf_op jit(solution)/shard_map/broadcast_in_dim | solution.py:173
  2.6 16.4 %all-to-all-start = ((bf16[16,128,256]{2,1,0:T(8,128)(2,1)}), bf16[16,128,256]{2,1,0:T(8,128)(2,1)S(1)}, u32[]{:S(2)}, u32[]{:S(2)}) async-start(bf16[16,128,256]{2,1,0:T(8,128)(2,1)} %broadcast_in_dim.14), calls=%async_computation | async-start | bytes 2097152 | tf_op jit(solution)/shard_map/all_to_all | solution.py:169
  19.6 22.7 %all-to-all-done.src = bf16[16,128,256]{2,1,0:T(8,128)(2,1)S(1)} async-done(((bf16[16,128,256]{2,1,0:T(8,128)(2,1)}), bf16[16,128,256]{2,1,0:T(8,128)(2,1)S(1)}, u32[]{:S(2)}, u32[]{:S(2)}) %all-to-all-start) | async-done | bytes 1048608 | tf_op jit(solution)/shard_map/all_to_all | solution.py:169
  42.4 3.0 %forward_tiles.1 = (bf16[16,128,256]{2,1,0:T(8,128)(2,1)S(1)}, bf16[16,128,256]{2,1,0:T(8,128)(2,1)S(1)}) custom-call(s32[128]{0:T(128)S(1)} %bitcast.22, s32[128]{0:T(128)S(1)} %bitcast.24, s32[1]{0:T(128)} %bitcast.18.live_ref, s32[1]{0:T(128)} %bitcast.3.core_ref, bf16[128,128,128]{2,1,0:T(8,128)(2,1)} %bitcast.20, bf16[16,128,256]{2,1,0:T(8,128)(2,1)S(1)} %all-to-all-done.src), custom_call_target="tpu_custom_call" | custom-call | flops 1073741824 | bytes 4194304 | tf_op jit(solution)/shard_map/forward_tiles/pallas_call | solution.py:129
  45.3 6.5 %collective-permute-start = (bf16[16,128,256]{2,1,0:T(8,128)(2,1)S(1)}, bf16[16,128,256]{2,1,0:T(8,128)(2,1)S(1)}, u32[]{:S(2)}, u32[]{:S(2)}) collective-permute-start(bf16[16,128,256]{2,1,0:T(8,128)(2,1)S(1)} %get-tuple-element.9), channel_id=1, source_target_pairs={{0,1},{1,0},{2,3},{3,2},{4,5},{5,4},{6,7},{7,6},{8,9},{9,8},{10,11... | collective-permute-start | bytes 3145736 | tf_op jit(solution)/shard_map/ppermute | solution.py:165
  51.8 2.3 %collective-permute-done = bf16[16,128,256]{2,1,0:T(8,128)(2,1)S(1)} collective-permute-done((bf16[16,128,256]{2,1,0:T(8,128)(2,1)S(1)}, bf16[16,128,256]{2,1,0:T(8,128)(2,1)S(1)}, u32[]{:S(2)}, u32[]{:S(2)}) %collective-permute-start) | collective-permute-done | bytes 1048608 | tf_op jit(solution)/shard_map/ppermute | solution.py:165
  54.1 0.4 add_convert_fusion
  54.5 18.0 %all_to_all.35 = bf16[4,4,128,256]{3,2,1,0:T(8,128)(2,1)S(1)} all-to-all(bf16[4,4,128,256]{3,2,1,0:T(8,128)(2,1)S(1)} %bitcast.26), channel_id=1, replica_groups=mesh['yh'=2,'z'=8,'yl'=4,'x'=4,'core'=2] {'x'}, dimensions={0} | all-to-all | bytes 2097152 | tf_op jit(solution)/shard_map/all_to_all | solution.py:169
  72.5 0.2 reduce_sum.42
  72.7 14.7 %all_to_all.36 = bf16[4,128,256]{2,1,0:T(8,128)(2,1)S(1)} all-to-all(bf16[4,128,256]{2,1,0:T(8,128)(2,1)S(1)} %reduce_sum.42), channel_id=1, replica_groups=mesh['yh'=2,'z'=8,'yl'=4,'x'=4,'core'=2] {'yl'}, dimensions={0} | all-to-all | bytes 524288 | tf_op jit(solution)/shard_map/all_to_all | solution.py:169
  87.5 0.3 multiply_convert_fusion
  87.8 0.3 convolution_convert_fusion
  88.1 14.5 %all_to_all.37 = bf16[4,192,256]{2,1,0:T(8,128)(2,1)S(1)} all-to-all(bf16[4,192,256]{2,1,0:T(8,128)(2,1)S(1)} %pad_maximum_fusion.1), channel_id=1, replica_groups=mesh['yh'=2,'z'=8,'yl'=4,'x'=4,'core'=2] {'yl'}, dimensions={0} | all-to-all | bytes 786432 | tf_op jit(solution)/shard_map/all_to_all | solution.py:169
  102.7 0.1 broadcast_in_dim.34
  102.8 0.0 copy-start.1
  102.8 0.1 pad_maximum_fusion
  102.9 15.5 %all_to_all.38.own = bf16[4,528,256]{2,1,0:T(8,128)(2,1)S(1)} all-to-all(bf16[4,528,256]{2,1,0:T(8,128)(2,1)S(1)} %pad_maximum_fusion), channel_id=1, replica_groups=mesh['yh'=2,'z'=8,'yl'=4,'x'=4,'core'=2] {'x'}, dimensions={0} | all-to-all | bytes 2162688 | tf_op jit(solution)/shard_map/all_to_all | solution.py:169
  118.4 5.4 %collective-permute-start.1 = (bf16[4,528,256]{2,1,0:T(8,128)(2,1)S(1)}, bf16[4,528,256]{2,1,0:T(8,128)(2,1)S(1)}, u32[]{:S(2)}, u32[]{:S(2)}) collective-permute-start(bf16[4,528,256]{2,1,0:T(8,128)(2,1)S(1)} %all_to_all.38.own), channel_id=1, source_target_pairs={{0,1},{1,0},{2,3},{3,2},{4,5},{5,4},{6,7},{7,6},{8,9},{9,8},{10,11... | collective-permute-start | bytes 3244040 | tf_op jit(solution)/shard_map/ppermute | solution.py:165
  123.9 2.3 %collective-permute-done.1.other = bf16[4,528,256]{2,1,0:T(8,128)(2,1)S(1)} collective-permute-done((bf16[4,528,256]{2,1,0:T(8,128)(2,1)S(1)}, bf16[4,528,256]{2,1,0:T(8,128)(2,1)S(1)}, u32[]{:S(2)}, u32[]{:S(2)}) %collective-permute-start.1) | collective-permute-done | bytes 1081376 | tf_op jit(solution)/shard_map/ppermute | solution.py:165
  126.2 0.0 copy-done.1
  126.2 3.1 %backward_tiles.1 = bf16[16,144,256]{2,1,0:T(8,128)(2,1)} custom-call(s32[128]{0:T(128)S(1)} %bitcast.23, s32[128]{0:T(128)S(1)} %bitcast.25, s32[1]{0:T(128)} %bitcast.19.live_ref, s32[1]{0:T(128)} %bitcast.3.core_ref, bf16[128,128,128]{2,1,0:T(8,128)(2,1)S(1)} %bitcast.21, bf16[4,528,256]{2,1,0:T(8,128)(2,1)S(1)} %all_to_all.38.own, ...), custom_call_target="tpu_custom_call" | custom-call | flops 1073741824 | bytes 4194304 | tf_op jit(solution)/shard_map/backward_tiles/pallas_call | solution.py:148
  129.3 7.1 %all-to-all-start.5 = ((bf16[16,144,256]{2,1,0:T(8,128)(2,1)}), bf16[16,144,256]{2,1,0:T(8,128)(2,1)S(1)}, u32[]{:S(2)}, u32[]{:S(2)}) async-start(bf16[16,144,256]{2,1,0:T(8,128)(2,1)} %backward_tiles.1), calls=%async_computation.5 | async-start | bytes 2359296 | tf_op jit(solution)/shard_map/all_to_all | solution.py:169
  136.5 0.7 fusion
  137.1 32.0 %all-to-all-done.5 = bf16[16,144,256]{2,1,0:T(8,128)(2,1)S(1)} async-done(((bf16[16,144,256]{2,1,0:T(8,128)(2,1)}), bf16[16,144,256]{2,1,0:T(8,128)(2,1)S(1)}, u32[]{:S(2)}, u32[]{:S(2)}) %all-to-all-start.5) | async-done | bytes 1179680 | tf_op jit(solution)/shard_map/all_to_all | solution.py:169
  169.2 0.2 convert_reduce_fusion
  169.4 0.7 broadcast_in_dim.35
  170.0 7.4 %all-to-all-start.6 = ((bf16[32,8,256]{2,1,0:T(8,128)(2,1)}), bf16[32,8,256]{2,1,0:T(8,128)(2,1)S(1)}, u32[]{:S(2)}, u32[]{:S(2)}) async-start(bf16[32,8,256]{2,1,0:T(8,128)(2,1)} %broadcast_in_dim.35), calls=%async_computation.6 | async-start | bytes 262144 | tf_op jit(solution)/shard_map/all_to_all | solution.py:169
  177.4 0.6 slice_add_fusion
  178.0 0.8 convolution_convert_fusion.1
  178.8 7.1 %all-to-all-done.6 = bf16[32,8,256]{2,1,0:T(8,128)(2,1)S(1)} async-done(((bf16[32,8,256]{2,1,0:T(8,128)(2,1)}), bf16[32,8,256]{2,1,0:T(8,128)(2,1)S(1)}, u32[]{:S(2)}, u32[]{:S(2)}) %all-to-all-start.6) | async-done | bytes 131104 | tf_op jit(solution)/shard_map/all_to_all | solution.py:169
  186.0 0.7 bitcast_convert_fusion
  (16 shorter events, 0.1 us)
Async XLA Ops:
  0.6 86.8 %copy-start = (bf16[256,256]{1,0:T(8,128)(2,1)S(1)}, bf16[256,256]{1,0:T(8,128)(2,1)}, u32[]{:S(2)}) copy-start(bf16[256,256]{1,0:T(8,128)(2,1)} %param.9) | copy-start | bytes 393220
  2.6 39.8 %copy-start.2 = (s32[1,1,128]{2,1,0:T(1,128)S(1)}, s32[1,1,128]{2,1,0:T(1,128)}, u32[]{:S(2)}) copy-start(s32[1,1,128]{2,1,0:T(1,128)} %param.12) | copy-start | bytes 1540
  2.6 39.8 %copy-start.3 = (s32[1,1,128]{2,1,0:T(1,128)S(1)}, s32[1,1,128]{2,1,0:T(1,128)}, u32[]{:S(2)}) copy-start(s32[1,1,128]{2,1,0:T(1,128)} %param.13) | copy-start | bytes 1540
  2.6 39.8 %all-to-all-start = ((bf16[16,128,256]{2,1,0:T(8,128)(2,1)}), bf16[16,128,256]{2,1,0:T(8,128)(2,1)S(1)}, u32[]{:S(2)}, u32[]{:S(2)}) async-start(bf16[16,128,256]{2,1,0:T(8,128)(2,1)} %broadcast_in_dim.14), calls=%async_computation | async-start | bytes 2097152 | tf_op jit(solution)/shard_map/all_to_all | solution.py:169
  45.3 8.8 %collective-permute-start = (bf16[16,128,256]{2,1,0:T(8,128)(2,1)S(1)}, bf16[16,128,256]{2,1,0:T(8,128)(2,1)S(1)}, u32[]{:S(2)}, u32[]{:S(2)}) collective-permute-start(bf16[16,128,256]{2,1,0:T(8,128)(2,1)S(1)} %get-tuple-element.9), channel_id=1, source_target_pairs={{0,1},{1,0},{2,3},{3,2},{4,5},{5,4},{6,7},{7,6},{8,9},{9,8},{10,11... | collective-permute-start | bytes 3145736 | tf_op jit(solution)/shard_map/ppermute | solution.py:165
  72.5 15.0 %copy-start.4 = (bf16[128,256]{1,0:T(8,128)(2,1)S(1)}, bf16[128,256]{1,0:T(8,128)(2,1)}, u32[]{:S(2)}) copy-start(bf16[128,256]{1,0:T(8,128)(2,1)} %param.11) | copy-start | bytes 196612
  72.5 15.0 %copy-start.5 = (f32[256]{0:T(256)S(1)}, f32[256]{0:T(256)}, u32[]{:S(2)}) copy-start(f32[256]{0:T(256)} %param.10) | copy-start | bytes 3076
  102.8 23.4 %copy-start.1 = (bf16[1,1,128,128,128]{4,3,2,1,0:T(8,128)(2,1)S(1)}, bf16[1,1,128,128,128]{4,3,2,1,0:T(8,128)(2,1)}, u32[]{:S(2)}) copy-start(bf16[1,1,128,128,128]{4,3,2,1,0:T(8,128)(2,1)} %param.15) | copy-start | bytes 12582916
  118.4 7.7 %collective-permute-start.1 = (bf16[4,528,256]{2,1,0:T(8,128)(2,1)S(1)}, bf16[4,528,256]{2,1,0:T(8,128)(2,1)S(1)}, u32[]{:S(2)}, u32[]{:S(2)}) collective-permute-start(bf16[4,528,256]{2,1,0:T(8,128)(2,1)S(1)} %all_to_all.38.own), channel_id=1, source_target_pairs={{0,1},{1,0},{2,3},{3,2},{4,5},{5,4},{6,7},{7,6},{8,9},{9,8},{10,11... | collective-permute-start | bytes 3244040 | tf_op jit(solution)/shard_map/ppermute | solution.py:165
  129.3 39.8 %all-to-all-start.5 = ((bf16[16,144,256]{2,1,0:T(8,128)(2,1)}), bf16[16,144,256]{2,1,0:T(8,128)(2,1)S(1)}, u32[]{:S(2)}, u32[]{:S(2)}) async-start(bf16[16,144,256]{2,1,0:T(8,128)(2,1)} %backward_tiles.1), calls=%async_computation.5 | async-start | bytes 2359296 | tf_op jit(solution)/shard_map/all_to_all | solution.py:169
  170.0 15.9 %all-to-all-start.6 = ((bf16[32,8,256]{2,1,0:T(8,128)(2,1)}), bf16[32,8,256]{2,1,0:T(8,128)(2,1)S(1)}, u32[]{:S(2)}, u32[]{:S(2)}) async-start(bf16[32,8,256]{2,1,0:T(8,128)(2,1)} %broadcast_in_dim.35), calls=%async_computation.6 | async-start | bytes 262144 | tf_op jit(solution)/shard_map/all_to_all | solution.py:169
